TPU v7x, 32 devices: a whole 2x2x4 slice. The times are simulated.
32 devices in a mesh: dom: 8 (over y, x, core), rep: 4 (over z).
Axes of the slice: x: 2, y: 2, z: 4, core: 2. Of those that a mesh axis runs over, the one named last changes fastest.
Arguments:
- feature_grid: bfloat16 [8, 32, 32768], P('dom'), may hold values from -6 to 6
- fine_in: bfloat16 [8, 64, 32], P('dom'), may hold values from -1 to 1
- fine_mid: bfloat16 [8, 2, 64, 64], P('dom'), may hold values from -0.75 to 0.75
- fine_out: bfloat16 [8, 64], P('dom'), may hold values from -0.75 to 0.75
- prop_in: bfloat16 [8, 16, 32], P('dom'), may hold values from -1 to 1
- prop_out: bfloat16 [8, 16], P('dom'), may hold values from -1.5 to 1.5
- sample_cells: int32 [8, 4, 8, 2048], P('dom', 'rep'), may hold values from 0 to 31710, as said below
- sample_geometry: bfloat16 [4, 8, 4, 8, 2048], P(None, 'dom', 'rep'), may hold values from 0 to 1, as said below
- slot_ray: int32 [8, 4, 8, 32], P('dom', 'rep'), may hold values from 0 to 255, as said below
- slot_rank: int32 [8, 4, 8, 32], P('dom', 'rep'), may hold values from 0 to 7, as said below
- bucket_count: int32 [8, 4, 8], P('dom', 'rep'), may hold values from 1 to 32, as said below
Outputs:
- ray_loss: float32 [8, 4, 256], P('dom', 'rep')
- prop_in_grad: float32 [8, 16, 32], P('dom')
- prop_out_grad: float32 [8, 16], P('dom')
Inputs may be any that keep to these rules, and one draw needn't show every extreme that they name: `sample_cells`: each base cell's three coordinates lie in 0 to 30, so all eight corners are inside the grid. `sample_geometry`: rows 0 to 2 lie in 0 to 1; row 3 is positive. `slot_ray`: within one bucket the rays are distinct. `slot_rank`: live segments of one ray on one device have distinct ranks. `bucket_count`: the live slots of a bucket are its first ones; in every draw one partition receives full buckets from every device.
All inputs are finite; a program needn't handle non-finite values.
Results may differ from a plain program's by a relative error of at most 0.0024.
Values may be sent and summed in bfloat16 or wider, within the bound.
No kernel may reach another device: no remote copies, remote signals or barrier semaphores. Data moves between devices by JAX's collectives and lax.ppermute only.
A program may use at most 192 MiB of HBM per device.

v0:
```python
import jax
import jax.numpy as jnp
from jax import lax
from jax.sharding import PartitionSpec as P

GR = 32
RAY_DEV = 256


distill_weight = 50.0
group_size = 4


def corner_table(grid_local, side):
    cell_major = jnp.transpose(grid_local)
    cell_total = cell_major.shape[0]
    reach = side * side + side + 1
    padded = jnp.concatenate(
        [cell_major, jnp.zeros((reach, cell_major.shape[1]), cell_major.dtype)], axis=0
    )
    pieces = []
    for corner in range(8):
        step_x = corner // 4
        step_y = corner // 2 % 2
        step_z = corner % 2
        start = (step_x * side + step_y) * side + step_z
        pieces.append(padded[start : start + cell_total])
    return jnp.concatenate(pieces, axis=1)


def interpolate(table, cell_index, geometry):
    offsets = geometry[:3].astype(jnp.float32)
    width = table.shape[1] // 8
    rows = jnp.take(table, cell_index, axis=0)
    summed = jnp.zeros((cell_index.shape[0], width), jnp.float32)
    for corner in range(8):
        step_x = corner // 4
        step_y = corner // 2 % 2
        step_z = corner % 2
        factor = (
            (offsets[0] if step_x else 1.0 - offsets[0])
            * (offsets[1] if step_y else 1.0 - offsets[1])
            * (offsets[2] if step_z else 1.0 - offsets[2])
        )
        summed = (
            summed
            + rows[:, corner * width : (corner + 1) * width].astype(jnp.float32) * factor[:, None]
        )
    return jnp.transpose(summed.astype(jnp.bfloat16))


def fine_density(fine_in, fine_mid, fine_out, features):
    hidden_units = jax.nn.relu(
        jnp.dot(fine_in, features, preferred_element_type=jnp.float32)
    ).astype(jnp.bfloat16)
    for layer_index in range(fine_mid.shape[0]):
        hidden_units = jax.nn.relu(
            jnp.dot(fine_mid[layer_index], hidden_units, preferred_element_type=jnp.float32)
        ).astype(jnp.bfloat16)
    return jax.nn.softplus(jnp.dot(fine_out, hidden_units, preferred_element_type=jnp.float32))


def proposal_parts(prop_in, prop_out, features):
    pre_hidden = jnp.dot(prop_in, features, preferred_element_type=jnp.float32)
    hidden_units = jax.nn.relu(pre_hidden).astype(jnp.bfloat16)
    logits = jnp.dot(prop_out, hidden_units, preferred_element_type=jnp.float32)
    return (pre_hidden, hidden_units, logits)


def proposal_grads(prop_in, prop_out, features, sigma_grad):
    pre_hidden, hidden_units, logits = proposal_parts(prop_in, prop_out, features)
    logit_grad = (sigma_grad * jax.nn.sigmoid(logits)).astype(jnp.bfloat16)
    out_grad = jnp.dot(hidden_units, logit_grad, preferred_element_type=jnp.float32)
    spread = prop_out[:, None].astype(jnp.float32) * logit_grad[None, :].astype(jnp.float32)
    hidden_grad = jnp.where(pre_hidden > 0, spread, jnp.float32(0.0)).astype(jnp.bfloat16)
    in_grad = lax.dot_general(
        hidden_grad, features, (((1,), (1,)), ((), ())), preferred_element_type=jnp.float32
    )
    return (in_grad, out_grad)


def absorbed(sigma, spacing):
    optical = sigma * spacing
    count = optical.shape[-2]
    lower = (jnp.arange(count)[:, None] >= jnp.arange(count)[None, :]).astype(jnp.float32)
    depth_sum = jnp.einsum("ij,pjc->pic", lower, optical, precision=lax.Precision.HIGHEST)
    return (jnp.exp(optical - depth_sum) - jnp.exp(-depth_sum), -depth_sum[..., -1, :])


def proposal_terms(sigma, fine_absorbed, spacing):
    prop_absorbed, log_prop = absorbed(sigma, spacing)
    return (
        jnp.sum(prop_absorbed * prop_absorbed, axis=-2),
        jnp.sum(prop_absorbed * fine_absorbed, axis=-2),
        log_prop,
    )


def segment_stats(prop_sigma, fine_sigma, spacing):
    fine_absorbed, log_fine = absorbed(fine_sigma, spacing)
    sum_aa, sum_ab, log_prop = proposal_terms(prop_sigma, fine_absorbed, spacing)
    sum_bb = jnp.sum(fine_absorbed * fine_absorbed, axis=-2)
    return (log_prop, log_fine, sum_aa, sum_ab, sum_bb)


def spread_sum(values, ray_table, rank_table, matrix):
    per_ray = lax.dot_general(
        ray_table,
        rank_table * values[None, :],
        (((1,), (1,)), ((), ())),
        precision=lax.Precision.HIGHEST,
    )
    per_ray = jnp.dot(per_ray, matrix, precision=lax.Precision.HIGHEST)
    spread = lax.dot_general(
        per_ray, ray_table, (((0,), (0,)), ((), ())), precision=lax.Precision.HIGHEST
    )
    return jnp.sum(spread * rank_table, axis=0)


def ray_side(log_prop, log_fine, sum_aa, sum_ab, sum_bb, ray_ids, rank_ids, counts):
    part_count, capacity = ray_ids.shape
    live_mask = (jnp.arange(capacity)[None, :] < counts[:, None]).astype(jnp.float32).reshape(-1)
    ray_flat = ray_ids.reshape(-1)
    rank_flat = rank_ids.reshape(-1)
    ray_table = (jnp.arange(RAY_DEV)[:, None] == ray_flat[None, :]).astype(jnp.float32)
    rank_table = (jnp.arange(part_count)[:, None] == rank_flat[None, :]).astype(jnp.float32)
    later = (jnp.arange(part_count)[:, None] < jnp.arange(part_count)[None, :]).astype(jnp.float32)
    entry_prop = (
        jnp.exp(spread_sum(log_prop.reshape(-1) * live_mask, ray_table, rank_table, later))
        * live_mask
    )
    entry_fine = (
        jnp.exp(spread_sum(log_fine.reshape(-1) * live_mask, ray_table, rank_table, later))
        * live_mask
    )
    flat_aa = sum_aa.reshape(-1)
    flat_ab = sum_ab.reshape(-1)
    flat_bb = sum_bb.reshape(-1)
    seg_loss = (
        entry_prop * entry_prop * flat_aa
        - 2.0 * entry_prop * entry_fine * flat_ab
        + entry_fine * entry_fine * flat_bb
    )
    slot_grad = distill_weight * (entry_prop * flat_aa - entry_fine * flat_ab) * entry_prop
    carried = spread_sum(slot_grad, ray_table, rank_table, later.T) * live_mask
    ray_loss = 0.5 * distill_weight * jnp.dot(ray_table, seg_loss, precision=lax.Precision.HIGHEST)
    coef_aa = 0.5 * distill_weight * entry_prop * entry_prop
    coef_ab = -distill_weight * entry_prop * entry_fine
    return (jnp.stack([coef_aa, coef_ab, carried]).reshape(3, part_count, capacity), ray_loss)


def on_device(
    feature_grid,
    fine_in,
    fine_mid,
    fine_out,
    prop_in,
    prop_out,
    sample_cells,
    sample_geometry,
    slot_ray,
    slot_rank,
    bucket_count,
):
    part_count = lax.axis_size("dom")
    capacity = slot_ray.shape[3]
    bucket_width = sample_cells.shape[3]
    per_slot = bucket_width // capacity
    groups = part_count // group_size
    group_span = group_size * bucket_width
    arrived = lax.all_to_all(sample_geometry, "dom", split_axis=3, concat_axis=3, tiled=True)
    cell_groups = sample_cells.reshape(groups, group_span)
    geometry_groups = jnp.moveaxis(arrived.reshape(4, groups, group_span), 1, 0)
    table = corner_table(feature_grid[0], GR)

    def forward_group(packed):
        cell_index, geometry = packed
        features = interpolate(table, cell_index, geometry)
        fine_sigma = fine_density(fine_in[0], fine_mid[0], fine_out[0], features)
        prop_sigma = jax.nn.softplus(proposal_parts(prop_in[0], prop_out[0], features)[2])
        return (features, prop_sigma, fine_sigma)

    features_all, prop_sigma, fine_sigma = lax.map(forward_group, (cell_groups, geometry_groups))
    ray_ids = slot_ray[0, 0]
    rank_ids = slot_rank[0, 0]
    counts = bucket_count[0, 0]
    recv_spacing = arrived[3, 0, 0].astype(jnp.float32).reshape(part_count, per_slot, capacity)
    owner_prop = prop_sigma.reshape(part_count, per_slot, capacity)
    owner_fine = fine_sigma.reshape(part_count, per_slot, capacity)
    stats = segment_stats(owner_prop, owner_fine, recv_spacing)
    summary = jnp.stack(stats).reshape(5, 1, 1, part_count, capacity)
    returned = lax.all_to_all(summary, "dom", split_axis=3, concat_axis=3, tiled=True)
    factors, ray_loss = ray_side(
        returned[0, 0, 0],
        returned[1, 0, 0],
        returned[2, 0, 0],
        returned[3, 0, 0],
        returned[4, 0, 0],
        ray_ids,
        rank_ids,
        counts,
    )
    arrived_factors = lax.all_to_all(
        factors.reshape(3, 1, 1, part_count, capacity),
        "dom",
        split_axis=3,
        concat_axis=3,
        tiled=True,
    )
    fine_absorbed = absorbed(owner_fine, recv_spacing)[0]
    terms_value, pullback = jax.vjp(
        lambda sigma: proposal_terms(sigma, fine_absorbed, recv_spacing), owner_prop
    )
    sigma_grad = pullback(
        (arrived_factors[0, 0, 0], arrived_factors[1, 0, 0], arrived_factors[2, 0, 0])
    )[0]
    sigma_grad_owner = sigma_grad.reshape(groups, group_span)

    def backward_group(running, packed):
        features, sigma_block = packed
        in_grad, out_grad = proposal_grads(prop_in[0], prop_out[0], features, sigma_block)
        return ((running[0] + in_grad, running[1] + out_grad), None)

    initial = (
        jnp.zeros(prop_in.shape[1:], jnp.float32),
        jnp.zeros(prop_out.shape[1:], jnp.float32),
    )
    totals, unused = lax.scan(backward_group, initial, (features_all, sigma_grad_owner))
    in_sum, out_sum = lax.psum((totals[0], totals[1]), "rep")
    return (ray_loss.reshape(1, 1, -1), in_sum[None], out_sum[None])


def solution(mesh):
    return jax.shard_map(
        on_device,
        mesh=mesh,
        in_specs=(
            P("dom", None, None),
            P("dom", None, None),
            P("dom", None, None, None),
            P("dom", None),
            P("dom", None, None),
            P("dom", None),
            P("dom", "rep", None, None),
            P(None, "dom", "rep", None, None),
            P("dom", "rep", None, None),
            P("dom", "rep", None, None),
            P("dom", "rep", None),
        ),
        out_specs=(P("dom", "rep", None), P("dom", None, None), P("dom", None)),
        check_vma=False,
    )
```

profile of v0, /device:TPU:0, one launch (start us, length us, event | category | flops | bytes accessed | tf_op | source)
XLA Modules:
  0.0 269.4 jit_solution(14162294793358824451)
XLA Ops:
  0.6 1.6 copy.67
  2.3 5.2 %all-to-all-start = ((bf16[4,1,1,8,2048]{4,0,2,1,3:T(4,128)(2,1)}), bf16[4,1,1,8,2048]{4,0,2,1,3:T(4,128)(2,1)S(1)}, u32[]{:S(2)}, u32[]{:S(2)}) async-start(bf16[4,1,1,8,2048]{4,0,2,1,3:T(4,128)(2,1)} %copy.67), calls=%async_computation | async-start | bytes 262144 | tf_op jit(solution)/shard_map/all_to_all | solution.py:171
  7.5 7.4 %copy.66 = bf16[1,32,32768]{1,2,0:T(8,128)(2,1)} copy(bf16[1,32,32768]{2,1,0:T(8,128)(2,1)} %param.15) | data formatting | bytes 4194304 | tf_op args[0]
  14.8 47.0 %pad_slice_fusion = (bf16[32768,32]{1,0:T(8,128)(2,1)}, bf16[32768,32]{1,0:T(8,128)(2,1)}, bf16[32768,32]{1,0:T(8,128)(2,1)}, bf16[32768,32]{1,0:T(8,128)(2,1)},...) fusion(bf16[32768,32]{1,0:T(8,128)(2,1)} %bitcast.211), kind=kLoop, calls=%fused_computation.76 | loop fusion | bytes 16777216 | tf_op jit(solution)/shard_map/slice | solution.py:27
  62.0 63.3 %concatenate.8 = bf16[32768,256]{1,0:T(8,128)(2,1)} concatenate(bf16[32768,32]{1,0:T(8,128)(2,1)} %bitcast.212, bf16[32768,32]{1,0:T(8,128)(2,1)} %get-tuple-element.303, bf16[32768,32]{1,0:T(8,128)(2,1)} %get-tuple-element.298, bf16[32768,32]{1,0:T(8,128)(2,1)} %get-tuple-element.299, bf16[32768,32]{1,0:T(8,128)(2,1)} %get-tuple-element.300, ...), dimensions={1} | concatenate | bytes 33554432 | tf_op jit(solution)/shard_map/concatenate | solution.py:28
  125.7 102.7 %while.27 = (s32[]{:T(128)}, bf16[2,32,8192]{2,1,0:T(8,128)(2,1)S(1)}, f32[2,8192]{1,0:T(2,128)S(1)}, f32[2,8192]{1,0:T(2,128)S(1)}, s32[2,8192]{1,0:T(2,128)S(1...) while((s32[]{:T(128)}, ...), condition=%wide.region_1.2_spmd, body=%wide.region_0.1_spmd.sunk | while | flops 189595648 | bytes 35137208 | solution.py:183
  126.0 38.8 %gather_fusion = bf16[8192,256]{1,0:T(8,128)(2,1)} fusion(bf16[32768,256]{1,0:T(8,128)(2,1)} %get-tuple-element.499, s32[8192]{0:T(1024)S(1)} %broadcast_clamp_fusion.2), kind=kCustom, calls=%fused_computation.clone.1 | custom fusion | bytes 8421376 | tf_op jit(solution)/shard_map/while/body/eval_jaxpr/jit(_take)/gather | solution.py:34
  164.8 6.4 %copy.83 = bf16[8192,256]{0,1:T(8,128)(2,1)} copy(bf16[8192,256]{1,0:T(8,128)(2,1)} %gather_fusion) | data formatting | bytes 8388608 | tf_op jit(solution)/shard_map/while/body/eval_jaxpr/jit(_take)/gather | solution.py:34
  171.1 2.6 broadcast_select_fusion.5
  173.8 0.9 bitcast_dynamic-update-slice_fusion.2
  174.6 0.8 fusion.162
  177.2 38.8 %gather_fusion = bf16[8192,256]{1,0:T(8,128)(2,1)} fusion(bf16[32768,256]{1,0:T(8,128)(2,1)} %get-tuple-element.499, s32[8192]{0:T(1024)S(1)} %broadcast_clamp_fusion.2), kind=kCustom, calls=%fused_computation.clone.1 | custom fusion | bytes 8421376 | tf_op jit(solution)/shard_map/while/body/eval_jaxpr/jit(_take)/gather | solution.py:34
  216.0 6.4 %copy.83 = bf16[8192,256]{0,1:T(8,128)(2,1)} copy(bf16[8192,256]{1,0:T(8,128)(2,1)} %gather_fusion) | data formatting | bytes 8388608 | tf_op jit(solution)/shard_map/while/body/eval_jaxpr/jit(_take)/gather | solution.py:34
  222.4 2.6 broadcast_select_fusion.5
  225.0 0.9 bitcast_dynamic-update-slice_fusion.2
  225.9 0.8 fusion.162
  231.0 0.7 reduce.26
  231.7 0.7 reshape.487
  232.4 4.2 %all-to-all-start.1 = ((f32[8,1,160]{2,1,0:T(1,128)}), f32[8,1,160]{2,1,0:T(1,128)S(1)}, u32[]{:S(2)}, u32[]{:S(2)}) async-start(f32[8,1,160]{2,1,0:T(1,128)} %reshape.487), calls=%async_computation.1 | async-start | bytes 16384 | tf_op jit(solution)/shard_map/all_to_all | solution.py:192
  236.9 4.4 %all-to-all-done.1 = f32[8,1,160]{2,1,0:T(1,128)S(1)} async-done(((f32[8,1,160]{2,1,0:T(1,128)}), f32[8,1,160]{2,1,0:T(1,128)S(1)}, u32[]{:S(2)}, u32[]{:S(2)}) %all-to-all-start.1) | async-done | bytes 5152 | tf_op jit(solution)/shard_map/all_to_all | solution.py:192
  245.5 3.3 %all-to-all-start.2 = ((f32[3,1,1,8,32]{4,2,1,0,3:T(1,128)}), f32[3,1,1,8,32]{4,2,1,0,3:T(1,128)S(1)}, u32[]{:S(2)}, u32[]{:S(2)}) async-start(f32[3,1,1,8,32]{4,2,1,0,3:T(1,128)} %pad_maximum_fusion), calls=%async_computation.2 | async-start | bytes 24576 | tf_op jit(solution)/shard_map/all_to_all | solution.py:203
  249.7 3.8 %all-to-all-done.2 = f32[3,1,1,8,32]{4,2,1,0,3:T(1,128)S(1)} async-done(((f32[3,1,1,8,32]{4,2,1,0,3:T(1,128)}), f32[3,1,1,8,32]{4,2,1,0,3:T(1,128)S(1)}, u32[]{:S(2)}, u32[]{:S(2)}) %all-to-all-start.2) | async-done | bytes 3104 | tf_op jit(solution)/shard_map/all_to_all | solution.py:203
  254.3 2.1 while.28
  256.4 13.1 %all-reduce.2 = (f32[1,16,32]{2,1,0:T(8,128)}, f32[1,16]{1,0:T(1,128)}) all-reduce(f32[1,16,32]{2,1,0:T(8,128)S(1)} %bitcast.225, f32[1,16]{1,0:T(1,128)S(1)} %bitcast.229), channel_id=1, replica_groups=mesh['dom'=8,'rep'=4] {'rep'}, use_global_device_ids=true, to_apply=%region_10.11 | all-reduce | flops 528 | bytes 4224 | tf_op jit(solution)/shard_map/psum | solution.py:229
  (123 shorter events, 14.4 us)
Async XLA Ops:
  2.3 123.0 %all-to-all-start = ((bf16[4,1,1,8,2048]{4,0,2,1,3:T(4,128)(2,1)}), bf16[4,1,1,8,2048]{4,0,2,1,3:T(4,128)(2,1)S(1)}, u32[]{:S(2)}, u32[]{:S(2)}) async-start(bf16[4,1,1,8,2048]{4,0,2,1,3:T(4,128)(2,1)} %copy.67), calls=%async_computation | async-start | bytes 262144 | tf_op jit(solution)/shard_map/all_to_all | solution.py:171
  14.8 47.0 %copy-start.1 = (s32[1,1,8,2048]{3,2,1,0:T(8,128)S(1)}, s32[1,1,8,2048]{3,2,1,0:T(8,128)}, u32[]{:S(2)}) copy-start(s32[1,1,8,2048]{3,2,1,0:T(8,128)} %param.21) | copy-start | bytes 196612
  61.9 63.7 %copy-start = (bf16[1,16,32]{2,1,0:T(8,128)(2,1)S(1)}, bf16[1,16,32]{2,1,0:T(8,128)(2,1)}, u32[]{:S(2)}) copy-start(bf16[1,16,32]{2,1,0:T(8,128)(2,1)} %param.19) | copy-start | bytes 3076
  61.9 63.7 %copy-start.2 = (bf16[1,16]{1,0:T(2,128)(2,1)S(1)}, bf16[1,16]{1,0:T(2,128)(2,1)}, u32[]{:S(2)}) copy-start(bf16[1,16]{1,0:T(2,128)(2,1)} %param.20) | copy-start | bytes 100
  62.0 63.7 %copy-start.6 = (bf16[1,2,64,64]{3,2,1,0:T(8,128)(2,1)S(1)}, bf16[1,2,64,64]{3,2,1,0:T(8,128)(2,1)}, u32[]{:S(2)}) copy-start(bf16[1,2,64,64]{3,2,1,0:T(8,128)(2,1)} %param.17) | copy-start | bytes 49156
  62.0 63.7 %copy-start.7 = (bf16[1,64,32]{1,2,0:T(8,128)(2,1)S(1)}, bf16[1,64,32]{1,2,0:T(8,128)(2,1)}, u32[]{:S(2)}) copy-start(bf16[1,64,32]{1,2,0:T(8,128)(2,1)} %param.16) | copy-start | bytes 12292
  62.0 63.7 %copy-start.8 = (bf16[1,64]{1,0:T(2,128)(2,1)S(1)}, bf16[1,64]{1,0:T(2,128)(2,1)}, u32[]{:S(2)}) copy-start(bf16[1,64]{1,0:T(2,128)(2,1)} %param.18) | copy-start | bytes 388
  125.7 110.9 %copy-start.5 = (s32[1,1,8]{2,1,0:T(1,128)S(1)}, s32[1,1,8]{2,1,0:T(1,128)}, u32[]{:S(2)}) copy-start(s32[1,1,8]{2,1,0:T(1,128)} %param.25) | copy-start | bytes 100
  125.7 111.1 %copy-start.3 = (s32[1,1,8,32]{3,2,1,0:T(8,128)S(1)}, s32[1,1,8,32]{3,2,1,0:T(8,128)}, u32[]{:S(2)}) copy-start(s32[1,1,8,32]{3,2,1,0:T(8,128)} %param.23) | copy-start | bytes 3076
  125.7 111.1 %copy-start.4 = (s32[1,1,8,32]{3,2,1,0:T(8,128)S(1)}, s32[1,1,8,32]{3,2,1,0:T(8,128)}, u32[]{:S(2)}) copy-start(s32[1,1,8,32]{3,2,1,0:T(8,128)} %param.24) | copy-start | bytes 3076
  232.4 8.9 %all-to-all-start.1 = ((f32[8,1,160]{2,1,0:T(1,128)}), f32[8,1,160]{2,1,0:T(1,128)S(1)}, u32[]{:S(2)}, u32[]{:S(2)}) async-start(f32[8,1,160]{2,1,0:T(1,128)} %reshape.487), calls=%async_computation.1 | async-start | bytes 16384 | tf_op jit(solution)/shard_map/all_to_all | solution.py:192
  245.5 8.0 %all-to-all-start.2 = ((f32[3,1,1,8,32]{4,2,1,0,3:T(1,128)}), f32[3,1,1,8,32]{4,2,1,0,3:T(1,128)S(1)}, u32[]{:S(2)}, u32[]{:S(2)}) async-start(f32[3,1,1,8,32]{4,2,1,0,3:T(1,128)} %pad_maximum_fusion), calls=%async_computation.2 | async-start | bytes 24576 | tf_op jit(solution)/shard_map/all_to_all | solution.py:203
where the time goes:
time: 273 us; the launch traced here: 269 us
  local copies, waits for them, and re-layouts  215 us (79%)
  blocking collectives  13.1 us (5%)
  starting transfers between devices  12.7 us (5%)
  other arithmetic  10.8 us (4%)
  waiting for transfers between devices  8.22 us (3%)
  matrix products  8 us (3%)
    gather x4, local copies, waits for them, and re-layouts, interpolate(): rows = jnp.take(table, cell_index, axis=0)  90.3 us
    concatenate x1, local copies, waits for them, and re-layouts, corner_table(): return jnp.concatenate(pieces, axis=1)  63.3 us
    slice x1, local copies, waits for them, and re-layouts, corner_table(): pieces.append(padded[start:start + cell_total])  47 us
    psum x1, blocking collectives, on_device(): in_sum, out_sum = lax.psum((totals[0], totals[1]), 'rep')  13.1 us
    unnamed x27, local copies, waits for them, and re-layouts  10.3 us
  transfers between devices with their start and end apart: 3, of which 2 were waited for; matrix products, arithmetic and copies ran while one was open for 44% of the time, Pallas kernels for 0%

commit v1 on v0

v1 whole, which is shorter than its diff:
```python
import functools

import jax
import jax.numpy as jnp
from jax import lax
from jax.experimental import pallas as pl
from jax.experimental.pallas import tpu as pltpu
from jax.sharding import PartitionSpec as P

GR = 32
RAY_DEV = 256
LANES = 128
BLOCK = 256

distill_weight = 50.0
F32 = jnp.float32
BF16 = jnp.bfloat16


def dot(a, b):
    return lax.dot_general(a, b, (((1,), (0,)), ((), ())), preferred_element_type=F32)


def dot_nt(a, b):
    return lax.dot_general(a, b, (((1,), (1,)), ((), ())), preferred_element_type=F32)


def split3(x):
    hi = x.astype(BF16)
    rest = x - hi.astype(F32)
    mid = rest.astype(BF16)
    low = (rest - mid.astype(F32)).astype(BF16)
    return [hi, mid, low]


def gather_kernel(idx_ref, grid_ref, out_ref, table, shifted, near_a, far_a, near_b, far_b):
    step = pl.program_id(0)
    steps = pl.num_programs(0)
    cells = grid_ref.shape[1]
    plane = GR * GR
    width = out_ref.shape[1]
    blocks = width // BLOCK
    rows = lax.broadcasted_iota(jnp.int32, (BLOCK, BLOCK), 0)
    cols = lax.broadcasted_iota(jnp.int32, (BLOCK, BLOCK), 1)
    eye = (rows == cols).astype(BF16)

    def gather(block, near, far):
        row = block // blocks
        start = (block % blocks) * BLOCK
        for u in range(BLOCK):
            k = idx_ref[row, start + u]
            near[u : u + 1, :] = table[pl.ds(k, 1), :]
            far[u : u + 1, :] = table[pl.ds(k + 1, 1), :]

    @pl.when(step == 0)
    def _():
        span = 2048

        def shift(b, carry):
            c0 = pl.multiple_of(b * span, span)
            x = grid_ref[:, pl.ds(c0, span + LANES)]
            shifted[:, pl.ds(c0, span)] = x[:, GR : GR + span]
            return carry

        lax.fori_loop(0, cells // span - 1, shift, 0)
        last = grid_ref[:, cells - span :]
        shifted[:, cells - span :] = jnp.concatenate([last[:, GR:], last[:, :GR]], axis=1)

        def build(b, carry):
            c0 = pl.multiple_of(b * BLOCK, BLOCK)
            x = jnp.concatenate(
                [
                    grid_ref[:, pl.ds(c0, BLOCK)],
                    shifted[:, pl.ds(c0, BLOCK)],
                    grid_ref[:, pl.ds(c0 + plane, BLOCK)],
                    shifted[:, pl.ds(c0 + plane, BLOCK)],
                ],
                axis=0,
            )
            table[pl.ds(c0, BLOCK), :] = dot_nt(eye, x)
            return carry

        lax.fori_loop(0, (cells - plane) // BLOCK, build, 0, unroll=4)
        gather(0, near_a, far_a)

    def turn(j, near, far):
        d = jnp.concatenate([near[...].astype(BF16), far[...].astype(BF16)], axis=1)
        t = dot_nt(eye, d)
        out_ref[:, pl.ds(pl.multiple_of(j * BLOCK, BLOCK), BLOCK)] = t.astype(BF16)

    final = steps * blocks - 1

    def pair(i, carry):
        first = step * blocks + 2 * i
        gather(first + 1, near_b, far_b)
        turn(2 * i, near_a, far_a)
        gather(jnp.minimum(first + 2, final), near_a, far_a)
        turn(2 * i + 1, near_b, far_b)
        return carry

    lax.fori_loop(0, blocks // 2, pair, 0)


def gather_corners(cells, grid):
    parts, width = cells.shape
    features, total = grid.shape
    return pl.pallas_call(
        gather_kernel,
        grid=(parts,),
        out_shape=jax.ShapeDtypeStruct((8 * features, parts * width), BF16),
        in_specs=[
            pl.BlockSpec(memory_space=pltpu.SMEM),
            pl.BlockSpec((features, total), lambda q: (0, 0), pipeline_mode=pl.Buffered(1)),
        ],
        out_specs=pl.BlockSpec((8 * features, width), lambda q: (0, q)),
        scratch_shapes=[
            pltpu.VMEM((total, LANES), F32),
            pltpu.VMEM((features, total), BF16),
        ]
        + [pltpu.VMEM((BLOCK, LANES), F32)] * 4,
        compiler_params=pltpu.CompilerParams(vmem_limit_bytes=40 * 1024 * 1024),
        name="gather_corners",
    )(cells, grid)


def lane_fold(x, cap):
    shift = LANES // 2
    while shift >= cap:
        x = x + pltpu.roll(x, shift, 1)
        shift //= 2
    return x


def running(pieces, cap):
    lane = lax.broadcasted_iota(jnp.int32, pieces[0].shape, 1)
    carry = jnp.zeros_like(pieces[0])
    out = []
    for x in pieces:
        y = x
        shift = cap
        while shift < LANES:
            y = y + jnp.where(lane >= shift, pltpu.roll(y, shift, 1), 0.0)
            shift *= 2
        out.append(carry + y)
        carry = carry + lane_fold(x, cap)
    return out, carry


def trailing(pieces, cap):
    lane = lax.broadcasted_iota(jnp.int32, pieces[0].shape, 1)
    carry = jnp.zeros_like(pieces[0])
    out = []
    for x in reversed(pieces):
        y = x
        shift = cap
        while shift < LANES:
            y = y + jnp.where(lane < LANES - shift, pltpu.roll(y, LANES - shift, 1), 0.0)
            shift *= 2
        out.append(carry + y)
        carry = carry + lane_fold(x, cap)
    return out[::-1]


def softplus(x):
    return jnp.maximum(x, 0.0) + jnp.log1p(jnp.exp(-jnp.abs(x)))


def pieces_of(x):
    return [x[:, v * LANES : (v + 1) * LANES] for v in range(x.shape[1] // LANES)]


def forward_kernel(
    cap, corners_ref, geometry_ref, first_ref, mid_ref, head_ref,
    saved_ref, dense_ref, summary_ref, weights, fine_logit, prop_logit,
):
    step = pl.program_id(0)
    features = corners_ref.shape[0] // 8
    hidden = mid_ref.shape[1]
    width = corners_ref.shape[1]

    @pl.when(step == 0)
    def _():
        g = [geometry_ref[j].astype(F32) for j in range(3)]
        for corner in range(8):
            bits = (corner // 4, corner // 2 % 2, corner % 2)
            w = [x if bit else 1.0 - x for x, bit in zip(g, bits)]
            weights[corner] = w[0] * w[1] * w[2]

    feats = []
    for v in range(width // BLOCK):
        at = v * BLOCK
        total = jnp.zeros((features, BLOCK), F32)
        for corner in range(8):
            place = (corner % 2) * 4 + corner // 2
            x = corners_ref[place * features : (place + 1) * features, at : at + BLOCK].astype(F32)
            total = total + x * weights[corner, pl.ds(step, 1), at : at + BLOCK]
        feats.append(total.astype(BF16))
    feat = jnp.concatenate(feats, axis=1)
    both = jnp.maximum(dot(first_ref[...], feat), 0.0).astype(BF16)
    h = both[:hidden]
    ph = both[hidden:]
    for layer in range(mid_ref.shape[0]):
        h = jnp.maximum(dot(mid_ref[layer], h), 0.0).astype(BF16)
    logits = dot(head_ref[...], jnp.concatenate([h, ph], axis=0))
    fine_logit[pl.ds(step, 1), :] = logits[0:1]
    prop_logit[pl.ds(step, 1), :] = logits[1:2]
    saved_ref[:features, :] = feat
    saved_ref[features:, :] = ph

    @pl.when(step == pl.num_programs(0) - 1)
    def _():
        space = pieces_of(geometry_ref[3].astype(F32))
        results = []
        for k, ref in enumerate((prop_logit, fine_logit)):
            logit = pieces_of(ref[...])
            optical = [softplus(x) * s for x, s in zip(logit, space)]
            depth, whole = running(optical, cap)
            early = [jnp.exp(o - d) for o, d in zip(optical, depth)]
            absorb = [e - jnp.exp(-d) for e, d in zip(early, depth)]
            results.append((absorb, whole))
            if k == 0:
                slope = [s * jax.nn.sigmoid(x) for x, s in zip(logit, space)]
                dense_ref[0] = jnp.concatenate(early, axis=1)
                dense_ref[3] = jnp.concatenate(slope, axis=1)
        (a, log_prop), (b, log_fine) = results
        dense_ref[1] = jnp.concatenate(a, axis=1)
        dense_ref[2] = jnp.concatenate(b, axis=1)
        sums = [lane_fold(sum(x * y for x, y in zip(s, t)), cap) for s, t in ((a, a), (a, b), (b, b))]
        stats = [-log_prop, -log_fine] + sums
        per = LANES // cap
        group = lax.broadcasted_iota(jnp.int32, stats[0].shape, 1) // cap
        slabs = []
        for s in range(-(-len(stats) // per)):
            slab = jnp.zeros_like(stats[0])
            for k, x in enumerate(stats[s * per : (s + 1) * per]):
                slab = jnp.where(group == k, x, slab)
            slabs.append(slab)
        summary_ref[...] = jnp.concatenate(slabs, axis=1)


def forward(corners, geometry, first, mid, head, cap):
    rows, total = corners.shape
    parts, width = geometry.shape[1:]
    features = rows // 8
    prop_hidden = first.shape[0] - mid.shape[1]
    kept = features + prop_hidden
    stat_lanes = -(-5 // (LANES // cap)) * LANES
    whole = lambda shape: pl.BlockSpec(shape, lambda q: (0,) * len(shape))
    return pl.pallas_call(
        functools.partial(forward_kernel, cap),
        grid=(parts,),
        out_shape=(
            jax.ShapeDtypeStruct((kept, total), BF16),
            jax.ShapeDtypeStruct((4, parts, width), F32),
            jax.ShapeDtypeStruct((parts, stat_lanes), F32),
        ),
        in_specs=[
            pl.BlockSpec((rows, width), lambda q: (0, q)),
            whole(geometry.shape),
            whole(first.shape),
            whole(mid.shape),
            whole(head.shape),
        ],
        out_specs=(
            pl.BlockSpec((kept, width), lambda q: (0, q)),
            whole((4, parts, width)),
            whole((parts, stat_lanes)),
        ),
        scratch_shapes=[
            pltpu.VMEM((8, parts, width), F32),
            pltpu.VMEM((parts, width), F32),
            pltpu.VMEM((parts, width), F32),
        ],
        compiler_params=pltpu.CompilerParams(vmem_limit_bytes=32 * 1024 * 1024),
        name="forward",
    )(corners, geometry, first, mid, head)


def backward_kernel(
    cap, me_ref, stats_ref, key_ref, dense_ref, saved_ref, out_col_ref,
    loss_ref, grad_ref, keys_t, slope_ref, *masks,
):
    me = me_ref[0]
    parts = stats_ref.shape[0]
    slots = key_ref.shape[1]
    per = LANES // cap
    width = dense_ref.shape[2]
    prop_hidden = out_col_ref.shape[0]
    key = key_ref[...]
    live = (key >= 0).astype(F32)
    sub = lax.broadcasted_iota(jnp.int32, (parts, slots), 0)
    keys_t[...] = key.T

    def mask_of(q):
        if isinstance(q, int):
            col = keys_t[:, q : q + 1]
            row = key[q : q + 1]
        else:
            lane = lax.broadcasted_iota(jnp.int32, (slots, parts), 1)
            col = jnp.sum(jnp.where(lane == q, keys_t[...], 0.0), axis=1, keepdims=True)
            row = jnp.sum(jnp.where(sub == q, key, 0.0), axis=0, keepdims=True)
        gap = row - col
        return ((gap > 0) & (gap < parts)).astype(BF16)

    if masks:
        for q in range(parts):
            masks[0][q] = mask_of(q)

    def over(body, init):
        if masks:
            for q in range(parts):
                init = body(q, init)
            return init
        return lax.fori_loop(0, parts, body, init)

    group = lax.broadcasted_iota(jnp.int32, (parts, LANES), 1) // cap

    def flat(j):
        slab = slice((j // per) * LANES, (j // per + 1) * LANES)
        out = []
        for half in range(slots // LANES):
            x = jnp.zeros((parts, LANES), F32)
            for k in range(per):
                piece = stats_ref[half * per + k, :, slab]
                shift = ((k - j % per) * cap) % LANES
                x = jnp.where(group == k, pltpu.roll(piece, shift, 1) if shift else piece, x)
            out.append(x)
        return jnp.concatenate(out, axis=1)

    log_prop, log_fine, sum_aa, sum_ab, sum_bb = [flat(j) for j in range(5)]
    terms = split3(log_prop * live) + split3(log_fine * live)
    stacked = jnp.concatenate(terms, axis=0)

    def lead(q, acc):
        m = masks[0][q] if masks else mask_of(q)
        y = dot(stacked, m)
        return tuple(
            jnp.where(sub == q, y[k * parts : (k + 1) * parts], x) for k, x in enumerate(acc)
        )

    zero = jnp.zeros((parts, slots), F32)
    lead_sums = over(lead, (zero,) * 6)
    entry_prop = jnp.exp(lead_sums[0] + lead_sums[1] + lead_sums[2]) * live
    entry_fine = jnp.exp(lead_sums[3] + lead_sums[4] + lead_sums[5]) * live
    seg_loss = (
        entry_prop * entry_prop * sum_aa
        - 2.0 * entry_prop * entry_fine * sum_ab
        + entry_fine * entry_fine * sum_bb
    )
    slot_grad = distill_weight * (entry_prop * sum_aa - entry_fine * sum_ab) * entry_prop
    mine = pl.ds(pl.multiple_of(me * cap, cap), cap)
    grads = jnp.concatenate(split3(slot_grad), axis=0)
    sub_cap = lax.broadcasted_iota(jnp.int32, (parts, cap), 0)

    def tail(q, acc):
        if masks:
            m = masks[0][q, mine, :]
            y = dot_nt(grads, m)
        else:
            y = dot_nt(grads, mask_of(q))
            y = own_lanes(y)
        y = y[:parts] + y[parts : 2 * parts] + y[2 * parts :]
        return jnp.where(sub_cap == q, y, acc)

    def own_lanes(x):
        out = x[:, :cap]
        for p in range(1, parts):
            out = jnp.where(me == p, x[:, p * cap : (p + 1) * cap], out)
        return out

    carried = over(tail, jnp.zeros((parts, cap), F32)) * own_lanes(live)
    coef_aa = own_lanes(0.5 * distill_weight * entry_prop * entry_prop)
    coef_ab = own_lanes(-distill_weight * entry_prop * entry_fine)

    lane_me = lax.broadcasted_iota(jnp.int32, (slots, parts), 1)
    key_col = jnp.sum(jnp.where(lane_me == me, keys_t[...], 0.0), axis=1, keepdims=True)
    ray = lax.broadcasted_iota(jnp.int32, (slots, RAY_DEV), 1).astype(F32)
    rest = key_col - ray * (2.0 * parts)
    hot = ((rest >= 0) & (rest < 2 * parts)).astype(BF16)
    spread = dot(jnp.concatenate(split3(seg_loss), axis=0), hot)
    spread = spread[:parts] + spread[parts : 2 * parts] + spread[2 * parts :]
    sub_ray = lax.broadcasted_iota(jnp.int32, (parts, RAY_DEV), 0)
    loss_ref[...] = (0.5 * distill_weight) * jnp.sum(
        jnp.where(sub_ray == me, spread, 0.0), axis=0, keepdims=True
    )

    tile = lambda x: jnp.concatenate([x] * per, axis=1)
    c_aa, c_ab, c_log = tile(2.0 * coef_aa), tile(coef_ab), tile(carried)
    early, a, b, slope = [pieces_of(dense_ref[k]) for k in range(4)]
    d_absorb = [c_aa * x + c_ab * y for x, y in zip(a, b)]
    back = trailing([d * x for d, x in zip(d_absorb, a)], cap)
    logit_grad = [
        ((d * e - c_log - r) * s).astype(BF16).astype(F32)
        for d, e, r, s in zip(d_absorb, early, back, slope)
    ]
    slope_ref[...] = jnp.concatenate(logit_grad, axis=1)
    features = saved_ref.shape[0] - prop_hidden
    out_col = out_col_ref[...].astype(F32)
    first_row = lax.broadcasted_iota(jnp.int32, (prop_hidden, width), 0) == 0

    def accumulate(q, total):
        at = pl.ds(pl.multiple_of(q * width, width), width)
        row = slope_ref[pl.ds(q, 1), :]
        kept = saved_ref[:, at]
        hidden_grad = jnp.where(kept[features:].astype(F32) > 0, out_col * row, 0.0).astype(BF16)
        alone = jnp.where(first_row, row, 0.0).astype(BF16)
        return total + dot_nt(jnp.concatenate([hidden_grad, alone], axis=0), kept)

    total = jnp.zeros((2 * prop_hidden, saved_ref.shape[0]), F32)
    total = lax.fori_loop(0, parts, accumulate, total)
    grad_ref[...] = total


def backward(me, stats, key, dense, saved, out_col, cap):
    parts, slots = key.shape
    width = dense.shape[2]
    prop_hidden = out_col.shape[0]
    vmem = pl.BlockSpec(memory_space=pltpu.VMEM)
    keep = [pltpu.VMEM((parts, slots, slots), BF16)] if slots <= 256 else []
    return pl.pallas_call(
        functools.partial(backward_kernel, cap),
        out_shape=(
            jax.ShapeDtypeStruct((1, RAY_DEV), F32),
            jax.ShapeDtypeStruct((2 * prop_hidden, saved.shape[0]), F32),
        ),
        in_specs=[pl.BlockSpec(memory_space=pltpu.SMEM)] + [vmem] * 5,
        out_specs=(vmem, vmem),
        scratch_shapes=[pltpu.VMEM((slots, parts), F32), pltpu.VMEM((parts, width), F32)] + keep,
        compiler_params=pltpu.CompilerParams(vmem_limit_bytes=48 * 1024 * 1024),
        name="backward",
    )(me, stats, key, dense, saved, out_col)


def sum_replicas(x):
    count = lax.axis_size("rep")
    if count != 4:
        return lax.psum(x, "rep")
    other = [lax.ppermute(x, "rep", [(i, i ^ s) for i in range(count)]) for s in (1, 2, 3)]
    return (x + other[0]) + (other[1] + other[2])


def on_device(
    feature_grid,
    fine_in,
    fine_mid,
    fine_out,
    prop_in,
    prop_out,
    sample_cells,
    sample_geometry,
    slot_ray,
    slot_rank,
    bucket_count,
):
    parts = lax.axis_size("dom")
    cap = slot_ray.shape[3]
    width = sample_cells.shape[3]
    features = feature_grid.shape[1]
    prop_hidden = prop_in.shape[1]
    slots = parts * cap

    live = jnp.arange(cap)[None, :] < bucket_count[0, 0][:, None]
    ray = jnp.where(live, slot_ray[0, 0], -1).reshape(-1)
    marks = jnp.concatenate([ray, slot_rank[0, 0].reshape(-1)]).astype(BF16)
    extra = -(-2 * slots // width)
    marks = jnp.pad(marks, (0, extra * width - 2 * slots)).reshape(extra, 1, width)
    outgoing = jnp.concatenate(
        [sample_geometry[:, 0, 0], jnp.broadcast_to(marks, (extra, parts, width))], axis=0
    )
    arrived = lax.all_to_all(outgoing, "dom", split_axis=1, concat_axis=1, tiled=True)

    corners = gather_corners(sample_cells[0, 0], feature_grid[0])

    geometry = arrived[:4]
    marks = jnp.moveaxis(arrived[4:], 0, 1).reshape(parts, extra * width)[:, : 2 * slots].astype(F32)
    key = marks[:, :slots] * (2.0 * parts) + marks[:, slots:]
    first = jnp.concatenate([fine_in[0], prop_in[0]], axis=0)
    head = jnp.concatenate(
        [
            jnp.pad(fine_out, ((0, 0), (0, prop_hidden))),
            jnp.pad(prop_out, ((0, 0), (fine_out.shape[1], 0))),
        ],
        axis=0,
    )
    head = jnp.pad(head, ((0, 6), (0, 0)))
    saved, dense, summary = forward(corners, geometry, first, fine_mid[0], head, cap)

    stats = lax.all_to_all(
        jnp.broadcast_to(summary[None], (parts,) + summary.shape),
        "dom", split_axis=0, concat_axis=0, tiled=True,
    )
    me = lax.axis_index("dom").reshape(1).astype(jnp.int32)
    ray_loss, grads = backward(me, stats, key, dense, saved, prop_out.reshape(-1, 1), cap)
    sums = sum_replicas(grads)
    in_sum = sums[:prop_hidden, :features]
    out_sum = sums[prop_hidden, features:]
    return (ray_loss.reshape(1, 1, -1), in_sum[None], out_sum[None])


def solution(mesh):
    return jax.shard_map(
        on_device,
        mesh=mesh,
        in_specs=(
            P("dom", None, None),
            P("dom", None, None),
            P("dom", None, None, None),
            P("dom", None),
            P("dom", None, None),
            P("dom", None),
            P("dom", "rep", None, None),
            P(None, "dom", "rep", None, None),
            P("dom", "rep", None, None),
            P("dom", "rep", None, None),
            P("dom", "rep", None),
        ),
        out_specs=(P("dom", "rep", None), P("dom", None, None), P("dom", None)),
        check_vma=False,
    )
```

time: 273 us -> 113 us (0.41); the launches traced: 269 us -> 113 us
  local copies, waits for them, and re-layouts: 215 us -> 14.7 us
  Pallas kernels: 0 us -> 70.9 us
  blocking collectives: 13.1 us -> 0 us
  matrix products: 8 us -> 0 us
  other arithmetic: 10.8 us -> 3.85 us
    gather x4 -> x0, local copies, waits for them, and re-layouts: 90.3 us -> none  [interpolate(): rows = jnp.take(table, cell_index, axis=0)]
    pallas_call x0 -> x3, Pallas kernels: none -> 70.9 us  [the longest x1 59.4 us: gather_corners(): pl.pallas_call(gather_kernel, grid=(parts,), out_shape=jax.ShapeDtypeStru...]
    concatenate x1, local copies, waits for them, and re-layouts: 63.3 us -> 0.1 us  [on_device(): first = jnp.concatenate([fine_in[0], prop_in[0]], axis=0)]
    slice x5 -> x3, local copies, waits for them, and re-layouts: 47.2 us -> 0.7 us  [the longest x1 0.58 us: on_device(): out_sum = sums[prop_hidden, features:]]
    psum x1 -> x0, blocking collectives: 13.1 us -> none  [on_device(): in_sum, out_sum = lax.psum((totals[0], totals[1]), 'rep')]
    dot_general x27 -> x0, matrix products: 8 us -> none  [the longest x2 1.5 us: fine_density(): jnp.dot(fine_mid[layer_index], hidden_units, preferred_element_type=jnp.f...]
    select_n x8 -> x0, other arithmetic: 5.47 us -> none  [the longest x4 5.36 us: interpolate(): rows = jnp.take(table, cell_index, axis=0)]
    ppermute x0 -> x3, starting transfers between devices: none -> 4.39 us  [sum_replicas(): lax.ppermute(x, 'rep', [(i, i ^ s) for i in range(count)])]
  transfers between devices with their start and end apart: 3 -> 5, of which waited for: 2 -> 3; matrix products, arithmetic and copies ran while one was open for 44% -> 3% of each run, Pallas kernels for 0% -> 53%
where the time goes in v1:
time: 113 us
  Pallas kernels  70.9 us (63%)
  local copies, waits for them, and re-layouts  14.7 us (13%)
  starting transfers between devices  13.8 us (12%)
  waiting for transfers between devices  8.86 us (8%)
  other arithmetic  3.85 us (3%)
    pallas_call x1, Pallas kernels, gather_corners(): pl.pallas_call(gather_kernel, grid=(parts,), out_shape=jax.ShapeDtypeStru...  59.4 us
    unnamed x14, local copies, waits for them, and re-layouts  10.9 us
    pallas_call x1, Pallas kernels, forward(): pl.pallas_call(functools.partial(forward_kernel, cap), grid=(parts,), out...  7.61 us
    all_to_all x1, starting transfers between devices, on_device(): lax.all_to_all(outgoing, 'dom', split_axis=1, concat_axis=1, tiled=True)  5.2 us
    all_to_all x1, waiting for transfers between devices, on_device(): lax.all_to_all(jnp.broadcast_to(summary[None], (parts,) + summary.shape),...  5.01 us
    ppermute x3, starting transfers between devices, sum_replicas(): lax.ppermute(x, 'rep', [(i, i ^ s) for i in range(count)])  4.39 us
    all_to_all x1, starting transfers between devices, on_device(): lax.all_to_all(jnp.broadcast_to(summary[None], (parts,) + summary.shape),...  4.2 us
    pallas_call x1, Pallas kernels, backward(): pl.pallas_call(functools.partial(backward_kernel, cap), out_shape=(jax.Sh...  3.89 us
  transfers between devices with their start and end apart: 5, of which 3 were waited for; matrix products, arithmetic and copies ran while one was open for 3% of the time, Pallas kernels for 53%

profile of v1, /device:TPU:0, one launch (start us, length us, event | category | flops | bytes accessed | tf_op | source)
XLA Modules:
  0.0 112.8 jit_solution(10327865248193354277)
XLA Ops:
  0.6 0.8 squeeze.24
  1.4 0.7 iota_compare_fusion.1
  2.2 0.7 convert.8
  3.0 1.0 copy.26
  4.1 0.9 pad_maximum_fusion
  4.9 5.2 %all-to-all-start = ((bf16[5,8,2048]{2,0,1:T(8,128)(2,1)}), bf16[5,8,2048]{2,0,1:T(8,128)(2,1)S(1)}, u32[]{:S(2)}, u32[]{:S(2)}) async-start(bf16[5,8,2048]{2,0,1:T(8,128)(2,1)} %pad_maximum_fusion), calls=%async_computation | async-start | bytes 524288 | tf_op jit(solution)/shard_map/all_to_all | solution.py:470
  10.1 0.8 copy.18
  10.9 0.8 pad_maximum_fusion.1
  11.7 0.7 copy.21.out_col_ref
  12.5 0.8 fusion.3
  13.3 1.6 %copy-done.2 = bf16[1,32,32768]{2,1,0:T(8,128)(2,1)S(1)} copy-done((bf16[1,32,32768]{2,1,0:T(8,128)(2,1)S(1)}, bf16[1,32,32768]{2,1,0:T(8,128)(2,1)}, u32[]{:S(2)}) %copy-start.2) | copy-done | bytes 2097176
  14.9 0.8 copy-done.3
  15.7 59.4 %gather_corners.1.corners_ref = bf16[256,16384]{1,0:T(8,128)(2,1)S(1)} custom-call(s32[8,2048]{1,0:T(8,128)S(1)} %bitcast.22, bf16[32,32768]{1,0:T(8,128)(2,1)S(1)} %bitcast.21), custom_call_target="tpu_custom_call" | custom-call | tf_op jit(solution)/shard_map/gather_corners/pallas_call | solution.py:107
  75.2 3.2 %copy-done = bf16[256,16384]{1,0:T(8,128)(2,1)} copy-done((bf16[256,16384]{1,0:T(8,128)(2,1)}, bf16[256,16384]{1,0:T(8,128)(2,1)S(1)}, u32[]{:S(2)}) %copy-start) | copy-done | bytes 8388632
  78.7 3.4 %copy-done.1 = bf16[256,16384]{1,0:T(8,128)(2,1)S(1)} copy-done((bf16[256,16384]{1,0:T(8,128)(2,1)S(1)}, bf16[256,16384]{1,0:T(8,128)(2,1)}, u32[]{:S(2)}) %copy-start.1) | copy-done | bytes 8388632
  82.0 7.6 %forward.1 = (bf16[48,16384]{1,0:T(8,128)(2,1)S(1)}, f32[4,8,2048]{2,1,0:T(8,128)S(1)}, f32[8,256]{1,0:T(8,128)S(1)}) custom-call(bf16[256,16384]{1,0:T(8,128)(2,1)S(1)} %copy-done.1, bf16[4,8,2048]{2,1,0:T(8,128)(2,1)S(1)} %copy.22.geometry_ref, bf16[80,32]{1,0:T(8,128)(2,1)S(1)} %copy.19.first_ref, bf16[2,64,64]{2,1,0:T(8,128)(2,1)S(1)} %bitcast.23, ...), custom_call_target="tpu_custom_call" | custom-call | tf_op jit(solution)/shard_map/forward/pallas_call | solution.py:249
  89.6 0.6 broadcast_in_dim.21
  90.3 4.2 %all-to-all-start.1 = ((f32[8,8,256]{2,1,0:T(8,128)}), f32[8,8,256]{2,1,0:T(8,128)S(1)}, u32[]{:S(2)}, u32[]{:S(2)}) async-start(f32[8,8,256]{2,1,0:T(8,128)} %broadcast_in_dim.21), calls=%async_computation.1 | async-start | bytes 131072 | tf_op jit(solution)/shard_map/all_to_all | solution.py:488
  94.5 5.0 %all-to-all-done.1.stats_ref = f32[8,8,256]{2,1,0:T(8,128)S(1)} async-done(((f32[8,8,256]{2,1,0:T(8,128)}), f32[8,8,256]{2,1,0:T(8,128)S(1)}, u32[]{:S(2)}, u32[]{:S(2)}) %all-to-all-start.1) | async-done | bytes 65568 | tf_op jit(solution)/shard_map/all_to_all | solution.py:488
  99.5 3.9 %backward.1 = (f32[1,256]{1,0:T(1,128)}, f32[32,48]{1,0:T(8,128)S(1)}) custom-call(s32[1]{0:T(128)} %bitcast.me_ref, f32[8,8,256]{2,1,0:T(8,128)S(1)} %all-to-all-done.1.stats_ref, f32[8,256]{1,0:T(8,128)S(1)} %slice_add_fusion.key_ref, f32[4,8,2048]{2,1,0:T(8,128)S(1)} %get-tuple-element.9.dense_ref, bf16[48,16384]{1,0:T(8,128)(2,1)S(1)} %get-tuple-element.10.saved_ref, ...), custom_call_target="tpu_custom_call" | custom-call | tf_op jit(solution)/shard_map/backward/pallas_call | solution.py:420
  103.4 3.6 %collective-permute-start.2 = (f32[32,48]{1,0:T(8,128)S(1)}, f32[32,48]{1,0:T(8,128)S(1)}, u32[]{:S(2)}, u32[]{:S(2)}) collective-permute-start(f32[32,48]{1,0:T(8,128)S(1)} %get-tuple-element.12), channel_id=1, source_target_pairs={{0,3},{1,2},{2,1},{3,0},{4,7},{5,6},{6,5},{7,4},{8,11},{9,10},{10,... | collective-permute-start | bytes 18440 | tf_op jit(solution)/shard_map/ppermute | solution.py:438
  107.0 0.8 collective-permute-start
  107.8 1.2 %collective-permute-done.2 = f32[32,48]{1,0:T(8,128)S(1)} collective-permute-done((f32[32,48]{1,0:T(8,128)S(1)}, f32[32,48]{1,0:T(8,128)S(1)}, u32[]{:S(2)}, u32[]{:S(2)}) %collective-permute-start.2) | collective-permute-done | bytes 6176 | tf_op jit(solution)/shard_map/ppermute | solution.py:438
  109.0 2.6 %collective-permute-done.1 = f32[32,48]{1,0:T(8,128)S(1)} collective-permute-done((f32[32,48]{1,0:T(8,128)S(1)}, f32[32,48]{1,0:T(8,128)S(1)}, u32[]{:S(2)}, u32[]{:S(2)}) %collective-permute-start.1) | collective-permute-done | bytes 6176 | tf_op jit(solution)/shard_map/ppermute | solution.py:438
  (25 shorter events, 1.8 us)
Async XLA Ops:
  4.9 73.4 %all-to-all-start = ((bf16[5,8,2048]{2,0,1:T(8,128)(2,1)}), bf16[5,8,2048]{2,0,1:T(8,128)(2,1)S(1)}, u32[]{:S(2)}, u32[]{:S(2)}) async-start(bf16[5,8,2048]{2,0,1:T(8,128)(2,1)} %pad_maximum_fusion), calls=%async_computation | async-start | bytes 524288 | tf_op jit(solution)/shard_map/all_to_all | solution.py:470
  13.3 1.6 %copy-start.2 = (bf16[1,32,32768]{2,1,0:T(8,128)(2,1)S(1)}, bf16[1,32,32768]{2,1,0:T(8,128)(2,1)}, u32[]{:S(2)}) copy-start(bf16[1,32,32768]{2,1,0:T(8,128)(2,1)} %param.11) | copy-start | bytes 6291460
  14.9 0.8 copy-start.3
  15.7 62.9 %copy-start.4 = (bf16[1,2,64,64]{3,2,1,0:T(8,128)(2,1)S(1)}, bf16[1,2,64,64]{3,2,1,0:T(8,128)(2,1)}, u32[]{:S(2)}) copy-start(bf16[1,2,64,64]{3,2,1,0:T(8,128)(2,1)} %param.13) | copy-start | bytes 49156
  75.1 3.2 %copy-start = (bf16[256,16384]{1,0:T(8,128)(2,1)}, bf16[256,16384]{1,0:T(8,128)(2,1)S(1)}, u32[]{:S(2)}) copy-start(bf16[256,16384]{1,0:T(8,128)(2,1)S(1)} %gather_corners.1.corners_ref) | copy-start | bytes 25165828
  78.6 3.4 %copy-start.1 = (bf16[256,16384]{1,0:T(8,128)(2,1)S(1)}, bf16[256,16384]{1,0:T(8,128)(2,1)}, u32[]{:S(2)}) copy-start(bf16[256,16384]{1,0:T(8,128)(2,1)} %copy-done) | copy-start | bytes 25165828
  90.3 9.2 %all-to-all-start.1 = ((f32[8,8,256]{2,1,0:T(8,128)}), f32[8,8,256]{2,1,0:T(8,128)S(1)}, u32[]{:S(2)}, u32[]{:S(2)}) async-start(f32[8,8,256]{2,1,0:T(8,128)} %broadcast_in_dim.21), calls=%async_computation.1 | async-start | bytes 131072 | tf_op jit(solution)/shard_map/all_to_all | solution.py:488
  103.4 5.6 %collective-permute-start.2 = (f32[32,48]{1,0:T(8,128)S(1)}, f32[32,48]{1,0:T(8,128)S(1)}, u32[]{:S(2)}, u32[]{:S(2)}) collective-permute-start(f32[32,48]{1,0:T(8,128)S(1)} %get-tuple-element.12), channel_id=1, source_target_pairs={{0,3},{1,2},{2,1},{3,0},{4,7},{5,6},{6,5},{7,4},{8,11},{9,10},{10,... | collective-permute-start | bytes 18440 | tf_op jit(solution)/shard_map/ppermute | solution.py:438
  107.0 4.6 %collective-permute-start.1 = (f32[32,48]{1,0:T(8,128)S(1)}, f32[32,48]{1,0:T(8,128)S(1)}, u32[]{:S(2)}, u32[]{:S(2)}) collective-permute-start(f32[32,48]{1,0:T(8,128)S(1)} %get-tuple-element.12), channel_id=1, source_target_pairs={{0,2},{1,3},{2,0},{3,1},{4,6},{5,7},{6,4},{7,5},{8,10},{9,11},{10,... | collective-permute-start | bytes 18440 | tf_op jit(solution)/shard_map/ppermute | solution.py:438
  107.0 4.6 %collective-permute-start = (f32[32,48]{1,0:T(8,128)S(1)}, f32[32,48]{1,0:T(8,128)S(1)}, u32[]{:S(2)}, u32[]{:S(2)}) collective-permute-start(f32[32,48]{1,0:T(8,128)S(1)} %get-tuple-element.12), channel_id=1, source_target_pairs={{0,1},{1,0},{2,3},{3,2},{4,5},{5,4},{6,7},{7,6},{8,9},{9,8},{10,11... | collective-permute-start | bytes 18440 | tf_op jit(solution)/shard_map/ppermute | solution.py:438

commit v2 on v1

--- a/solution.py
+++ b/solution.py
@@ -11,6 +11,8 @@
 RAY_DEV = 256
 LANES = 128
 BLOCK = 256
+BUILD_UNROLL = 31
+DEPTH = 4
 
 distill_weight = 50.0
 F32 = jnp.float32
@@ -33,27 +35,128 @@
     return [hi, mid, low]
 
 
-def gather_kernel(idx_ref, grid_ref, out_ref, table, shifted, near_a, far_a, near_b, far_b):
+def stack_rows(arrays, row):
+    return jnp.concatenate([x[row : row + 1] for x in arrays], axis=0)
+
+
+def flatten_slots(x, cap):
+    parts = x.shape[0]
+    per = LANES // cap
+    lane = lax.broadcasted_iota(jnp.int32, (1, LANES), 1)
+    wide = jnp.concatenate([x] * per, axis=1)
+    out = []
+    for first in range(0, parts, per):
+        row = wide[first : first + 1]
+        for k in range(1, per):
+            row = jnp.where(lane // cap == k, wide[first + k : first + k + 1], row)
+        out.append(row)
+    return jnp.concatenate(out, axis=1)
+
+
+def pack_kernel(geometry_ref, ray_ref, rank_ref, count_ref, out_ref):
+    parts, cap = ray_ref.shape
+    width = geometry_ref.shape[2]
+    extra = out_ref.shape[1] - 4
+    live = lax.broadcasted_iota(jnp.int32, (parts, cap), 1) < count_ref[...]
+    ray = jnp.where(live, ray_ref[...], -1).astype(F32)
+    marks = jnp.concatenate(
+        [flatten_slots(ray, cap), flatten_slots(rank_ref[...].astype(F32), cap)], axis=1
+    )
+    spare = extra * width - marks.shape[1]
+    if spare:
+        marks = jnp.concatenate([marks, jnp.zeros((1, spare), F32)], axis=1)
+    marks = [marks[:, e * width : (e + 1) * width] for e in range(extra)]
+    g = [geometry_ref[j].astype(F32) for j in range(4)]
+    for p in range(parts):
+        block = [x[p : p + 1] for x in g] + marks
+        out_ref[p] = jnp.concatenate(block, axis=0).astype(BF16)
+
+
+def pack(geometry, ray, rank, count):
+    parts, width = geometry.shape[1:]
+    extra = -(-2 * ray.size // width)
+    vmem = pl.BlockSpec(memory_space=pltpu.VMEM)
+    return pl.pallas_call(
+        pack_kernel,
+        out_shape=jax.ShapeDtypeStruct((parts, 4 + extra, width), BF16),
+        in_specs=[vmem] * 4,
+        out_specs=vmem,
+        name="pack",
+    )(geometry, ray, rank, count)
+
+
+def marks_kernel(cap, me_ref, arrived_ref, key_ref, hot_ref, *mask_ref):
+    me = me_ref[0]
+    parts = arrived_ref.shape[0]
+    slots = parts * cap
+    width = arrived_ref.shape[2]
+    extra = arrived_ref.shape[1] - 4
+    ray, rank = [], []
+    for q in range(parts):
+        marks = [arrived_ref[q].astype(F32)[4 + e : 5 + e] for e in range(extra)]
+        marks = marks[0] if extra == 1 else jnp.concatenate(marks, axis=1)
+        ray.append(marks[:, :slots])
+        rank.append(marks[:, slots : 2 * slots])
+    key = jnp.concatenate(ray, axis=0) * (2.0 * parts) + jnp.concatenate(rank, axis=0)
+    key_ref[...] = key
+    key_t = key.T
+    mine = lax.broadcasted_iota(jnp.int32, (slots, parts), 1) == me
+    key_col = jnp.sum(jnp.where(mine, key_t, 0.0), axis=1, keepdims=True)
+    ray = lax.broadcasted_iota(jnp.int32, (slots, RAY_DEV), 1).astype(F32)
+    rest = key_col - ray * (2.0 * parts)
+    hot_ref[...] = ((rest >= 0) & (rest < 2 * parts)).astype(BF16)
+    if mask_ref:
+        for q in range(parts):
+            gap = key[q : q + 1] - key_t[:, q : q + 1]
+            mask_ref[0][q] = ((gap > 0) & (gap < parts)).astype(BF16)
+
+
+def slot_marks(me, arrived, cap):
+    parts = arrived.shape[0]
+    slots = parts * cap
+    vmem = pl.BlockSpec(memory_space=pltpu.VMEM)
+    shapes = [
+        jax.ShapeDtypeStruct((parts, slots), F32),
+        jax.ShapeDtypeStruct((slots, RAY_DEV), BF16),
+    ]
+    if slots <= 256:
+        shapes.append(jax.ShapeDtypeStruct((parts, slots, slots), BF16))
+    return pl.pallas_call(
+        functools.partial(marks_kernel, cap),
+        out_shape=tuple(shapes),
+        in_specs=[pl.BlockSpec(memory_space=pltpu.SMEM), vmem],
+        out_specs=(vmem,) * len(shapes),
+        cost_estimate=pl.CostEstimate(
+            flops=parts * slots * slots * 8, bytes_accessed=4 << 20, transcendentals=0
+        ),
+        name="slot_marks",
+    )(me, arrived)
+
+
+def gather_kernel(idx_ref, grid_ref, out_ref, table, shifted, rows, eye):
     step = pl.program_id(0)
     steps = pl.num_programs(0)
     cells = grid_ref.shape[1]
     plane = GR * GR
-    width = out_ref.shape[1]
+    width = out_ref.shape[0] * LANES
     blocks = width // BLOCK
-    rows = lax.broadcasted_iota(jnp.int32, (BLOCK, BLOCK), 0)
-    cols = lax.broadcasted_iota(jnp.int32, (BLOCK, BLOCK), 1)
-    eye = (rows == cols).astype(BF16)
-
-    def gather(block, near, far):
-        row = block // blocks
-        start = (block % blocks) * BLOCK
+
+    def unit():
+        return jnp.concatenate([eye[0], eye[1]], axis=1)
+
+    def gather(row, block, pair):
+        start = row * width
         for u in range(BLOCK):
-            k = idx_ref[row, start + u]
-            near[u : u + 1, :] = table[pl.ds(k, 1), :]
-            far[u : u + 1, :] = table[pl.ds(k + 1, 1), :]
+            k = idx_ref.at[pl.ds(block * BLOCK + u, idx_ref.shape[0] - width + 1)][start]
+            pair[2 * u : 2 * u + 2, :] = table[pl.ds(k, 2), :]
 
     @pl.when(step == 0)
     def _():
+        down = lax.broadcasted_iota(jnp.int32, (BLOCK, BLOCK), 0)
+        across = lax.broadcasted_iota(jnp.int32, (BLOCK, BLOCK), 1)
+        same = (down == across).astype(BF16)
+        eye[0] = same[:, :LANES]
+        eye[1] = same[:, LANES:]
         span = 2048
 
         def shift(b, carry):
@@ -67,58 +170,58 @@
         shifted[:, cells - span :] = jnp.concatenate([last[:, GR:], last[:, :GR]], axis=1)
 
         def build(b, carry):
-            c0 = pl.multiple_of(b * BLOCK, BLOCK)
+            c0 = pl.multiple_of(b * 2 * BLOCK, 2 * BLOCK)
             x = jnp.concatenate(
                 [
-                    grid_ref[:, pl.ds(c0, BLOCK)],
-                    shifted[:, pl.ds(c0, BLOCK)],
-                    grid_ref[:, pl.ds(c0 + plane, BLOCK)],
-                    shifted[:, pl.ds(c0 + plane, BLOCK)],
+                    ref[:, pl.ds(c0 + half * BLOCK + across, BLOCK)]
+                    for half in range(2)
+                    for across in (0, plane)
+                    for ref in (grid_ref, shifted)
                 ],
                 axis=0,
             )
-            table[pl.ds(c0, BLOCK), :] = dot_nt(eye, x)
+            table[pl.ds(c0, BLOCK), :] = x[:LANES].T.astype(F32)
+            table[pl.ds(c0 + BLOCK, BLOCK), :] = x[LANES:].T.astype(F32)
             return carry
 
-        lax.fori_loop(0, (cells - plane) // BLOCK, build, 0, unroll=4)
-        gather(0, near_a, far_a)
-
-    def turn(j, near, far):
-        d = jnp.concatenate([near[...].astype(BF16), far[...].astype(BF16)], axis=1)
-        t = dot_nt(eye, d)
-        out_ref[:, pl.ds(pl.multiple_of(j * BLOCK, BLOCK), BLOCK)] = t.astype(BF16)
-
-    final = steps * blocks - 1
-
-    def pair(i, carry):
-        first = step * blocks + 2 * i
-        gather(first + 1, near_b, far_b)
-        turn(2 * i, near_a, far_a)
-        gather(jnp.minimum(first + 2, final), near_a, far_a)
-        turn(2 * i + 1, near_b, far_b)
-        return carry
-
-    lax.fori_loop(0, blocks // 2, pair, 0)
-
-
-def gather_corners(cells, grid):
-    parts, width = cells.shape
+        lax.fori_loop(0, (cells - plane) // (2 * BLOCK), build, 0, unroll=BUILD_UNROLL)
+        gather(0, 0, rows.at[0])
+
+    def turn(j, pair):
+        near = pair[pl.ds(0, BLOCK, stride=2), :].astype(BF16)
+        far = pair[pl.ds(1, BLOCK, stride=2), :].astype(BF16)
+        t = dot_nt(unit(), jnp.concatenate([near, far], axis=1)).astype(BF16)
+        out_ref[2 * j] = t[:, :LANES]
+        out_ref[2 * j + 1] = t[:, LANES:]
+
+    for j in range(blocks):
+        ahead = rows.at[(j + 1) % DEPTH]
+        if j + 1 < blocks:
+            gather(step, j + 1, ahead)
+        else:
+            gather(jnp.minimum(step + 1, steps - 1), 0, ahead)
+        turn(j, rows.at[j % DEPTH])
+
+
+def gather_corners(cells, grid, parts):
+    width = cells.shape[0] // parts
     features, total = grid.shape
     return pl.pallas_call(
         gather_kernel,
         grid=(parts,),
-        out_shape=jax.ShapeDtypeStruct((8 * features, parts * width), BF16),
+        out_shape=jax.ShapeDtypeStruct((parts * width // LANES, 8 * features, LANES), BF16),
         in_specs=[
             pl.BlockSpec(memory_space=pltpu.SMEM),
             pl.BlockSpec((features, total), lambda q: (0, 0), pipeline_mode=pl.Buffered(1)),
         ],
-        out_specs=pl.BlockSpec((8 * features, width), lambda q: (0, q)),
+        out_specs=pl.BlockSpec((width // LANES, 8 * features, LANES), lambda q: (q, 0, 0)),
         scratch_shapes=[
             pltpu.VMEM((total, LANES), F32),
             pltpu.VMEM((features, total), BF16),
         ]
-        + [pltpu.VMEM((BLOCK, LANES), F32)] * 4,
-        compiler_params=pltpu.CompilerParams(vmem_limit_bytes=40 * 1024 * 1024),
+        + [pltpu.VMEM((DEPTH, 2 * BLOCK, LANES), F32)]
+        + [pltpu.VMEM((2, BLOCK, LANES), BF16)],
+        compiler_params=pltpu.CompilerParams(vmem_limit_bytes=60 * 1024 * 1024),
         name="gather_corners",
     )(cells, grid)
 
@@ -170,38 +273,51 @@
 
 
 def forward_kernel(
-    cap, corners_ref, geometry_ref, first_ref, mid_ref, head_ref,
-    saved_ref, dense_ref, summary_ref, weights, fine_logit, prop_logit,
+    cap, corners_ref, arrived_ref, fine_in_ref, prop_in_ref, mid_ref, fine_out_ref, prop_out_ref,
+    saved_ref, dense_ref, summary_ref, weights, spacing, first, head, fine_logit, prop_logit,
 ):
     step = pl.program_id(0)
-    features = corners_ref.shape[0] // 8
+    features = corners_ref.shape[1] // 8
     hidden = mid_ref.shape[1]
-    width = corners_ref.shape[1]
+    prop_hidden = prop_in_ref.shape[0]
+    width = corners_ref.shape[0] * LANES
 
     @pl.when(step == 0)
     def _():
-        g = [geometry_ref[j].astype(F32) for j in range(3)]
+        parts = arrived_ref.shape[0]
+        blocks = [arrived_ref[q].astype(F32) for q in range(parts)]
+        g = [stack_rows(blocks, j) for j in range(4)]
+        spacing[...] = g[3]
+        first[:hidden, :] = fine_in_ref[...].astype(F32).T.astype(BF16)
+        first[hidden:, :] = prop_in_ref[...]
+        zero_f = jnp.zeros((1, prop_hidden), F32)
+        zero_p = jnp.zeros((1, hidden), F32)
+        top = jnp.concatenate([fine_out_ref[...].astype(F32), zero_f], axis=1)
+        low = jnp.concatenate([zero_p, prop_out_ref[...].astype(F32)], axis=1)
+        rest = jnp.zeros((6, hidden + prop_hidden), F32)
+        head[...] = jnp.concatenate([top, low, rest], axis=0).astype(BF16)
         for corner in range(8):
             bits = (corner // 4, corner // 2 % 2, corner % 2)
             w = [x if bit else 1.0 - x for x, bit in zip(g, bits)]
             weights[corner] = w[0] * w[1] * w[2]
 
     feats = []
-    for v in range(width // BLOCK):
-        at = v * BLOCK
-        total = jnp.zeros((features, BLOCK), F32)
+    row = [weights[corner, pl.ds(step, 1), :] for corner in range(8)]
+    for v in range(width // LANES):
+        at = v * LANES
+        total = jnp.zeros((features, LANES), F32)
         for corner in range(8):
             place = (corner % 2) * 4 + corner // 2
-            x = corners_ref[place * features : (place + 1) * features, at : at + BLOCK].astype(F32)
-            total = total + x * weights[corner, pl.ds(step, 1), at : at + BLOCK]
+            x = corners_ref[v, place * features : (place + 1) * features, :].astype(F32)
+            total = total + x * row[corner][:, at : at + LANES]
         feats.append(total.astype(BF16))
     feat = jnp.concatenate(feats, axis=1)
-    both = jnp.maximum(dot(first_ref[...], feat), 0.0).astype(BF16)
+    both = jnp.maximum(dot(first[...], feat), 0.0).astype(BF16)
     h = both[:hidden]
     ph = both[hidden:]
     for layer in range(mid_ref.shape[0]):
         h = jnp.maximum(dot(mid_ref[layer], h), 0.0).astype(BF16)
-    logits = dot(head_ref[...], jnp.concatenate([h, ph], axis=0))
+    logits = dot(head[...], jnp.concatenate([h, ph], axis=0))
     fine_logit[pl.ds(step, 1), :] = logits[0:1]
     prop_logit[pl.ds(step, 1), :] = logits[1:2]
     saved_ref[:features, :] = feat
@@ -209,7 +325,7 @@
 
     @pl.when(step == pl.num_programs(0) - 1)
     def _():
-        space = pieces_of(geometry_ref[3].astype(F32))
+        space = pieces_of(spacing[...])
         results = []
         for k, ref in enumerate((prop_logit, fine_logit)):
             logit = pieces_of(ref[...])
@@ -238,14 +354,17 @@
         summary_ref[...] = jnp.concatenate(slabs, axis=1)
 
 
-def forward(corners, geometry, first, mid, head, cap):
-    rows, total = corners.shape
-    parts, width = geometry.shape[1:]
+def forward(corners, arrived, fine_in, prop_in, mid, fine_out, prop_out, cap):
+    rows = corners.shape[1]
+    total = corners.shape[0] * LANES
+    parts, _, width = arrived.shape
     features = rows // 8
-    prop_hidden = first.shape[0] - mid.shape[1]
+    hidden = mid.shape[1]
+    prop_hidden = prop_in.shape[0]
     kept = features + prop_hidden
     stat_lanes = -(-5 // (LANES // cap)) * LANES
     whole = lambda shape: pl.BlockSpec(shape, lambda q: (0,) * len(shape))
+    small = (arrived, fine_in, prop_in, mid, fine_out, prop_out)
     return pl.pallas_call(
         functools.partial(forward_kernel, cap),
         grid=(parts,),
@@ -254,13 +373,8 @@
             jax.ShapeDtypeStruct((4, parts, width), F32),
             jax.ShapeDtypeStruct((parts, stat_lanes), F32),
         ),
-        in_specs=[
-            pl.BlockSpec((rows, width), lambda q: (0, q)),
-            whole(geometry.shape),
-            whole(first.shape),
-            whole(mid.shape),
-            whole(head.shape),
-        ],
+        in_specs=[pl.BlockSpec((width // LANES, rows, LANES), lambda q: (q, 0, 0))]
+        + [whole(x.shape) for x in small],
         out_specs=(
             pl.BlockSpec((kept, width), lambda q: (0, q)),
             whole((4, parts, width)),
@@ -269,42 +383,40 @@
         scratch_shapes=[
             pltpu.VMEM((8, parts, width), F32),
             pltpu.VMEM((parts, width), F32),
+            pltpu.VMEM((hidden + prop_hidden, features), BF16),
+            pltpu.VMEM((8, hidden + prop_hidden), BF16),
+            pltpu.VMEM((parts, width), F32),
             pltpu.VMEM((parts, width), F32),
         ],
-        compiler_params=pltpu.CompilerParams(vmem_limit_bytes=32 * 1024 * 1024),
+        compiler_params=pltpu.CompilerParams(vmem_limit_bytes=60 * 1024 * 1024),
         name="forward",
-    )(corners, geometry, first, mid, head)
+    )(corners, *small)
 
 
 def backward_kernel(
-    cap, me_ref, stats_ref, key_ref, dense_ref, saved_ref, out_col_ref,
-    loss_ref, grad_ref, keys_t, slope_ref, *masks,
+    cap, me_ref, stats_ref, key_ref, hot_ref, dense_ref, saved_ref, prop_out_ref, *rest,
 ):
+    masks, (loss_ref, grad_ref, slope_ref, *keys_t) = rest[:-3], rest[-3:]
+    if stats_ref.shape[0] * cap > 256:
+        masks, (loss_ref, grad_ref, slope_ref, *keys_t) = (), rest
     me = me_ref[0]
     parts = stats_ref.shape[0]
     slots = key_ref.shape[1]
     per = LANES // cap
     width = dense_ref.shape[2]
-    prop_hidden = out_col_ref.shape[0]
+    prop_hidden = prop_out_ref.shape[1]
     key = key_ref[...]
     live = (key >= 0).astype(F32)
     sub = lax.broadcasted_iota(jnp.int32, (parts, slots), 0)
-    keys_t[...] = key.T
+    if not masks:
+        keys_t[0][...] = key.T
 
     def mask_of(q):
-        if isinstance(q, int):
-            col = keys_t[:, q : q + 1]
-            row = key[q : q + 1]
-        else:
-            lane = lax.broadcasted_iota(jnp.int32, (slots, parts), 1)
-            col = jnp.sum(jnp.where(lane == q, keys_t[...], 0.0), axis=1, keepdims=True)
-            row = jnp.sum(jnp.where(sub == q, key, 0.0), axis=0, keepdims=True)
+        lane = lax.broadcasted_iota(jnp.int32, (slots, parts), 1)
+        col = jnp.sum(jnp.where(lane == q, keys_t[0][...], 0.0), axis=1, keepdims=True)
+        row = jnp.sum(jnp.where(sub == q, key, 0.0), axis=0, keepdims=True)
         gap = row - col
         return ((gap > 0) & (gap < parts)).astype(BF16)
-
-    if masks:
-        for q in range(parts):
-            masks[0][q] = mask_of(q)
 
     def over(body, init):
         if masks:
@@ -372,12 +484,7 @@
     coef_aa = own_lanes(0.5 * distill_weight * entry_prop * entry_prop)
     coef_ab = own_lanes(-distill_weight * entry_prop * entry_fine)
 
-    lane_me = lax.broadcasted_iota(jnp.int32, (slots, parts), 1)
-    key_col = jnp.sum(jnp.where(lane_me == me, keys_t[...], 0.0), axis=1, keepdims=True)
-    ray = lax.broadcasted_iota(jnp.int32, (slots, RAY_DEV), 1).astype(F32)
-    rest = key_col - ray * (2.0 * parts)
-    hot = ((rest >= 0) & (rest < 2 * parts)).astype(BF16)
-    spread = dot(jnp.concatenate(split3(seg_loss), axis=0), hot)
+    spread = dot(jnp.concatenate(split3(seg_loss), axis=0), hot_ref[...])
     spread = spread[:parts] + spread[parts : 2 * parts] + spread[2 * parts :]
     sub_ray = lax.broadcasted_iota(jnp.int32, (parts, RAY_DEV), 0)
     loss_ref[...] = (0.5 * distill_weight) * jnp.sum(
@@ -395,7 +502,11 @@
     ]
     slope_ref[...] = jnp.concatenate(logit_grad, axis=1)
     features = saved_ref.shape[0] - prop_hidden
-    out_col = out_col_ref[...].astype(F32)
+    wide = jnp.broadcast_to(prop_out_ref[...].astype(F32), (prop_hidden, prop_hidden))
+    same = lax.broadcasted_iota(jnp.int32, wide.shape, 0) == lax.broadcasted_iota(
+        jnp.int32, wide.shape, 1
+    )
+    out_col = jnp.sum(jnp.where(same, wide, 0.0), axis=1, keepdims=True)
     first_row = lax.broadcasted_iota(jnp.int32, (prop_hidden, width), 0) == 0
 
     def accumulate(q, total):
@@ -411,24 +522,25 @@
     grad_ref[...] = total
 
 
-def backward(me, stats, key, dense, saved, out_col, cap):
+def backward(me, stats, dense, saved, prop_out, marks, cap):
+    key, hot, *masks = marks
     parts, slots = key.shape
     width = dense.shape[2]
-    prop_hidden = out_col.shape[0]
+    prop_hidden = prop_out.shape[1]
     vmem = pl.BlockSpec(memory_space=pltpu.VMEM)
-    keep = [pltpu.VMEM((parts, slots, slots), BF16)] if slots <= 256 else []
     return pl.pallas_call(
         functools.partial(backward_kernel, cap),
         out_shape=(
             jax.ShapeDtypeStruct((1, RAY_DEV), F32),
             jax.ShapeDtypeStruct((2 * prop_hidden, saved.shape[0]), F32),
         ),
-        in_specs=[pl.BlockSpec(memory_space=pltpu.SMEM)] + [vmem] * 5,
+        in_specs=[pl.BlockSpec(memory_space=pltpu.SMEM)] + [vmem] * (6 + len(masks)),
         out_specs=(vmem, vmem),
-        scratch_shapes=[pltpu.VMEM((slots, parts), F32), pltpu.VMEM((parts, width), F32)] + keep,
+        scratch_shapes=[pltpu.VMEM((parts, width), F32)]
+        + ([] if masks else [pltpu.VMEM((slots, parts), F32)]),
         compiler_params=pltpu.CompilerParams(vmem_limit_bytes=48 * 1024 * 1024),
         name="backward",
-    )(me, stats, key, dense, saved, out_col)
+    )(me, stats, key, hot, dense, saved, prop_out, *masks)
 
 
 def sum_replicas(x):
@@ -454,43 +566,23 @@
 ):
     parts = lax.axis_size("dom")
     cap = slot_ray.shape[3]
-    width = sample_cells.shape[3]
     features = feature_grid.shape[1]
     prop_hidden = prop_in.shape[1]
-    slots = parts * cap
-
-    live = jnp.arange(cap)[None, :] < bucket_count[0, 0][:, None]
-    ray = jnp.where(live, slot_ray[0, 0], -1).reshape(-1)
-    marks = jnp.concatenate([ray, slot_rank[0, 0].reshape(-1)]).astype(BF16)
-    extra = -(-2 * slots // width)
-    marks = jnp.pad(marks, (0, extra * width - 2 * slots)).reshape(extra, 1, width)
-    outgoing = jnp.concatenate(
-        [sample_geometry[:, 0, 0], jnp.broadcast_to(marks, (extra, parts, width))], axis=0
-    )
-    arrived = lax.all_to_all(outgoing, "dom", split_axis=1, concat_axis=1, tiled=True)
-
-    corners = gather_corners(sample_cells[0, 0], feature_grid[0])
-
-    geometry = arrived[:4]
-    marks = jnp.moveaxis(arrived[4:], 0, 1).reshape(parts, extra * width)[:, : 2 * slots].astype(F32)
-    key = marks[:, :slots] * (2.0 * parts) + marks[:, slots:]
-    first = jnp.concatenate([fine_in[0], prop_in[0]], axis=0)
-    head = jnp.concatenate(
-        [
-            jnp.pad(fine_out, ((0, 0), (0, prop_hidden))),
-            jnp.pad(prop_out, ((0, 0), (fine_out.shape[1], 0))),
-        ],
-        axis=0,
-    )
-    head = jnp.pad(head, ((0, 6), (0, 0)))
-    saved, dense, summary = forward(corners, geometry, first, fine_mid[0], head, cap)
-
+    outgoing = pack(
+        sample_geometry[:, 0, 0], slot_ray[0, 0], slot_rank[0, 0], bucket_count.reshape(-1, 1)
+    )
+    arrived = lax.all_to_all(outgoing, "dom", split_axis=0, concat_axis=0, tiled=True)
+    corners = gather_corners(sample_cells.reshape(-1), feature_grid[0], parts)
+    saved, dense, summary = forward(
+        corners, arrived, fine_in[0].T, prop_in[0], fine_mid[0], fine_out, prop_out, cap
+    )
     stats = lax.all_to_all(
         jnp.broadcast_to(summary[None], (parts,) + summary.shape),
         "dom", split_axis=0, concat_axis=0, tiled=True,
     )
     me = lax.axis_index("dom").reshape(1).astype(jnp.int32)
-    ray_loss, grads = backward(me, stats, key, dense, saved, prop_out.reshape(-1, 1), cap)
+    marks = slot_marks(me, arrived, cap)
+    ray_loss, grads = backward(me, stats, dense, saved, prop_out, marks, cap)
     sums = sum_replicas(grads)
     in_sum = sums[:prop_hidden, :features]
     out_sum = sums[prop_hidden, features:]

time: 113 us -> 72.1 us (0.64)
  Pallas kernels: 70.9 us -> 39.4 us
  other arithmetic: 3.85 us -> 0.01 us
  local copies, waits for them, and re-layouts: 14.7 us -> 11.2 us
  waiting for transfers between devices: 8.86 us -> 6.39 us
    pallas_call x1, Pallas kernels: 59.4 us -> 20.9 us  [gather_corners(): pl.pallas_call(gather_kernel, grid=(parts,), out_shape=jax.ShapeDtypeStru...]
    pallas_call x0 -> x2, Pallas kernels: none -> 4.44 us  [the longest x1 2.58 us: slot_marks(): pl.pallas_call(functools.partial(marks_kernel, cap), out_shape=tuple(shap...]
    unnamed x14 -> x15, local copies, waits for them, and re-layouts: 10.9 us -> 7.41 us
    pallas_call x1, Pallas kernels: 7.61 us -> 11 us  [forward(): pl.pallas_call(functools.partial(forward_kernel, cap), grid=(parts,), out...]
    all_to_all x1, waiting for transfers between devices: 5.01 us -> 2.44 us  [on_device(): lax.all_to_all(jnp.broadcast_to(summary[None], (parts,) + summary.shape),...]
    concatenate x4 -> x0, other arithmetic: 2.4 us -> none  [the longest x1 0.86 us: on_device(): jnp.concatenate([sample_geometry[:, 0, 0], jnp.broadcast_to(marks, (extra...]
  transfers between devices with their start and end apart: 5 -> 5, of which waited for: 3 -> 3; matrix products, arithmetic and copies ran while one was open for 3% -> 2% of each run, Pallas kernels for 53% -> 33%
where the time goes in v2:
time: 72.1 us; the launch traced here: 71.3 us
  Pallas kernels  39.4 us (55%)
  starting transfers between devices  13.6 us (19%)
  local copies, waits for them, and re-layouts  11.2 us (16%)
  waiting for transfers between devices  6.39 us (9%)
    pallas_call x1, Pallas kernels, gather_corners(): pl.pallas_call(gather_kernel, grid=(parts,), out_shape=jax.ShapeDtypeStru...  20.9 us
    pallas_call x1, Pallas kernels, forward(): pl.pallas_call(functools.partial(forward_kernel, cap), grid=(parts,), out...  11 us
    unnamed x15, local copies, waits for them, and re-layouts  7.41 us
    all_to_all x1, starting transfers between devices, on_device(): lax.all_to_all(outgoing, 'dom', split_axis=0, concat_axis=0, tiled=True)  5.2 us
    ppermute x3, starting transfers between devices, sum_replicas(): lax.ppermute(x, 'rep', [(i, i ^ s) for i in range(count)])  4.19 us
    all_to_all x1, starting transfers between devices, on_device(): lax.all_to_all(jnp.broadcast_to(summary[None], (parts,) + summary.shape),...  4.18 us
    ppermute x3, waiting for transfers between devices, sum_replicas(): lax.ppermute(x, 'rep', [(i, i ^ s) for i in range(count)])  3.94 us
    pallas_call x1, Pallas kernels, backward(): pl.pallas_call(functools.partial(backward_kernel, cap), out_shape=(jax.Sh...  3.1 us
  transfers between devices with their start and end apart: 5, of which 3 were waited for; matrix products, arithmetic and copies ran while one was open for 2% of the time, Pallas kernels for 33%

profile of v2, /device:TPU:0, one launch (start us, length us, event | category | flops | bytes accessed | tf_op | source)
XLA Modules:
  0.0 71.3 jit_solution(1134370419322200940)
XLA Ops:
  0.6 1.3 %copy.14.count_ref = s32[8,1]{1,0:T(8,128)} copy(s32[8,1]{0,1:T(1,128)} %bitcast.25) | data formatting | bytes 64 | tf_op jit(solution)/shard_map/reshape | solution.py:572
  2.0 1.9 %pack.1 = bf16[8,5,2048]{2,1,0:T(8,128)(2,1)} custom-call(bf16[4,8,2048]{2,1,0:T(8,128)(2,1)} %bitcast.18, s32[8,32]{1,0:T(8,128)} %bitcast.23, s32[8,32]{1,0:T(8,128)} %bitcast.24, s32[8,1]{1,0:T(8,128)} %copy.14.count_ref), custom_call_target="tpu_custom_call" | custom-call | tf_op jit(solution)/shard_map/pack/pallas_call | solution.py:79
  3.8 5.2 %all-to-all-start = ((bf16[8,5,2048]{2,1,0:T(8,128)(2,1)}), bf16[8,5,2048]{2,1,0:T(8,128)(2,1)S(1)}, u32[]{:S(2)}, u32[]{:S(2)}) async-start(bf16[8,5,2048]{2,1,0:T(8,128)(2,1)} %pack.1), calls=%async_computation | async-start | bytes 524288 | tf_op jit(solution)/shard_map/all_to_all | solution.py:574
  9.0 1.5 %copy.15 = s32[1,16,8,128]{3,1,2,0:T(8,128)} copy(s32[1,16,8,128]{3,2,1,0:T(8,128)} %bitcast.19) | data formatting | bytes 131072
  10.5 20.9 %gather_corners.1.corners_ref = bf16[128,256,128]{2,1,0:T(8,128)(2,1)} custom-call(s32[16384]{0:T(1024)} %bitcast.17, bf16[32,32768]{1,0:T(8,128)(2,1)} %bitcast.16), custom_call_target="tpu_custom_call" | custom-call | tf_op jit(solution)/shard_map/gather_corners/pallas_call | solution.py:209
  31.4 0.7 %copy-done.6 = bf16[8,5,2048]{2,1,0:T(8,128)(2,1)} copy-done((bf16[8,5,2048]{2,1,0:T(8,128)(2,1)}, bf16[8,5,2048]{2,1,0:T(8,128)(2,1)S(1)}, u32[]{:S(2)}) %copy-start.6) | copy-done | bytes 163864
  32.2 11.0 %forward.1 = (bf16[48,16384]{1,0:T(8,128)(2,1)}, f32[4,8,2048]{2,1,0:T(8,128)}, f32[8,256]{1,0:T(8,128)}) custom-call(bf16[128,256,128]{2,1,0:T(8,128)(2,1)} %gather_corners.1.corners_ref, bf16[8,5,2048]{2,1,0:T(8,128)(2,1)} %copy-done.6, bf16[32,64]{1,0:T(8,128)(2,1)} %bitcast.21, bf16[16,32]{1,0:T(8,128)(2,1)} %bitcast.22, bf16[2,64,64]{2,1,0:T(8,128)(2,1)} %bitcast.20, ...), custom_call_target="tpu_custom_call" | custom-call | tf_op jit(solution)/shard_map/forward/pallas_call | solution.py:368
  43.1 1.3 %broadcast_in_dim.4 = f32[8,8,256]{2,1,0:T(8,128)} broadcast(f32[8,256]{1,0:T(8,128)} %get-tuple-element.11), dimensions={1,2} | broadcast | bytes 73728 | tf_op jit(solution)/shard_map/broadcast_in_dim | solution.py:580
  44.5 4.2 %all-to-all-start.1 = ((f32[8,8,256]{2,1,0:T(8,128)}), f32[8,8,256]{2,1,0:T(8,128)S(1)}, u32[]{:S(2)}, u32[]{:S(2)}) async-start(f32[8,8,256]{2,1,0:T(8,128)} %broadcast_in_dim.4), calls=%async_computation.1 | async-start | bytes 131072 | tf_op jit(solution)/shard_map/all_to_all | solution.py:579
  48.6 2.6 %slot_marks.1 = (f32[8,256]{1,0:T(8,128)}, bf16[256,256]{1,0:T(8,128)(2,1)}, bf16[8,256,256]{2,1,0:T(8,128)(2,1)}) custom-call(s32[1]{0:T(128)} %bitcast.me_ref, bf16[8,5,2048]{2,1,0:T(8,128)(2,1)} %copy-done.6), custom_call_target="tpu_custom_call" | custom-call | flops 4194304 | bytes 4194304 | tf_op jit(solution)/shard_map/slot_marks/pallas_call | solution.py:124
  51.2 2.4 %all-to-all-done.1.stats_ref = f32[8,8,256]{2,1,0:T(8,128)S(1)} async-done(((f32[8,8,256]{2,1,0:T(8,128)}), f32[8,8,256]{2,1,0:T(8,128)S(1)}, u32[]{:S(2)}, u32[]{:S(2)}) %all-to-all-start.1) | async-done | bytes 65568 | tf_op jit(solution)/shard_map/all_to_all | solution.py:579
  53.7 1.4 %copy-done = bf16[48,16384]{1,0:T(8,128)(2,1)S(1)} copy-done((bf16[48,16384]{1,0:T(8,128)(2,1)S(1)}, bf16[48,16384]{1,0:T(8,128)(2,1)}, u32[]{:S(2)}) %copy-start) | copy-done | bytes 1572888
  55.1 1.2 %copy-done.1 = bf16[8,256,256]{2,1,0:T(8,128)(2,1)S(1)} copy-done((bf16[8,256,256]{2,1,0:T(8,128)(2,1)S(1)}, bf16[8,256,256]{2,1,0:T(8,128)(2,1)}, u32[]{:S(2)}) %copy-start.1) | copy-done | bytes 1048600
  56.3 0.9 %copy-done.2 = f32[4,8,2048]{2,1,0:T(8,128)S(1)} copy-done((f32[4,8,2048]{2,1,0:T(8,128)S(1)}, f32[4,8,2048]{2,1,0:T(8,128)}, u32[]{:S(2)}) %copy-start.2) | copy-done | bytes 262168
  57.2 0.9 %copy-done.3 = bf16[256,256]{1,0:T(8,128)(2,1)S(1)} copy-done((bf16[256,256]{1,0:T(8,128)(2,1)S(1)}, bf16[256,256]{1,0:T(8,128)(2,1)}, u32[]{:S(2)}) %copy-start.3) | copy-done | bytes 131096
  58.1 0.7 copy-done.4
  58.8 3.1 %backward.1 = (f32[1,256]{1,0:T(1,128)}, f32[32,48]{1,0:T(8,128)S(1)}) custom-call(s32[1]{0:T(128)} %bitcast.me_ref, f32[8,8,256]{2,1,0:T(8,128)S(1)} %all-to-all-done.1.stats_ref, f32[8,256]{1,0:T(8,128)S(1)} %copy-done.4, bf16[256,256]{1,0:T(8,128)(2,1)S(1)} %copy-done.3, f32[4,8,2048]{2,1,0:T(8,128)S(1)} %copy-done.2, bf16[48,16384]{1,0:T(8,128)(2,1)S(1)} %copy-done, ...), custom_call_target="tpu_custom_call" | custom-call | tf_op jit(solution)/shard_map/backward/pallas_call | solution.py:531
  61.9 2.6 %collective-permute-start.1 = (f32[32,48]{1,0:T(8,128)S(1)}, f32[32,48]{1,0:T(8,128)S(1)}, u32[]{:S(2)}, u32[]{:S(2)}) collective-permute-start(f32[32,48]{1,0:T(8,128)S(1)} %get-tuple-element.18), channel_id=1, source_target_pairs={{0,2},{1,3},{2,0},{3,1},{4,6},{5,7},{6,4},{7,5},{8,10},{9,11},{10,... | collective-permute-start | bytes 18440 | tf_op jit(solution)/shard_map/ppermute | solution.py:550
  64.5 1.3 %collective-permute-start.2 = (f32[32,48]{1,0:T(8,128)S(1)}, f32[32,48]{1,0:T(8,128)S(1)}, u32[]{:S(2)}, u32[]{:S(2)}) collective-permute-start(f32[32,48]{1,0:T(8,128)S(1)} %get-tuple-element.18), channel_id=1, source_target_pairs={{0,3},{1,2},{2,1},{3,0},{4,7},{5,6},{6,5},{7,4},{8,11},{9,10},{10,... | collective-permute-start | bytes 18440 | tf_op jit(solution)/shard_map/ppermute | solution.py:550
  65.9 0.3 collective-permute-start
  66.1 0.4 collective-permute-done.1
  66.6 3.5 %collective-permute-done.2 = f32[32,48]{1,0:T(8,128)S(1)} collective-permute-done((f32[32,48]{1,0:T(8,128)S(1)}, f32[32,48]{1,0:T(8,128)S(1)}, u32[]{:S(2)}, u32[]{:S(2)}) %collective-permute-start.2) | collective-permute-done | bytes 6176 | tf_op jit(solution)/shard_map/ppermute | solution.py:550
  70.1 0.6 slice_bitcast_fusion
  70.7 0.6 slice.9
  (11 shorter events, 0.0 us)
Async XLA Ops:
  3.8 27.6 %all-to-all-start = ((bf16[8,5,2048]{2,1,0:T(8,128)(2,1)}), bf16[8,5,2048]{2,1,0:T(8,128)(2,1)S(1)}, u32[]{:S(2)}, u32[]{:S(2)}) async-start(bf16[8,5,2048]{2,1,0:T(8,128)(2,1)} %pack.1), calls=%async_computation | async-start | bytes 524288 | tf_op jit(solution)/shard_map/all_to_all | solution.py:574
  31.4 0.7 %copy-start.6 = (bf16[8,5,2048]{2,1,0:T(8,128)(2,1)}, bf16[8,5,2048]{2,1,0:T(8,128)(2,1)S(1)}, u32[]{:S(2)}) copy-start(bf16[8,5,2048]{2,1,0:T(8,128)(2,1)S(1)} %all-to-all-done.arrived_ref) | copy-start | bytes 491524
  32.2 21.5 %copy-start.5 = (bf16[1,16]{1,0:T(2,128)(2,1)S(1)}, bf16[1,16]{1,0:T(2,128)(2,1)}, u32[]{:S(2)}) copy-start(bf16[1,16]{1,0:T(2,128)(2,1)} %prop_out_ref.3) | copy-start | bytes 100
  44.5 9.2 %all-to-all-start.1 = ((f32[8,8,256]{2,1,0:T(8,128)}), f32[8,8,256]{2,1,0:T(8,128)S(1)}, u32[]{:S(2)}, u32[]{:S(2)}) async-start(f32[8,8,256]{2,1,0:T(8,128)} %broadcast_in_dim.4), calls=%async_computation.1 | async-start | bytes 131072 | tf_op jit(solution)/shard_map/all_to_all | solution.py:579
  53.7 1.4 %copy-start = (bf16[48,16384]{1,0:T(8,128)(2,1)S(1)}, bf16[48,16384]{1,0:T(8,128)(2,1)}, u32[]{:S(2)}) copy-start(bf16[48,16384]{1,0:T(8,128)(2,1)} %get-tuple-element.15.saved_ref) | copy-start | bytes 4718596
  55.1 1.2 %copy-start.1 = (bf16[8,256,256]{2,1,0:T(8,128)(2,1)S(1)}, bf16[8,256,256]{2,1,0:T(8,128)(2,1)}, u32[]{:S(2)}) copy-start(bf16[8,256,256]{2,1,0:T(8,128)(2,1)} %get-tuple-element.16.rest_0_) | copy-start | bytes 3145732
  56.3 0.9 %copy-start.2 = (f32[4,8,2048]{2,1,0:T(8,128)S(1)}, f32[4,8,2048]{2,1,0:T(8,128)}, u32[]{:S(2)}) copy-start(f32[4,8,2048]{2,1,0:T(8,128)} %get-tuple-element.14.dense_ref) | copy-start | bytes 786436
  57.2 0.9 %copy-start.3 = (bf16[256,256]{1,0:T(8,128)(2,1)S(1)}, bf16[256,256]{1,0:T(8,128)(2,1)}, u32[]{:S(2)}) copy-start(bf16[256,256]{1,0:T(8,128)(2,1)} %get-tuple-element.13.hot_ref) | copy-start | bytes 393220
  58.1 0.7 copy-start.4
  61.9 4.6 %collective-permute-start.1 = (f32[32,48]{1,0:T(8,128)S(1)}, f32[32,48]{1,0:T(8,128)S(1)}, u32[]{:S(2)}, u32[]{:S(2)}) collective-permute-start(f32[32,48]{1,0:T(8,128)S(1)} %get-tuple-element.18), channel_id=1, source_target_pairs={{0,2},{1,3},{2,0},{3,1},{4,6},{5,7},{6,4},{7,5},{8,10},{9,11},{10,... | collective-permute-start | bytes 18440 | tf_op jit(solution)/shard_map/ppermute | solution.py:550
  64.5 5.5 %collective-permute-start.2 = (f32[32,48]{1,0:T(8,128)S(1)}, f32[32,48]{1,0:T(8,128)S(1)}, u32[]{:S(2)}, u32[]{:S(2)}) collective-permute-start(f32[32,48]{1,0:T(8,128)S(1)} %get-tuple-element.18), channel_id=1, source_target_pairs={{0,3},{1,2},{2,1},{3,0},{4,7},{5,6},{6,5},{7,4},{8,11},{9,10},{10,... | collective-permute-start | bytes 18440 | tf_op jit(solution)/shard_map/ppermute | solution.py:550
  65.9 4.2 %collective-permute-start = (f32[32,48]{1,0:T(8,128)S(1)}, f32[32,48]{1,0:T(8,128)S(1)}, u32[]{:S(2)}, u32[]{:S(2)}) collective-permute-start(f32[32,48]{1,0:T(8,128)S(1)} %get-tuple-element.18), channel_id=1, source_target_pairs={{0,1},{1,0},{2,3},{3,2},{4,5},{5,4},{6,7},{7,6},{8,9},{9,8},{10,11... | collective-permute-start | bytes 18440 | tf_op jit(solution)/shard_map/ppermute | solution.py:550

commit v3 on v2

--- a/solution.py
+++ b/solution.py
@@ -57,7 +57,11 @@
     parts, cap = ray_ref.shape
     width = geometry_ref.shape[2]
     extra = out_ref.shape[1] - 4
-    live = lax.broadcasted_iota(jnp.int32, (parts, cap), 1) < count_ref[...]
+    sub = lax.broadcasted_iota(jnp.int32, (parts, cap), 0)
+    count = jnp.zeros((parts, cap), jnp.int32)
+    for p in range(parts):
+        count = jnp.where(sub == p, count_ref[p], count)
+    live = lax.broadcasted_iota(jnp.int32, (parts, cap), 1) < count
     ray = jnp.where(live, ray_ref[...], -1).astype(F32)
     marks = jnp.concatenate(
         [flatten_slots(ray, cap), flatten_slots(rank_ref[...].astype(F32), cap)], axis=1
@@ -79,7 +83,7 @@
     return pl.pallas_call(
         pack_kernel,
         out_shape=jax.ShapeDtypeStruct((parts, 4 + extra, width), BF16),
-        in_specs=[vmem] * 4,
+        in_specs=[vmem] * 3 + [pl.BlockSpec(memory_space=pltpu.SMEM)],
         out_specs=vmem,
         name="pack",
     )(geometry, ray, rank, count)
@@ -133,99 +137,6 @@
     )(me, arrived)
 
 
-def gather_kernel(idx_ref, grid_ref, out_ref, table, shifted, rows, eye):
-    step = pl.program_id(0)
-    steps = pl.num_programs(0)
-    cells = grid_ref.shape[1]
-    plane = GR * GR
-    width = out_ref.shape[0] * LANES
-    blocks = width // BLOCK
-
-    def unit():
-        return jnp.concatenate([eye[0], eye[1]], axis=1)
-
-    def gather(row, block, pair):
-        start = row * width
-        for u in range(BLOCK):
-            k = idx_ref.at[pl.ds(block * BLOCK + u, idx_ref.shape[0] - width + 1)][start]
-            pair[2 * u : 2 * u + 2, :] = table[pl.ds(k, 2), :]
-
-    @pl.when(step == 0)
-    def _():
-        down = lax.broadcasted_iota(jnp.int32, (BLOCK, BLOCK), 0)
-        across = lax.broadcasted_iota(jnp.int32, (BLOCK, BLOCK), 1)
-        same = (down == across).astype(BF16)
-        eye[0] = same[:, :LANES]
-        eye[1] = same[:, LANES:]
-        span = 2048
-
-        def shift(b, carry):
-            c0 = pl.multiple_of(b * span, span)
-            x = grid_ref[:, pl.ds(c0, span + LANES)]
-            shifted[:, pl.ds(c0, span)] = x[:, GR : GR + span]
-            return carry
-
-        lax.fori_loop(0, cells // span - 1, shift, 0)
-        last = grid_ref[:, cells - span :]
-        shifted[:, cells - span :] = jnp.concatenate([last[:, GR:], last[:, :GR]], axis=1)
-
-        def build(b, carry):
-            c0 = pl.multiple_of(b * 2 * BLOCK, 2 * BLOCK)
-            x = jnp.concatenate(
-                [
-                    ref[:, pl.ds(c0 + half * BLOCK + across, BLOCK)]
-                    for half in range(2)
-                    for across in (0, plane)
-                    for ref in (grid_ref, shifted)
-                ],
-                axis=0,
-            )
-            table[pl.ds(c0, BLOCK), :] = x[:LANES].T.astype(F32)
-            table[pl.ds(c0 + BLOCK, BLOCK), :] = x[LANES:].T.astype(F32)
-            return carry
-
-        lax.fori_loop(0, (cells - plane) // (2 * BLOCK), build, 0, unroll=BUILD_UNROLL)
-        gather(0, 0, rows.at[0])
-
-    def turn(j, pair):
-        near = pair[pl.ds(0, BLOCK, stride=2), :].astype(BF16)
-        far = pair[pl.ds(1, BLOCK, stride=2), :].astype(BF16)
-        t = dot_nt(unit(), jnp.concatenate([near, far], axis=1)).astype(BF16)
-        out_ref[2 * j] = t[:, :LANES]
-        out_ref[2 * j + 1] = t[:, LANES:]
-
-    for j in range(blocks):
-        ahead = rows.at[(j + 1) % DEPTH]
-        if j + 1 < blocks:
-            gather(step, j + 1, ahead)
-        else:
-            gather(jnp.minimum(step + 1, steps - 1), 0, ahead)
-        turn(j, rows.at[j % DEPTH])
-
-
-def gather_corners(cells, grid, parts):
-    width = cells.shape[0] // parts
-    features, total = grid.shape
-    return pl.pallas_call(
-        gather_kernel,
-        grid=(parts,),
-        out_shape=jax.ShapeDtypeStruct((parts * width // LANES, 8 * features, LANES), BF16),
-        in_specs=[
-            pl.BlockSpec(memory_space=pltpu.SMEM),
-            pl.BlockSpec((features, total), lambda q: (0, 0), pipeline_mode=pl.Buffered(1)),
-        ],
-        out_specs=pl.BlockSpec((width // LANES, 8 * features, LANES), lambda q: (q, 0, 0)),
-        scratch_shapes=[
-            pltpu.VMEM((total, LANES), F32),
-            pltpu.VMEM((features, total), BF16),
-        ]
-        + [pltpu.VMEM((DEPTH, 2 * BLOCK, LANES), F32)]
-        + [pltpu.VMEM((2, BLOCK, LANES), BF16)],
-        compiler_params=pltpu.CompilerParams(vmem_limit_bytes=60 * 1024 * 1024),
-        name="gather_corners",
-    )(cells, grid)
-
-
 def lane_fold(x, cap):
     shift = LANES // 2
     while shift >= cap:
@@ -272,21 +183,91 @@
     return [x[:, v * LANES : (v + 1) * LANES] for v in range(x.shape[1] // LANES)]
 
 
+def build_table(grid_ref, table, shifted):
+    cells = grid_ref.shape[1]
+    plane = GR * GR
+    span = 2048
+
+    def shift(b, carry):
+        c0 = pl.multiple_of(b * span, span)
+        x = grid_ref[:, pl.ds(c0, span + LANES)]
+        shifted[:, pl.ds(c0, span)] = x[:, GR : GR + span]
+        return carry
+
+    lax.fori_loop(0, cells // span - 1, shift, 0)
+    last = grid_ref[:, cells - span :]
+    shifted[:, cells - span :] = jnp.concatenate([last[:, GR:], last[:, :GR]], axis=1)
+
+    def build(b, carry):
+        c0 = pl.multiple_of(b * 2 * BLOCK, 2 * BLOCK)
+        for half in range(2):
+            x = [
+                ref[:, pl.ds(c0 + half * BLOCK + across, BLOCK)]
+                for across in (0, plane)
+                for ref in (grid_ref, shifted)
+            ]
+            rows = jnp.concatenate(x, axis=0).T.astype(F32)
+            table[pl.ds(c0 + half * BLOCK, BLOCK), :] = rows
+        return carry
+
+    lax.fori_loop(0, (cells - plane) // (2 * BLOCK), build, 0, unroll=BUILD_UNROLL)
+
+
 def forward_kernel(
-    cap, corners_ref, arrived_ref, fine_in_ref, prop_in_ref, mid_ref, fine_out_ref, prop_out_ref,
-    saved_ref, dense_ref, summary_ref, weights, spacing, first, head, fine_logit, prop_logit,
+    cap, idx_ref, grid_ref, arrived_ref, fine_in_ref, prop_in_ref, mid_ref, fine_out_ref,
+    prop_out_ref, saved_ref, dense_ref, summary_ref,
+    table, shifted, rows, eye, feats, weights, spacing, first, head, fine_logit, prop_logit,
 ):
     step = pl.program_id(0)
-    features = corners_ref.shape[1] // 8
+    parts = arrived_ref.shape[0]
+    width = arrived_ref.shape[2]
+    blocks = width // BLOCK
+    features = grid_ref.shape[0]
     hidden = mid_ref.shape[1]
     prop_hidden = prop_in_ref.shape[0]
-    width = corners_ref.shape[0] * LANES
+
+    def gather(row, block, pair):
+        start = row * width
+        for u in range(BLOCK):
+            k = idx_ref.at[pl.ds(block * BLOCK + u, idx_ref.shape[0] - width + 1)][start]
+            pair[2 * u : 2 * u + 2, :] = table[pl.ds(k, 2), :]
+
+    def interpolate(block, pair, slot):
+        near = pair[pl.ds(0, BLOCK, stride=2), :].astype(BF16)
+        far = pair[pl.ds(1, BLOCK, stride=2), :].astype(BF16)
+        unit = jnp.concatenate([eye[0], eye[1]], axis=1)
+        t = dot_nt(unit, jnp.concatenate([near, far], axis=1))
+        at = slice(block * BLOCK, (block + 1) * BLOCK)
+        total = jnp.zeros((features, BLOCK), F32)
+        for corner in range(8):
+            place = (corner % 2) * 4 + corner // 2
+            w = weights[corner, pl.ds(step, 1), at]
+            total = total + t[place * features : (place + 1) * features] * w
+        feats[slot, :, at] = total.astype(BF16)
+
+    def networks(row, slot):
+        feat = feats[slot]
+        both = jnp.maximum(dot(first[...], feat), 0.0).astype(BF16)
+        h = both[:hidden]
+        ph = both[hidden:]
+        for layer in range(mid_ref.shape[0]):
+            h = jnp.maximum(dot(mid_ref[layer], h), 0.0).astype(BF16)
+        logits = dot(head[...], jnp.concatenate([h, ph], axis=0))
+        fine_logit[pl.ds(row, 1), :] = logits[0:1]
+        prop_logit[pl.ds(row, 1), :] = logits[1:2]
+        saved_ref[:features, :] = feat
+        saved_ref[features:, :] = ph
 
     @pl.when(step == 0)
     def _():
-        parts = arrived_ref.shape[0]
-        blocks = [arrived_ref[q].astype(F32) for q in range(parts)]
-        g = [stack_rows(blocks, j) for j in range(4)]
+        down = lax.broadcasted_iota(jnp.int32, (BLOCK, BLOCK), 0)
+        across = lax.broadcasted_iota(jnp.int32, (BLOCK, BLOCK), 1)
+        same = (down == across).astype(BF16)
+        eye[0] = same[:, :LANES]
+        eye[1] = same[:, LANES:]
+        feats[...] = jnp.zeros(feats.shape, BF16)
+        whole = [arrived_ref[q].astype(F32) for q in range(parts)]
+        g = [stack_rows(whole, j) for j in range(4)]
         spacing[...] = g[3]
         first[:hidden, :] = fine_in_ref[...].astype(F32).T.astype(BF16)
         first[hidden:, :] = prop_in_ref[...]
@@ -300,31 +281,23 @@
             bits = (corner // 4, corner // 2 % 2, corner % 2)
             w = [x if bit else 1.0 - x for x, bit in zip(g, bits)]
             weights[corner] = w[0] * w[1] * w[2]
-
-    feats = []
-    row = [weights[corner, pl.ds(step, 1), :] for corner in range(8)]
-    for v in range(width // LANES):
-        at = v * LANES
-        total = jnp.zeros((features, LANES), F32)
-        for corner in range(8):
-            place = (corner % 2) * 4 + corner // 2
-            x = corners_ref[v, place * features : (place + 1) * features, :].astype(F32)
-            total = total + x * row[corner][:, at : at + LANES]
-        feats.append(total.astype(BF16))
-    feat = jnp.concatenate(feats, axis=1)
-    both = jnp.maximum(dot(first[...], feat), 0.0).astype(BF16)
-    h = both[:hidden]
-    ph = both[hidden:]
-    for layer in range(mid_ref.shape[0]):
-        h = jnp.maximum(dot(mid_ref[layer], h), 0.0).astype(BF16)
-    logits = dot(head[...], jnp.concatenate([h, ph], axis=0))
-    fine_logit[pl.ds(step, 1), :] = logits[0:1]
-    prop_logit[pl.ds(step, 1), :] = logits[1:2]
-    saved_ref[:features, :] = feat
-    saved_ref[features:, :] = ph
-
-    @pl.when(step == pl.num_programs(0) - 1)
+        build_table(grid_ref, table, shifted)
+        gather(0, 0, rows.at[0])
+
+    @pl.when(step < parts)
     def _():
+        networks(jnp.maximum(step - 1, 0), (step + 1) % 2)
+        for j in range(blocks):
+            ahead = rows.at[(j + 1) % DEPTH]
+            if j + 1 < blocks:
+                gather(step, j + 1, ahead)
+            else:
+                gather(jnp.minimum(step + 1, parts - 1), 0, ahead)
+            interpolate(j, rows.at[j % DEPTH], step % 2)
+
+    @pl.when(step == parts)
+    def _():
+        networks(parts - 1, (parts - 1) % 2)
         space = pieces_of(spacing[...])
         results = []
         for k, ref in enumerate((prop_logit, fine_logit)):
@@ -351,14 +324,14 @@
             for k, x in enumerate(stats[s * per : (s + 1) * per]):
                 slab = jnp.where(group == k, x, slab)
             slabs.append(slab)
-        summary_ref[...] = jnp.concatenate(slabs, axis=1)
-
-
-def forward(corners, arrived, fine_in, prop_in, mid, fine_out, prop_out, cap):
-    rows = corners.shape[1]
-    total = corners.shape[0] * LANES
+        summary = jnp.concatenate(slabs, axis=1)
+        for p in range(parts):
+            summary_ref[p] = summary
+
+
+def forward(cells, grid, arrived, fine_in, prop_in, mid, fine_out, prop_out, cap):
     parts, _, width = arrived.shape
-    features = rows // 8
+    features, total = grid.shape
     hidden = mid.shape[1]
     prop_hidden = prop_in.shape[0]
     kept = features + prop_hidden
@@ -367,20 +340,28 @@
     small = (arrived, fine_in, prop_in, mid, fine_out, prop_out)
     return pl.pallas_call(
         functools.partial(forward_kernel, cap),
-        grid=(parts,),
+        grid=(parts + 1,),
         out_shape=(
-            jax.ShapeDtypeStruct((kept, total), BF16),
+            jax.ShapeDtypeStruct((kept, parts * width), BF16),
             jax.ShapeDtypeStruct((4, parts, width), F32),
-            jax.ShapeDtypeStruct((parts, stat_lanes), F32),
+            jax.ShapeDtypeStruct((parts, parts, stat_lanes), F32),
         ),
-        in_specs=[pl.BlockSpec((width // LANES, rows, LANES), lambda q: (q, 0, 0))]
+        in_specs=[
+            pl.BlockSpec(memory_space=pltpu.SMEM),
+            pl.BlockSpec((features, total), lambda q: (0, 0), pipeline_mode=pl.Buffered(1)),
+        ]
         + [whole(x.shape) for x in small],
         out_specs=(
-            pl.BlockSpec((kept, width), lambda q: (0, q)),
+            pl.BlockSpec((kept, width), lambda q: (0, jnp.maximum(q - 1, 0))),
             whole((4, parts, width)),
-            whole((parts, stat_lanes)),
+            whole((parts, parts, stat_lanes)),
         ),
         scratch_shapes=[
+            pltpu.VMEM((total, LANES), F32),
+            pltpu.VMEM((features, total), BF16),
+            pltpu.VMEM((DEPTH, 2 * BLOCK, LANES), F32),
+            pltpu.VMEM((2, BLOCK, LANES), BF16),
+            pltpu.VMEM((2, features, width), BF16),
             pltpu.VMEM((8, parts, width), F32),
             pltpu.VMEM((parts, width), F32),
             pltpu.VMEM((hidden + prop_hidden, features), BF16),
@@ -388,9 +369,9 @@
             pltpu.VMEM((parts, width), F32),
             pltpu.VMEM((parts, width), F32),
         ],
-        compiler_params=pltpu.CompilerParams(vmem_limit_bytes=60 * 1024 * 1024),
+        compiler_params=pltpu.CompilerParams(vmem_limit_bytes=40 * 1024 * 1024),
         name="forward",
-    )(corners, *small)
+    )(cells, grid, *small)
 
 
 def backward_kernel(
@@ -538,7 +519,7 @@
         out_specs=(vmem, vmem),
         scratch_shapes=[pltpu.VMEM((parts, width), F32)]
         + ([] if masks else [pltpu.VMEM((slots, parts), F32)]),
-        compiler_params=pltpu.CompilerParams(vmem_limit_bytes=48 * 1024 * 1024),
+        compiler_params=pltpu.CompilerParams(vmem_limit_bytes=(16 if masks else 48) * 1024 * 1024),
         name="backward",
     )(me, stats, key, hot, dense, saved, prop_out, *masks)
 
@@ -569,17 +550,14 @@
     features = feature_grid.shape[1]
     prop_hidden = prop_in.shape[1]
     outgoing = pack(
-        sample_geometry[:, 0, 0], slot_ray[0, 0], slot_rank[0, 0], bucket_count.reshape(-1, 1)
+        sample_geometry[:, 0, 0], slot_ray[0, 0], slot_rank[0, 0], bucket_count.reshape(-1)
     )
     arrived = lax.all_to_all(outgoing, "dom", split_axis=0, concat_axis=0, tiled=True)
-    corners = gather_corners(sample_cells.reshape(-1), feature_grid[0], parts)
     saved, dense, summary = forward(
-        corners, arrived, fine_in[0].T, prop_in[0], fine_mid[0], fine_out, prop_out, cap
-    )
-    stats = lax.all_to_all(
-        jnp.broadcast_to(summary[None], (parts,) + summary.shape),
-        "dom", split_axis=0, concat_axis=0, tiled=True,
-    )
+        sample_cells.reshape(-1), feature_grid[0], arrived,
+        fine_in[0].T, prop_in[0], fine_mid[0], fine_out, prop_out, cap,
+    )
+    stats = lax.all_to_all(summary, "dom", split_axis=0, concat_axis=0, tiled=True)
     me = lax.axis_index("dom").reshape(1).astype(jnp.int32)
     marks = slot_marks(me, arrived, cap)
     ray_loss, grads = backward(me, stats, dense, saved, prop_out, marks, cap)

time: 72.1 us -> 69.4 us (0.963)
  Pallas kernels: 39.4 us -> 32.9 us
  waiting for transfers between devices: 6.39 us -> 12.4 us
  local copies, waits for them, and re-layouts: 11.2 us -> 10 us
  starting transfers between devices: 13.6 us -> 12.7 us
    pallas_call x2 -> x1, Pallas kernels: 31.9 us -> 25.4 us  [forward(): pl.pallas_call(functools.partial(forward_kernel, cap), grid=(parts + 1,),...]
    all_to_all x1, waiting for transfers between devices: 0.01 us -> 6.05 us  [on_device(): lax.all_to_all(outgoing, 'dom', split_axis=0, concat_axis=0, tiled=True)]
    unnamed x15 -> x23, local copies, waits for them, and re-layouts: 7.41 us -> 8.82 us
    broadcast_in_dim x1 -> x0, local copies, waits for them, and re-layouts: 1.32 us -> none  [on_device(): jnp.broadcast_to(summary[None], (parts,) + summary.shape)]
    reshape x1 -> x0, local copies, waits for them, and re-layouts: 1.32 us -> none  [on_device(): bucket_count.reshape(-1, 1)]
    all_to_all x1, starting transfers between devices: 4.18 us -> 3.35 us  [on_device(): lax.all_to_all(summary, 'dom', split_axis=0, concat_axis=0, tiled=True)]
  transfers between devices with their start and end apart: 5 -> 5, of which waited for: 3 -> 4; matrix products, arithmetic and copies ran while one was open for 2% -> 1% of each run, Pallas kernels for 33% -> 4%
where the time goes in v3:
time: 69.4 us; the launch traced here: 68.7 us
  Pallas kernels  32.9 us (47%)
  starting transfers between devices  12.7 us (18%)
  waiting for transfers between devices  12.4 us (18%)
  local copies, waits for them, and re-layouts  10 us (14%)
    pallas_call x1, Pallas kernels, forward(): pl.pallas_call(functools.partial(forward_kernel, cap), grid=(parts + 1,),...  25.4 us
    unnamed x23, local copies, waits for them, and re-layouts  8.82 us
    all_to_all x1, waiting for transfers between devices, on_device(): lax.all_to_all(outgoing, 'dom', split_axis=0, concat_axis=0, tiled=True)  6.05 us
    all_to_all x1, starting transfers between devices, on_device(): lax.all_to_all(outgoing, 'dom', split_axis=0, concat_axis=0, tiled=True)  5.2 us
    ppermute x3, starting transfers between devices, sum_replicas(): lax.ppermute(x, 'rep', [(i, i ^ s) for i in range(count)])  4.16 us
    ppermute x3, waiting for transfers between devices, sum_replicas(): lax.ppermute(x, 'rep', [(i, i ^ s) for i in range(count)])  3.97 us
    all_to_all x1, starting transfers between devices, on_device(): lax.all_to_all(summary, 'dom', split_axis=0, concat_axis=0, tiled=True)  3.35 us
    pallas_call x1, Pallas kernels, backward(): pl.pallas_call(functools.partial(backward_kernel, cap), out_shape=(jax.Sh...  3.09 us
  transfers between devices with their start and end apart: 5, of which 4 were waited for; matrix products, arithmetic and copies ran while one was open for 1% of the time, Pallas kernels for 4%

profile of v3, /device:TPU:0, one launch (start us, length us, event | category | flops | bytes accessed | tf_op | source)
XLA Modules:
  0.0 68.7 jit_solution(2623392059307417795)
XLA Ops:
  0.6 1.8 %pack.1 = bf16[8,5,2048]{2,1,0:T(8,128)(2,1)} custom-call(bf16[4,8,2048]{2,1,0:T(8,128)(2,1)} %bitcast.21, s32[8,32]{1,0:T(8,128)} %bitcast.23, s32[8,32]{1,0:T(8,128)} %bitcast.24, s32[8]{0:T(128)} %bitcast.25), custom_call_target="tpu_custom_call" | custom-call | tf_op jit(solution)/shard_map/pack/pallas_call | solution.py:83
  2.5 5.2 %all-to-all-start = ((bf16[8,5,2048]{2,1,0:T(8,128)(2,1)}), bf16[8,5,2048]{2,1,0:T(8,128)(2,1)S(1)}, u32[]{:S(2)}, u32[]{:S(2)}) async-start(bf16[8,5,2048]{2,1,0:T(8,128)(2,1)} %pack.1), calls=%async_computation | async-start | bytes 524288 | tf_op jit(solution)/shard_map/all_to_all | solution.py:555
  7.7 0.9 %copy.14 = s32[1,16,8,128]{3,1,2,0:T(8,128)S(1)} copy(s32[1,16,8,128]{3,2,1,0:T(8,128)} %bitcast.22) | data formatting | bytes 131072
  8.5 6.0 %all-to-all-done.arrived_ref = bf16[8,5,2048]{2,1,0:T(8,128)(2,1)S(1)} async-done(((bf16[8,5,2048]{2,1,0:T(8,128)(2,1)}), bf16[8,5,2048]{2,1,0:T(8,128)(2,1)S(1)}, u32[]{:S(2)}, u32[]{:S(2)}) %all-to-all-start) | async-done | bytes 163872 | tf_op jit(solution)/shard_map/all_to_all | solution.py:555
  14.6 1.7 %copy-done.1 = bf16[1,32,32768]{2,1,0:T(8,128)(2,1)S(1)} copy-done((bf16[1,32,32768]{2,1,0:T(8,128)(2,1)S(1)}, bf16[1,32,32768]{2,1,0:T(8,128)(2,1)}, u32[]{:S(2)}) %copy-start.1) | copy-done | bytes 2097176
  16.2 0.8 %copy-done.4 = bf16[1,2,64,64]{3,2,1,0:T(8,128)(2,1)S(1)} copy-done((bf16[1,2,64,64]{3,2,1,0:T(8,128)(2,1)S(1)}, bf16[1,2,64,64]{3,2,1,0:T(8,128)(2,1)}, u32[]{:S(2)}) %copy-start.4) | copy-done | bytes 16408
  17.0 0.7 %copy-done.5 = bf16[1,64,32]{1,2,0:T(8,128)(2,1)S(1)} copy-done((bf16[1,64,32]{1,2,0:T(8,128)(2,1)S(1)}, bf16[1,64,32]{1,2,0:T(8,128)(2,1)}, u32[]{:S(2)}) %copy-start.5) | copy-done | bytes 4120
  17.7 0.7 copy-done.7
  18.4 0.7 copy-done.8
  19.0 0.7 copy-done.10
  19.7 25.4 %forward.1 = (bf16[48,16384]{1,0:T(8,128)(2,1)S(1)}, f32[4,8,2048]{2,1,0:T(8,128)S(1)}, f32[8,8,256]{2,1,0:T(8,128)}) custom-call(s32[16384]{0:T(1024)S(1)} %bitcast.17, bf16[32,32768]{1,0:T(8,128)(2,1)S(1)} %bitcast.16, bf16[8,5,2048]{2,1,0:T(8,128)(2,1)S(1)} %all-to-all-done.arrived_ref, bf16[32,64]{1,0:T(8,128)(2,1)S(1)} %bitcast.19, ...), custom_call_target="tpu_custom_call" | custom-call | tf_op jit(solution)/shard_map/forward/pallas_call | solution.py:341
  45.1 3.3 %all-to-all-start.1 = ((f32[8,8,256]{2,1,0:T(8,128)}), f32[8,8,256]{2,1,0:T(8,128)S(1)}, u32[]{:S(2)}, u32[]{:S(2)}) async-start(f32[8,8,256]{2,1,0:T(8,128)} %get-tuple-element.11), calls=%async_computation.1 | async-start | bytes 131072 | tf_op jit(solution)/shard_map/all_to_all | solution.py:560
  48.5 2.6 %slot_marks.1 = (f32[8,256]{1,0:T(8,128)}, bf16[256,256]{1,0:T(8,128)(2,1)}, bf16[8,256,256]{2,1,0:T(8,128)(2,1)}) custom-call(s32[1]{0:T(128)} %bitcast.me_ref, bf16[8,5,2048]{2,1,0:T(8,128)(2,1)} %copy-done), custom_call_target="tpu_custom_call" | custom-call | flops 4194304 | bytes 4194304 | tf_op jit(solution)/shard_map/slot_marks/pallas_call | solution.py:128
  51.1 2.3 %all-to-all-done.1.stats_ref = f32[8,8,256]{2,1,0:T(8,128)S(1)} async-done(((f32[8,8,256]{2,1,0:T(8,128)}), f32[8,8,256]{2,1,0:T(8,128)S(1)}, u32[]{:S(2)}, u32[]{:S(2)}) %all-to-all-start.1) | async-done | bytes 65568 | tf_op jit(solution)/shard_map/all_to_all | solution.py:560
  53.4 1.2 %copy-done.2 = bf16[8,256,256]{2,1,0:T(8,128)(2,1)S(1)} copy-done((bf16[8,256,256]{2,1,0:T(8,128)(2,1)S(1)}, bf16[8,256,256]{2,1,0:T(8,128)(2,1)}, u32[]{:S(2)}) %copy-start.2) | copy-done | bytes 1048600
  54.6 0.9 %copy-done.3 = bf16[256,256]{1,0:T(8,128)(2,1)S(1)} copy-done((bf16[256,256]{1,0:T(8,128)(2,1)S(1)}, bf16[256,256]{1,0:T(8,128)(2,1)}, u32[]{:S(2)}) %copy-start.3) | copy-done | bytes 131096
  55.5 0.7 %copy-done.6 = f32[8,256]{1,0:T(8,128)S(1)} copy-done((f32[8,256]{1,0:T(8,128)S(1)}, f32[8,256]{1,0:T(8,128)}, u32[]{:S(2)}) %copy-start.6) | copy-done | bytes 8216
  56.2 3.1 %backward.1 = (f32[1,256]{1,0:T(1,128)}, f32[32,48]{1,0:T(8,128)S(1)}) custom-call(s32[1]{0:T(128)} %bitcast.me_ref, f32[8,8,256]{2,1,0:T(8,128)S(1)} %all-to-all-done.1.stats_ref, f32[8,256]{1,0:T(8,128)S(1)} %copy-done.6, bf16[256,256]{1,0:T(8,128)(2,1)S(1)} %copy-done.3, f32[4,8,2048]{2,1,0:T(8,128)S(1)} %get-tuple-element.14.dense_ref, ...), custom_call_target="tpu_custom_call" | custom-call | tf_op jit(solution)/shard_map/backward/pallas_call | solution.py:512
  59.3 2.6 %collective-permute-start.1 = (f32[32,48]{1,0:T(8,128)S(1)}, f32[32,48]{1,0:T(8,128)S(1)}, u32[]{:S(2)}, u32[]{:S(2)}) collective-permute-start(f32[32,48]{1,0:T(8,128)S(1)} %get-tuple-element.18), channel_id=1, source_target_pairs={{0,2},{1,3},{2,0},{3,1},{4,6},{5,7},{6,4},{7,5},{8,10},{9,11},{10,... | collective-permute-start | bytes 18440 | tf_op jit(solution)/shard_map/ppermute | solution.py:531
  61.9 1.4 %collective-permute-start.2 = (f32[32,48]{1,0:T(8,128)S(1)}, f32[32,48]{1,0:T(8,128)S(1)}, u32[]{:S(2)}, u32[]{:S(2)}) collective-permute-start(f32[32,48]{1,0:T(8,128)S(1)} %get-tuple-element.18), channel_id=1, source_target_pairs={{0,3},{1,2},{2,1},{3,0},{4,7},{5,6},{6,5},{7,4},{8,11},{9,10},{10,... | collective-permute-start | bytes 18440 | tf_op jit(solution)/shard_map/ppermute | solution.py:531
  63.5 0.5 collective-permute-done.1
  64.0 3.5 %collective-permute-done.2 = f32[32,48]{1,0:T(8,128)S(1)} collective-permute-done((f32[32,48]{1,0:T(8,128)S(1)}, f32[32,48]{1,0:T(8,128)S(1)}, u32[]{:S(2)}, u32[]{:S(2)}) %collective-permute-start.2) | collective-permute-done | bytes 6176 | tf_op jit(solution)/shard_map/ppermute | solution.py:531
  67.5 0.6 slice_bitcast_fusion
  68.1 0.6 slice.9
  (16 shorter events, 0.2 us)
Async XLA Ops:
  0.6 52.8 %copy-start.9 = (bf16[1,16]{1,0:T(2,128)(2,1)S(1)}, bf16[1,16]{1,0:T(2,128)(2,1)}, u32[]{:S(2)}) copy-start(bf16[1,16]{1,0:T(2,128)(2,1)} %prop_out_ref.3) | copy-start | bytes 100
  2.5 12.1 %all-to-all-start = ((bf16[8,5,2048]{2,1,0:T(8,128)(2,1)}), bf16[8,5,2048]{2,1,0:T(8,128)(2,1)S(1)}, u32[]{:S(2)}, u32[]{:S(2)}) async-start(bf16[8,5,2048]{2,1,0:T(8,128)(2,1)} %pack.1), calls=%async_computation | async-start | bytes 524288 | tf_op jit(solution)/shard_map/all_to_all | solution.py:555
  14.6 33.9 %copy-start = (bf16[8,5,2048]{2,1,0:T(8,128)(2,1)}, bf16[8,5,2048]{2,1,0:T(8,128)(2,1)S(1)}, u32[]{:S(2)}) copy-start(bf16[8,5,2048]{2,1,0:T(8,128)(2,1)S(1)} %all-to-all-done.arrived_ref) | copy-start | bytes 491524
  14.6 1.7 %copy-start.1 = (bf16[1,32,32768]{2,1,0:T(8,128)(2,1)S(1)}, bf16[1,32,32768]{2,1,0:T(8,128)(2,1)}, u32[]{:S(2)}) copy-start(bf16[1,32,32768]{2,1,0:T(8,128)(2,1)} %param.11) | copy-start | bytes 6291460
  16.2 0.8 %copy-start.4 = (bf16[1,2,64,64]{3,2,1,0:T(8,128)(2,1)S(1)}, bf16[1,2,64,64]{3,2,1,0:T(8,128)(2,1)}, u32[]{:S(2)}) copy-start(bf16[1,2,64,64]{3,2,1,0:T(8,128)(2,1)} %param.13) | copy-start | bytes 49156
  17.0 0.7 %copy-start.5 = (bf16[1,64,32]{1,2,0:T(8,128)(2,1)S(1)}, bf16[1,64,32]{1,2,0:T(8,128)(2,1)}, u32[]{:S(2)}) copy-start(bf16[1,64,32]{1,2,0:T(8,128)(2,1)} %param.12) | copy-start | bytes 12292
  17.7 0.7 %copy-start.7 = (bf16[1,16,32]{2,1,0:T(8,128)(2,1)S(1)}, bf16[1,16,32]{2,1,0:T(8,128)(2,1)}, u32[]{:S(2)}) copy-start(bf16[1,16,32]{2,1,0:T(8,128)(2,1)} %param.15) | copy-start | bytes 3076
  18.4 0.7 copy-start.8
  19.0 0.7 copy-start.10
  45.1 8.3 %all-to-all-start.1 = ((f32[8,8,256]{2,1,0:T(8,128)}), f32[8,8,256]{2,1,0:T(8,128)S(1)}, u32[]{:S(2)}, u32[]{:S(2)}) async-start(f32[8,8,256]{2,1,0:T(8,128)} %get-tuple-element.11), calls=%async_computation.1 | async-start | bytes 131072 | tf_op jit(solution)/shard_map/all_to_all | solution.py:560
  53.4 1.2 %copy-start.2 = (bf16[8,256,256]{2,1,0:T(8,128)(2,1)S(1)}, bf16[8,256,256]{2,1,0:T(8,128)(2,1)}, u32[]{:S(2)}) copy-start(bf16[8,256,256]{2,1,0:T(8,128)(2,1)} %get-tuple-element.16.rest_0_) | copy-start | bytes 3145732
  54.6 0.9 %copy-start.3 = (bf16[256,256]{1,0:T(8,128)(2,1)S(1)}, bf16[256,256]{1,0:T(8,128)(2,1)}, u32[]{:S(2)}) copy-start(bf16[256,256]{1,0:T(8,128)(2,1)} %get-tuple-element.13.hot_ref) | copy-start | bytes 393220
  55.5 0.7 %copy-start.6 = (f32[8,256]{1,0:T(8,128)S(1)}, f32[8,256]{1,0:T(8,128)}, u32[]{:S(2)}) copy-start(f32[8,256]{1,0:T(8,128)} %get-tuple-element.12.key_ref) | copy-start | bytes 24580
  59.3 4.6 %collective-permute-start.1 = (f32[32,48]{1,0:T(8,128)S(1)}, f32[32,48]{1,0:T(8,128)S(1)}, u32[]{:S(2)}, u32[]{:S(2)}) collective-permute-start(f32[32,48]{1,0:T(8,128)S(1)} %get-tuple-element.18), channel_id=1, source_target_pairs={{0,2},{1,3},{2,0},{3,1},{4,6},{5,7},{6,4},{7,5},{8,10},{9,11},{10,... | collective-permute-start | bytes 18440 | tf_op jit(solution)/shard_map/ppermute | solution.py:531
  61.9 5.5 %collective-permute-start.2 = (f32[32,48]{1,0:T(8,128)S(1)}, f32[32,48]{1,0:T(8,128)S(1)}, u32[]{:S(2)}, u32[]{:S(2)}) collective-permute-start(f32[32,48]{1,0:T(8,128)S(1)} %get-tuple-element.18), channel_id=1, source_target_pairs={{0,3},{1,2},{2,1},{3,0},{4,7},{5,6},{6,5},{7,4},{8,11},{9,10},{10,... | collective-permute-start | bytes 18440 | tf_op jit(solution)/shard_map/ppermute | solution.py:531
  63.3 4.2 %collective-permute-start = (f32[32,48]{1,0:T(8,128)S(1)}, f32[32,48]{1,0:T(8,128)S(1)}, u32[]{:S(2)}, u32[]{:S(2)}) collective-permute-start(f32[32,48]{1,0:T(8,128)S(1)} %get-tuple-element.18), channel_id=1, source_target_pairs={{0,1},{1,0},{2,3},{3,2},{4,5},{5,4},{6,7},{7,6},{8,9},{9,8},{10,11... | collective-permute-start | bytes 18440 | tf_op jit(solution)/shard_map/ppermute | solution.py:531

commit v4 on v3

--- a/solution.py
+++ b/solution.py
@@ -11,7 +11,7 @@
 RAY_DEV = 256
 LANES = 128
 BLOCK = 256
-BUILD_UNROLL = 31
+CHUNKS = 8
 DEPTH = 4
 
 distill_weight = 50.0
@@ -33,6 +33,10 @@
     mid = rest.astype(BF16)
     low = (rest - mid.astype(F32)).astype(BF16)
     return [hi, mid, low]
+
+
+def in_hbm(x):
+    return pltpu.with_memory_space_constraint(x, pltpu.HBM)
 
 
 def stack_rows(arrays, row):
@@ -55,8 +59,6 @@
 
 def pack_kernel(geometry_ref, ray_ref, rank_ref, count_ref, out_ref):
     parts, cap = ray_ref.shape
-    width = geometry_ref.shape[2]
-    extra = out_ref.shape[1] - 4
     sub = lax.broadcasted_iota(jnp.int32, (parts, cap), 0)
     count = jnp.zeros((parts, cap), jnp.int32)
     for p in range(parts):
@@ -66,23 +68,22 @@
     marks = jnp.concatenate(
         [flatten_slots(ray, cap), flatten_slots(rank_ref[...].astype(F32), cap)], axis=1
     )
-    spare = extra * width - marks.shape[1]
-    if spare:
-        marks = jnp.concatenate([marks, jnp.zeros((1, spare), F32)], axis=1)
-    marks = [marks[:, e * width : (e + 1) * width] for e in range(extra)]
+    quarter = marks.shape[1] // 4
     g = [geometry_ref[j].astype(F32) for j in range(4)]
     for p in range(parts):
-        block = [x[p : p + 1] for x in g] + marks
-        out_ref[p] = jnp.concatenate(block, axis=0).astype(BF16)
+        rows = [
+            jnp.concatenate([x[p : p + 1], marks[:, j * quarter : (j + 1) * quarter]], axis=1)
+            for j, x in enumerate(g)
+        ]
+        out_ref[p] = jnp.concatenate(rows, axis=0).astype(BF16)
 
 
 def pack(geometry, ray, rank, count):
     parts, width = geometry.shape[1:]
-    extra = -(-2 * ray.size // width)
     vmem = pl.BlockSpec(memory_space=pltpu.VMEM)
     return pl.pallas_call(
         pack_kernel,
-        out_shape=jax.ShapeDtypeStruct((parts, 4 + extra, width), BF16),
+        out_shape=jax.ShapeDtypeStruct((parts, 4, width + ray.size // 2), BF16),
         in_specs=[vmem] * 3 + [pl.BlockSpec(memory_space=pltpu.SMEM)],
         out_specs=vmem,
         name="pack",
@@ -93,14 +94,12 @@
     me = me_ref[0]
     parts = arrived_ref.shape[0]
     slots = parts * cap
-    width = arrived_ref.shape[2]
-    extra = arrived_ref.shape[1] - 4
+    width = arrived_ref.shape[2] - slots // 2
     ray, rank = [], []
     for q in range(parts):
-        marks = [arrived_ref[q].astype(F32)[4 + e : 5 + e] for e in range(extra)]
-        marks = marks[0] if extra == 1 else jnp.concatenate(marks, axis=1)
-        ray.append(marks[:, :slots])
-        rank.append(marks[:, slots : 2 * slots])
+        marks = arrived_ref[q, :, width:].astype(F32)
+        ray.append(jnp.concatenate([marks[0:1], marks[1:2]], axis=1))
+        rank.append(jnp.concatenate([marks[2:3], marks[3:4]], axis=1))
     key = jnp.concatenate(ray, axis=0) * (2.0 * parts) + jnp.concatenate(rank, axis=0)
     key_ref[...] = key
     key_t = key.T
@@ -133,6 +132,7 @@
         cost_estimate=pl.CostEstimate(
             flops=parts * slots * slots * 8, bytes_accessed=4 << 20, transcendentals=0
         ),
+        compiler_params=pltpu.CompilerParams(vmem_limit_bytes=12 * 1024 * 1024),
         name="slot_marks",
     )(me, arrived)
 
@@ -183,46 +183,47 @@
     return [x[:, v * LANES : (v + 1) * LANES] for v in range(x.shape[1] // LANES)]
 
 
-def build_table(grid_ref, table, shifted):
-    cells = grid_ref.shape[1]
+def fetch_grid(grid_hbm, grid_ref, sem, c):
+    chunk = grid_ref.shape[1] // CHUNKS
+    at = pl.ds(c * chunk, chunk)
+    return pltpu.make_async_copy(grid_hbm.at[:, at], grid_ref.at[:, at], sem.at[c])
+
+
+def build_table(grid_hbm, grid_ref, sem, table):
+    features, cells = grid_ref.shape
     plane = GR * GR
-    span = 2048
-
-    def shift(b, carry):
-        c0 = pl.multiple_of(b * span, span)
-        x = grid_ref[:, pl.ds(c0, span + LANES)]
-        shifted[:, pl.ds(c0, span)] = x[:, GR : GR + span]
-        return carry
-
-    lax.fori_loop(0, cells // span - 1, shift, 0)
-    last = grid_ref[:, cells - span :]
-    shifted[:, cells - span :] = jnp.concatenate([last[:, GR:], last[:, :GR]], axis=1)
-
-    def build(b, carry):
-        c0 = pl.multiple_of(b * 2 * BLOCK, 2 * BLOCK)
-        for half in range(2):
-            x = [
-                ref[:, pl.ds(c0 + half * BLOCK + across, BLOCK)]
-                for across in (0, plane)
-                for ref in (grid_ref, shifted)
-            ]
-            rows = jnp.concatenate(x, axis=0).T.astype(F32)
-            table[pl.ds(c0 + half * BLOCK, BLOCK), :] = rows
-        return carry
-
-    lax.fori_loop(0, (cells - plane) // (2 * BLOCK), build, 0, unroll=BUILD_UNROLL)
+    span = 2 * BLOCK
+    chunk = cells // CHUNKS
+    upper = lax.broadcasted_iota(jnp.int32, (span, LANES), 1) // features % 2 == 1
+
+    def build(i, carry, top):
+        c0 = pl.multiple_of(top - (i + 1) * span, span)
+        base = grid_ref[:, pl.ds(c0, span)]
+        across = grid_ref[:, pl.ds(c0 + plane, span)]
+        rows = jnp.concatenate([base, base, across, across], axis=0).T.astype(F32)
+        table[pl.ds(c0, span), :] = jnp.where(
+            upper, jnp.concatenate([rows[GR:], carry], axis=0), rows
+        )
+        return rows[:GR]
+
+    carry = jnp.zeros((GR, LANES), F32)
+    for c in reversed(range(CHUNKS)):
+        fetch_grid(grid_hbm, grid_ref, sem, c).wait()
+        top = cells - plane if c == CHUNKS - 1 else (c + 1) * chunk
+        body = functools.partial(build, top=top)
+        carry = lax.fori_loop(0, (top - c * chunk) // span, body, carry, unroll=True)
 
 
 def forward_kernel(
-    cap, idx_ref, grid_ref, arrived_ref, fine_in_ref, prop_in_ref, mid_ref, fine_out_ref,
+    cap, idx_ref, grid_hbm, arrived_ref, fine_in_ref, prop_in_ref, mid_ref, fine_out_ref,
     prop_out_ref, saved_ref, dense_ref, summary_ref,
-    table, shifted, rows, eye, feats, weights, spacing, first, head, fine_logit, prop_logit,
+    table, grid_ref, grid_sem, rows, eye, feats, weights, spacing, first, head, fine_logit, prop_logit,
 ):
     step = pl.program_id(0)
     parts = arrived_ref.shape[0]
-    width = arrived_ref.shape[2]
+    width = idx_ref.shape[0] // parts
     blocks = width // BLOCK
-    features = grid_ref.shape[0]
+    features = prop_in_ref.shape[1]
     hidden = mid_ref.shape[1]
     prop_hidden = prop_in_ref.shape[0]
 
@@ -260,13 +261,15 @@
 
     @pl.when(step == 0)
     def _():
+        for c in reversed(range(CHUNKS)):
+            fetch_grid(grid_hbm, grid_ref, grid_sem, c).start()
         down = lax.broadcasted_iota(jnp.int32, (BLOCK, BLOCK), 0)
         across = lax.broadcasted_iota(jnp.int32, (BLOCK, BLOCK), 1)
         same = (down == across).astype(BF16)
         eye[0] = same[:, :LANES]
         eye[1] = same[:, LANES:]
         feats[...] = jnp.zeros(feats.shape, BF16)
-        whole = [arrived_ref[q].astype(F32) for q in range(parts)]
+        whole = [arrived_ref[q, :, :width].astype(F32) for q in range(parts)]
         g = [stack_rows(whole, j) for j in range(4)]
         spacing[...] = g[3]
         first[:hidden, :] = fine_in_ref[...].astype(F32).T.astype(BF16)
@@ -281,7 +284,7 @@
             bits = (corner // 4, corner // 2 % 2, corner % 2)
             w = [x if bit else 1.0 - x for x, bit in zip(g, bits)]
             weights[corner] = w[0] * w[1] * w[2]
-        build_table(grid_ref, table, shifted)
+        build_table(grid_hbm, grid_ref, grid_sem, table)
         gather(0, 0, rows.at[0])
 
     @pl.when(step < parts)
@@ -330,7 +333,8 @@
 
 
 def forward(cells, grid, arrived, fine_in, prop_in, mid, fine_out, prop_out, cap):
-    parts, _, width = arrived.shape
+    parts = arrived.shape[0]
+    width = cells.shape[0] // parts
     features, total = grid.shape
     hidden = mid.shape[1]
     prop_hidden = prop_in.shape[0]
@@ -348,7 +352,7 @@
         ),
         in_specs=[
             pl.BlockSpec(memory_space=pltpu.SMEM),
-            pl.BlockSpec((features, total), lambda q: (0, 0), pipeline_mode=pl.Buffered(1)),
+            pl.BlockSpec(memory_space=pltpu.HBM),
         ]
         + [whole(x.shape) for x in small],
         out_specs=(
@@ -359,6 +363,7 @@
         scratch_shapes=[
             pltpu.VMEM((total, LANES), F32),
             pltpu.VMEM((features, total), BF16),
+            pltpu.SemaphoreType.DMA((CHUNKS,)),
             pltpu.VMEM((DEPTH, 2 * BLOCK, LANES), F32),
             pltpu.VMEM((2, BLOCK, LANES), BF16),
             pltpu.VMEM((2, features, width), BF16),
@@ -369,9 +374,9 @@
             pltpu.VMEM((parts, width), F32),
             pltpu.VMEM((parts, width), F32),
         ],
-        compiler_params=pltpu.CompilerParams(vmem_limit_bytes=40 * 1024 * 1024),
+        compiler_params=pltpu.CompilerParams(vmem_limit_bytes=(32 + parts // 2) * 1024 * 1024),
         name="forward",
-    )(cells, grid, *small)
+    )(cells, in_hbm(grid), arrived, *[in_hbm(x) for x in small[1:]])
 
 
 def backward_kernel(
@@ -519,7 +524,7 @@
         out_specs=(vmem, vmem),
         scratch_shapes=[pltpu.VMEM((parts, width), F32)]
         + ([] if masks else [pltpu.VMEM((slots, parts), F32)]),
-        compiler_params=pltpu.CompilerParams(vmem_limit_bytes=(16 if masks else 48) * 1024 * 1024),
+        compiler_params=pltpu.CompilerParams(vmem_limit_bytes=(12 if masks else 48) * 1024 * 1024),
         name="backward",
     )(me, stats, key, hot, dense, saved, prop_out, *masks)
 

time: 69.4 us -> 59.4 us (0.86)
  local copies, waits for them, and re-layouts: 10 us -> 2.04 us
  Pallas kernels: 32.9 us -> 30.5 us
    unnamed x23 -> x3, local copies, waits for them, and re-layouts: 8.82 us -> 0.86 us
    all_to_all x1, waiting for transfers between devices: 2.34 us -> 4.29 us  [on_device(): lax.all_to_all(summary, 'dom', split_axis=0, concat_axis=0, tiled=True)]
    pallas_call x1, Pallas kernels: 2.6 us -> 0.64 us  [slot_marks(): pl.pallas_call(functools.partial(marks_kernel, cap), out_shape=tuple(shap...]
    all_to_all x1, waiting for transfers between devices: 6.05 us -> 4.73 us  [on_device(): lax.all_to_all(outgoing, 'dom', split_axis=0, concat_axis=0, tiled=True)]
  transfers between devices with their start and end apart: 5 -> 5, of which waited for: 4 -> 4; matrix products, arithmetic and copies ran while one was open for 1% -> 1% of each run, Pallas kernels for 4% -> 1%
where the time goes in v4:
time: 59.4 us; the launch traced here: 59 us
  Pallas kernels  30.5 us (51%)
  waiting for transfers between devices  13 us (22%)
  starting transfers between devices  12.8 us (22%)
  local copies, waits for them, and re-layouts  2.04 us (3%)
  between operations  0.68 us (1%)
    pallas_call x1, Pallas kernels, forward(): pl.pallas_call(functools.partial(forward_kernel, cap), grid=(parts + 1,),...  25.1 us
    all_to_all x1, starting transfers between devices, on_device(): lax.all_to_all(outgoing, 'dom', split_axis=0, concat_axis=0, tiled=True)  5.2 us
    all_to_all x1, waiting for transfers between devices, on_device(): lax.all_to_all(outgoing, 'dom', split_axis=0, concat_axis=0, tiled=True)  4.73 us
    all_to_all x1, waiting for transfers between devices, on_device(): lax.all_to_all(summary, 'dom', split_axis=0, concat_axis=0, tiled=True)  4.29 us
    ppermute x3, starting transfers between devices, sum_replicas(): lax.ppermute(x, 'rep', [(i, i ^ s) for i in range(count)])  4.2 us
    ppermute x3, waiting for transfers between devices, sum_replicas(): lax.ppermute(x, 'rep', [(i, i ^ s) for i in range(count)])  3.96 us
    all_to_all x1, starting transfers between devices, on_device(): lax.all_to_all(summary, 'dom', split_axis=0, concat_axis=0, tiled=True)  3.36 us
    pallas_call x1, Pallas kernels, backward(): pl.pallas_call(functools.partial(backward_kernel, cap), out_shape=(jax.Sh...  3.1 us
  transfers between devices with their start and end apart: 5, of which 4 were waited for; matrix products, arithmetic and copies ran while one was open for 1% of the time, Pallas kernels for 1%

profile of v4, /device:TPU:0, one launch (start us, length us, event | category | flops | bytes accessed | tf_op | source)
XLA Modules:
  0.0 59.0 jit_solution(5368218114156368881)
XLA Ops:
  0.6 0.0 copy-start
  0.6 1.7 %pack.1 = bf16[8,4,2176]{2,1,0:T(4,128)(2,1)} custom-call(bf16[4,8,2048]{2,1,0:T(8,128)(2,1)} %bitcast.18, s32[8,32]{1,0:T(8,128)} %bitcast.22, s32[8,32]{1,0:T(8,128)} %bitcast.23, s32[8]{0:T(128)} %bitcast.25), custom_call_target="tpu_custom_call" | custom-call | tf_op jit(solution)/shard_map/pack/pallas_call | solution.py:84
  2.4 5.2 %all-to-all-start = ((bf16[8,4,2176]{2,1,0:T(4,128)(2,1)}), bf16[8,4,2176]{2,1,0:T(4,128)(2,1)S(1)}, u32[]{:S(2)}, u32[]{:S(2)}) async-start(bf16[8,4,2176]{2,1,0:T(4,128)(2,1)} %pack.1), calls=%async_computation | async-start | bytes 278528 | tf_op jit(solution)/shard_map/all_to_all | solution.py:560
  7.6 0.9 %copy.14 = s32[1,16,8,128]{3,1,2,0:T(8,128)S(1)} copy(s32[1,16,8,128]{3,2,1,0:T(8,128)} %bitcast.19) | data formatting | bytes 131072
  8.4 4.7 %all-to-all-done.arrived_ref = bf16[8,4,2176]{2,1,0:T(4,128)(2,1)S(1)} async-done(((bf16[8,4,2176]{2,1,0:T(4,128)(2,1)}), bf16[8,4,2176]{2,1,0:T(4,128)(2,1)S(1)}, u32[]{:S(2)}, u32[]{:S(2)}) %all-to-all-start) | async-done | bytes 139296 | tf_op jit(solution)/shard_map/all_to_all | solution.py:560
  13.2 25.1 %forward.1 = (bf16[48,16384]{1,0:T(8,128)(2,1)S(1)}, f32[4,8,2048]{2,1,0:T(8,128)S(1)}, f32[8,8,256]{2,1,0:T(8,128)}) custom-call(s32[16384]{0:T(1024)S(1)} %bitcast.16, bf16[32,32768]{1,0:T(8,128)(2,1)} %bitcast.17, bf16[8,4,2176]{2,1,0:T(4,128)(2,1)S(1)} %all-to-all-done.arrived_ref, bf16[32,64]{1,0:T(8,128)(2,1)} %bitcast.21, bf16[16,32]{1,0:T(8,128)(2,1)} %bitcast.24, ...), custom_call_target="tpu_custom_call" | custom-call | tf_op jit(solution)/shard_map/forward/pallas_call | solution.py:345
  38.2 3.4 %all-to-all-start.1 = ((f32[8,8,256]{2,1,0:T(8,128)}), f32[8,8,256]{2,1,0:T(8,128)S(1)}, u32[]{:S(2)}, u32[]{:S(2)}) async-start(f32[8,8,256]{2,1,0:T(8,128)} %get-tuple-element.11), calls=%async_computation.1 | async-start | bytes 131072 | tf_op jit(solution)/shard_map/all_to_all | solution.py:565
  41.6 0.6 %slot_marks.1 = (f32[8,256]{1,0:T(8,128)S(1)}, bf16[256,256]{1,0:T(8,128)(2,1)S(1)}, bf16[8,256,256]{2,1,0:T(8,128)(2,1)S(1)}) custom-call(s32[1]{0:T(128)} %bitcast.me_ref, bf16[8,4,2176]{2,1,0:T(4,128)(2,1)S(1)} %all-to-all-done.arrived_ref), custom_call_target="tpu_custom_call" | custom-call | flops 4194304 | bytes 4194304 | tf_op jit(solution)/shard_map/slot_marks/pallas_call | solution.py:127
  42.3 4.3 %all-to-all-done.1.stats_ref = f32[8,8,256]{2,1,0:T(8,128)S(1)} async-done(((f32[8,8,256]{2,1,0:T(8,128)}), f32[8,8,256]{2,1,0:T(8,128)S(1)}, u32[]{:S(2)}, u32[]{:S(2)}) %all-to-all-start.1) | async-done | bytes 65568 | tf_op jit(solution)/shard_map/all_to_all | solution.py:565
  46.6 0.0 copy-done
  46.6 3.1 %backward.1 = (f32[1,256]{1,0:T(1,128)}, f32[32,48]{1,0:T(8,128)S(1)}) custom-call(s32[1]{0:T(128)} %bitcast.me_ref, f32[8,8,256]{2,1,0:T(8,128)S(1)} %all-to-all-done.1.stats_ref, f32[8,256]{1,0:T(8,128)S(1)} %get-tuple-element.12.key_ref, bf16[256,256]{1,0:T(8,128)(2,1)S(1)} %get-tuple-element.13.hot_ref, f32[4,8,2048]{2,1,0:T(8,128)S(1)} %get-tuple-element.14.dense_ref, ...), custom_call_target="tpu_custom_call" | custom-call | tf_op jit(solution)/shard_map/backward/pallas_call | solution.py:517
  49.7 2.6 %collective-permute-start.1 = (f32[32,48]{1,0:T(8,128)S(1)}, f32[32,48]{1,0:T(8,128)S(1)}, u32[]{:S(2)}, u32[]{:S(2)}) collective-permute-start(f32[32,48]{1,0:T(8,128)S(1)} %get-tuple-element.18), channel_id=1, source_target_pairs={{0,2},{1,3},{2,0},{3,1},{4,6},{5,7},{6,4},{7,5},{8,10},{9,11},{10,... | collective-permute-start | bytes 18440 | tf_op jit(solution)/shard_map/ppermute | solution.py:536
  52.3 1.3 %collective-permute-start.2 = (f32[32,48]{1,0:T(8,128)S(1)}, f32[32,48]{1,0:T(8,128)S(1)}, u32[]{:S(2)}, u32[]{:S(2)}) collective-permute-start(f32[32,48]{1,0:T(8,128)S(1)} %get-tuple-element.18), channel_id=1, source_target_pairs={{0,3},{1,2},{2,1},{3,0},{4,7},{5,6},{6,5},{7,4},{8,11},{9,10},{10,... | collective-permute-start | bytes 18440 | tf_op jit(solution)/shard_map/ppermute | solution.py:536
  53.6 0.2 collective-permute-start
  53.9 0.4 collective-permute-done.1
  54.3 3.5 %collective-permute-done.2 = f32[32,48]{1,0:T(8,128)S(1)} collective-permute-done((f32[32,48]{1,0:T(8,128)S(1)}, f32[32,48]{1,0:T(8,128)S(1)}, u32[]{:S(2)}, u32[]{:S(2)}) %collective-permute-start.2) | collective-permute-done | bytes 6176 | tf_op jit(solution)/shard_map/ppermute | solution.py:536
  57.8 0.0 collective-permute-done
  57.8 0.6 %slice_bitcast_fusion = f32[1,16,32]{2,1,0:T(8,128)} fusion(f32[32,48]{1,0:T(8,128)S(1)} %add_add_fusion), kind=kLoop, calls=%fused_computation.1 | loop fusion | bytes 4096 | tf_op jit(solution)/shard_map/broadcast_in_dim | solution.py:572
  58.4 0.6 slice.9
  (1 shorter events, 0.0 us)
Async XLA Ops:
  0.6 45.9 %copy-start = (bf16[1,16]{1,0:T(2,128)(2,1)S(1)}, bf16[1,16]{1,0:T(2,128)(2,1)}, u32[]{:S(2)}) copy-start(bf16[1,16]{1,0:T(2,128)(2,1)} %prop_out_ref.3) | copy-start | bytes 100
  2.4 10.8 %all-to-all-start = ((bf16[8,4,2176]{2,1,0:T(4,128)(2,1)}), bf16[8,4,2176]{2,1,0:T(4,128)(2,1)S(1)}, u32[]{:S(2)}, u32[]{:S(2)}) async-start(bf16[8,4,2176]{2,1,0:T(4,128)(2,1)} %pack.1), calls=%async_computation | async-start | bytes 278528 | tf_op jit(solution)/shard_map/all_to_all | solution.py:560
  38.2 8.3 %all-to-all-start.1 = ((f32[8,8,256]{2,1,0:T(8,128)}), f32[8,8,256]{2,1,0:T(8,128)S(1)}, u32[]{:S(2)}, u32[]{:S(2)}) async-start(f32[8,8,256]{2,1,0:T(8,128)} %get-tuple-element.11), calls=%async_computation.1 | async-start | bytes 131072 | tf_op jit(solution)/shard_map/all_to_all | solution.py:565
  49.7 4.6 %collective-permute-start.1 = (f32[32,48]{1,0:T(8,128)S(1)}, f32[32,48]{1,0:T(8,128)S(1)}, u32[]{:S(2)}, u32[]{:S(2)}) collective-permute-start(f32[32,48]{1,0:T(8,128)S(1)} %get-tuple-element.18), channel_id=1, source_target_pairs={{0,2},{1,3},{2,0},{3,1},{4,6},{5,7},{6,4},{7,5},{8,10},{9,11},{10,... | collective-permute-start | bytes 18440 | tf_op jit(solution)/shard_map/ppermute | solution.py:536
  52.3 5.5 %collective-permute-start.2 = (f32[32,48]{1,0:T(8,128)S(1)}, f32[32,48]{1,0:T(8,128)S(1)}, u32[]{:S(2)}, u32[]{:S(2)}) collective-permute-start(f32[32,48]{1,0:T(8,128)S(1)} %get-tuple-element.18), channel_id=1, source_target_pairs={{0,3},{1,2},{2,1},{3,0},{4,7},{5,6},{6,5},{7,4},{8,11},{9,10},{10,... | collective-permute-start | bytes 18440 | tf_op jit(solution)/shard_map/ppermute | solution.py:536
  53.6 4.2 %collective-permute-start = (f32[32,48]{1,0:T(8,128)S(1)}, f32[32,48]{1,0:T(8,128)S(1)}, u32[]{:S(2)}, u32[]{:S(2)}) collective-permute-start(f32[32,48]{1,0:T(8,128)S(1)} %get-tuple-element.18), channel_id=1, source_target_pairs={{0,1},{1,0},{2,3},{3,2},{4,5},{5,4},{6,7},{7,6},{8,9},{9,8},{10,11... | collective-permute-start | bytes 18440 | tf_op jit(solution)/shard_map/ppermute | solution.py:536

commit v5 on v4

--- a/solution.py
+++ b/solution.py
@@ -12,6 +12,8 @@
 LANES = 128
 BLOCK = 256
 CHUNKS = 8
+TABLE_PAD = 8
+NET_SPLIT = 4
 DEPTH = 4
 
 distill_weight = 50.0
@@ -201,7 +203,7 @@
         base = grid_ref[:, pl.ds(c0, span)]
         across = grid_ref[:, pl.ds(c0 + plane, span)]
         rows = jnp.concatenate([base, base, across, across], axis=0).T.astype(F32)
-        table[pl.ds(c0, span), :] = jnp.where(
+        table[pl.ds(c0 + TABLE_PAD, span), :] = jnp.where(
             upper, jnp.concatenate([rows[GR:], carry], axis=0), rows
         )
         return rows[:GR]
@@ -215,9 +217,9 @@
 
 
 def forward_kernel(
-    cap, idx_ref, grid_hbm, arrived_ref, fine_in_ref, prop_in_ref, mid_ref, fine_out_ref,
+    cap, idx_hbm, grid_hbm, arrived_ref, fine_in_ref, prop_in_ref, mid_ref, fine_out_ref,
     prop_out_ref, saved_ref, dense_ref, summary_ref,
-    table, grid_ref, grid_sem, rows, eye, feats, weights, spacing, first, head, fine_logit, prop_logit,
+    idx_ref, idx_sem, table, grid_ref, grid_sem, rows, feats, hidden_rows, weights, spacing, first, head, fine_logit, prop_logit,
 ):
     step = pl.program_id(0)
     parts = arrived_ref.shape[0]
@@ -229,15 +231,20 @@
 
     def gather(row, block, pair):
         start = row * width
-        for u in range(BLOCK):
-            k = idx_ref.at[pl.ds(block * BLOCK + u, idx_ref.shape[0] - width + 1)][start]
-            pair[2 * u : 2 * u + 2, :] = table[pl.ds(k, 2), :]
+        sub = lax.broadcasted_iota(jnp.int32, (8, LANES), 0)
+        for u in range(0, BLOCK, 4):
+            merged = None
+            for e in range(4):
+                at = pl.ds(block * BLOCK + u + e, idx_ref.shape[0] - width + 1)
+                k = idx_ref.at[at][start]
+                loaded = table[pl.ds(k + (TABLE_PAD - 2 * e), 8), :]
+                merged = loaded if merged is None else jnp.where(sub < 2 * e, merged, loaded)
+            pair[2 * u : 2 * u + 8, :] = merged
 
     def interpolate(block, pair, slot):
         near = pair[pl.ds(0, BLOCK, stride=2), :].astype(BF16)
         far = pair[pl.ds(1, BLOCK, stride=2), :].astype(BF16)
-        unit = jnp.concatenate([eye[0], eye[1]], axis=1)
-        t = dot_nt(unit, jnp.concatenate([near, far], axis=1))
+        t = jnp.concatenate([near, far], axis=1).T.astype(F32)
         at = slice(block * BLOCK, (block + 1) * BLOCK)
         total = jnp.zeros((features, BLOCK), F32)
         for corner in range(8):
@@ -246,28 +253,38 @@
             total = total + t[place * features : (place + 1) * features] * w
         feats[slot, :, at] = total.astype(BF16)
 
-    def networks(row, slot):
-        feat = feats[slot]
-        both = jnp.maximum(dot(first[...], feat), 0.0).astype(BF16)
-        h = both[:hidden]
-        ph = both[hidden:]
-        for layer in range(mid_ref.shape[0]):
-            h = jnp.maximum(dot(mid_ref[layer], h), 0.0).astype(BF16)
-        logits = dot(head[...], jnp.concatenate([h, ph], axis=0))
-        fine_logit[pl.ds(row, 1), :] = logits[0:1]
-        prop_logit[pl.ds(row, 1), :] = logits[1:2]
-        saved_ref[:features, :] = feat
-        saved_ref[features:, :] = ph
+    layers = mid_ref.shape[0]
+
+    def stage(row, slot, layer, lanes):
+        if layer == 0:
+            feat = feats[slot, :, lanes]
+            saved_ref[:features, lanes] = feat
+            both = jnp.maximum(dot(first[...], feat), 0.0).astype(BF16)
+            hidden_rows[:, lanes] = both
+            saved_ref[features:, lanes] = both[hidden:]
+        elif layer <= layers:
+            h = dot(mid_ref[layer - 1], hidden_rows[:hidden, lanes])
+            hidden_rows[:hidden, lanes] = jnp.maximum(h, 0.0).astype(BF16)
+        else:
+            logits = dot(head[...], hidden_rows[:, lanes])
+            fine_logit[pl.ds(row, 1), lanes] = logits[0:1]
+            prop_logit[pl.ds(row, 1), lanes] = logits[1:2]
+
+    def stages(row, slot):
+        parts_of = NET_SPLIT
+        size = width // parts_of
+        return [
+            functools.partial(stage, row, slot, layer, slice(h * size, (h + 1) * size))
+            for layer in range(layers + 2)
+            for h in range(parts_of)
+        ]
 
     @pl.when(step == 0)
     def _():
+        fetch_idx = pltpu.make_async_copy(idx_hbm, idx_ref, idx_sem)
+        fetch_idx.start()
         for c in reversed(range(CHUNKS)):
             fetch_grid(grid_hbm, grid_ref, grid_sem, c).start()
-        down = lax.broadcasted_iota(jnp.int32, (BLOCK, BLOCK), 0)
-        across = lax.broadcasted_iota(jnp.int32, (BLOCK, BLOCK), 1)
-        same = (down == across).astype(BF16)
-        eye[0] = same[:, :LANES]
-        eye[1] = same[:, LANES:]
         feats[...] = jnp.zeros(feats.shape, BF16)
         whole = [arrived_ref[q, :, :width].astype(F32) for q in range(parts)]
         g = [stack_rows(whole, j) for j in range(4)]
@@ -285,22 +302,26 @@
             w = [x if bit else 1.0 - x for x, bit in zip(g, bits)]
             weights[corner] = w[0] * w[1] * w[2]
         build_table(grid_hbm, grid_ref, grid_sem, table)
+        fetch_idx.wait()
         gather(0, 0, rows.at[0])
 
     @pl.when(step < parts)
     def _():
-        networks(jnp.maximum(step - 1, 0), (step + 1) % 2)
+        todo = stages(jnp.maximum(step - 1, 0), (step + 1) % 2)
         for j in range(blocks):
+            for run in todo[j * len(todo) // blocks : (j + 1) * len(todo) // blocks]:
+                run()
+            interpolate(j, rows.at[j % DEPTH], step % 2)
             ahead = rows.at[(j + 1) % DEPTH]
             if j + 1 < blocks:
                 gather(step, j + 1, ahead)
             else:
                 gather(jnp.minimum(step + 1, parts - 1), 0, ahead)
-            interpolate(j, rows.at[j % DEPTH], step % 2)
 
     @pl.when(step == parts)
     def _():
-        networks(parts - 1, (parts - 1) % 2)
+        for run in stages(parts - 1, (parts - 1) % 2):
+            run()
         space = pieces_of(spacing[...])
         results = []
         for k, ref in enumerate((prop_logit, fine_logit)):
@@ -351,7 +372,7 @@
             jax.ShapeDtypeStruct((parts, parts, stat_lanes), F32),
         ),
         in_specs=[
-            pl.BlockSpec(memory_space=pltpu.SMEM),
+            pl.BlockSpec(memory_space=pltpu.HBM),
             pl.BlockSpec(memory_space=pltpu.HBM),
         ]
         + [whole(x.shape) for x in small],
@@ -361,12 +382,14 @@
             whole((parts, parts, stat_lanes)),
         ),
         scratch_shapes=[
-            pltpu.VMEM((total, LANES), F32),
+            pltpu.SMEM(cells.shape, jnp.int32),
+            pltpu.SemaphoreType.DMA,
+            pltpu.VMEM((total + 2 * TABLE_PAD, LANES), F32),
             pltpu.VMEM((features, total), BF16),
             pltpu.SemaphoreType.DMA((CHUNKS,)),
             pltpu.VMEM((DEPTH, 2 * BLOCK, LANES), F32),
-            pltpu.VMEM((2, BLOCK, LANES), BF16),
             pltpu.VMEM((2, features, width), BF16),
+            pltpu.VMEM((hidden + prop_hidden, width), BF16),
             pltpu.VMEM((8, parts, width), F32),
             pltpu.VMEM((parts, width), F32),
             pltpu.VMEM((hidden + prop_hidden, features), BF16),
@@ -376,7 +399,7 @@
         ],
         compiler_params=pltpu.CompilerParams(vmem_limit_bytes=(32 + parts // 2) * 1024 * 1024),
         name="forward",
-    )(cells, in_hbm(grid), arrived, *[in_hbm(x) for x in small[1:]])
+    )(in_hbm(cells), in_hbm(grid), arrived, *[in_hbm(x) for x in small[1:]])
 
 
 def backward_kernel(

time: 59.4 us -> 54.7 us (0.921)
  Pallas kernels: 30.5 us -> 25.8 us
  local copies, waits for them, and re-layouts: 2.04 us -> 2.67 us
  waiting for transfers between devices: 13 us -> 12.4 us
    pallas_call x1, Pallas kernels: 25.1 us -> 20.3 us  [forward(): pl.pallas_call(functools.partial(forward_kernel, cap), grid=(parts + 1,),...]
    unnamed x3, local copies, waits for them, and re-layouts: 0.86 us -> 1.48 us
    all_to_all x1, waiting for transfers between devices: 4.73 us -> 4.11 us  [on_device(): lax.all_to_all(outgoing, 'dom', split_axis=0, concat_axis=0, tiled=True)]
  transfers between devices with their start and end apart: 5 -> 5, of which waited for: 4 -> 4; matrix products, arithmetic and copies ran while one was open for 1% -> 3% of each run, Pallas kernels for 1% -> 1%
where the time goes in v5:
time: 54.7 us; the launch traced here: 54.3 us
  Pallas kernels  25.8 us (47%)
  starting transfers between devices  12.7 us (23%)
  waiting for transfers between devices  12.4 us (23%)
  local copies, waits for them, and re-layouts  2.67 us (5%)
  between operations  0.68 us (1%)
    pallas_call x1, Pallas kernels, forward(): pl.pallas_call(functools.partial(forward_kernel, cap), grid=(parts + 1,),...  20.3 us
    all_to_all x1, starting transfers between devices, on_device(): lax.all_to_all(outgoing, 'dom', split_axis=0, concat_axis=0, tiled=True)  5.2 us
    all_to_all x1, waiting for transfers between devices, on_device(): lax.all_to_all(summary, 'dom', split_axis=0, concat_axis=0, tiled=True)  4.29 us
    ppermute x3, starting transfers between devices, sum_replicas(): lax.ppermute(x, 'rep', [(i, i ^ s) for i in range(count)])  4.16 us
    all_to_all x1, waiting for transfers between devices, on_device(): lax.all_to_all(outgoing, 'dom', split_axis=0, concat_axis=0, tiled=True)  4.11 us
    ppermute x3, waiting for transfers between devices, sum_replicas(): lax.ppermute(x, 'rep', [(i, i ^ s) for i in range(count)])  3.96 us
    all_to_all x1, starting transfers between devices, on_device(): lax.all_to_all(summary, 'dom', split_axis=0, concat_axis=0, tiled=True)  3.36 us
    pallas_call x1, Pallas kernels, backward(): pl.pallas_call(functools.partial(backward_kernel, cap), out_shape=(jax.Sh...  3.1 us
  transfers between devices with their start and end apart: 5, of which 4 were waited for; matrix products, arithmetic and copies ran while one was open for 3% of the time, Pallas kernels for 1%

profile of v5, /device:TPU:0, one launch (start us, length us, event | category | flops | bytes accessed | tf_op | source)
XLA Modules:
  0.0 54.3 jit_solution(10325689193261182753)
XLA Ops:
  0.6 0.0 copy-start
  0.6 1.8 %pack.1 = bf16[8,4,2176]{2,1,0:T(4,128)(2,1)} custom-call(bf16[4,8,2048]{2,1,0:T(8,128)(2,1)} %bitcast.18, s32[8,32]{1,0:T(8,128)} %bitcast.22, s32[8,32]{1,0:T(8,128)} %bitcast.23, s32[8]{0:T(128)} %bitcast.25), custom_call_target="tpu_custom_call" | custom-call | tf_op jit(solution)/shard_map/pack/pallas_call | solution.py:86
  2.4 5.2 %all-to-all-start = ((bf16[8,4,2176]{2,1,0:T(4,128)(2,1)}), bf16[8,4,2176]{2,1,0:T(4,128)(2,1)S(1)}, u32[]{:S(2)}, u32[]{:S(2)}) async-start(bf16[8,4,2176]{2,1,0:T(4,128)(2,1)} %pack.1), calls=%async_computation | async-start | bytes 278528 | tf_op jit(solution)/shard_map/all_to_all | solution.py:583
  7.6 1.5 %copy.14 = s32[1,16,8,128]{3,1,2,0:T(8,128)} copy(s32[1,16,8,128]{3,2,1,0:T(8,128)} %bitcast.19) | data formatting | bytes 131072
  9.1 4.1 %all-to-all-done.arrived_ref = bf16[8,4,2176]{2,1,0:T(4,128)(2,1)S(1)} async-done(((bf16[8,4,2176]{2,1,0:T(4,128)(2,1)}), bf16[8,4,2176]{2,1,0:T(4,128)(2,1)S(1)}, u32[]{:S(2)}, u32[]{:S(2)}) %all-to-all-start) | async-done | bytes 139296 | tf_op jit(solution)/shard_map/all_to_all | solution.py:583
  13.2 20.3 %forward.1 = (bf16[48,16384]{1,0:T(8,128)(2,1)S(1)}, f32[4,8,2048]{2,1,0:T(8,128)S(1)}, f32[8,8,256]{2,1,0:T(8,128)}) custom-call(s32[16384]{0:T(1024)} %bitcast.17, bf16[32,32768]{1,0:T(8,128)(2,1)} %bitcast.16, bf16[8,4,2176]{2,1,0:T(4,128)(2,1)S(1)} %all-to-all-done.arrived_ref, bf16[32,64]{1,0:T(8,128)(2,1)} %bitcast.21, bf16[16,32]{1,0:T(8,128)(2,1)} %bitcast.24, ...), custom_call_target="tpu_custom_call" | custom-call | tf_op jit(solution)/shard_map/forward/pallas_call | solution.py:366
  33.5 3.4 %all-to-all-start.1 = ((f32[8,8,256]{2,1,0:T(8,128)}), f32[8,8,256]{2,1,0:T(8,128)S(1)}, u32[]{:S(2)}, u32[]{:S(2)}) async-start(f32[8,8,256]{2,1,0:T(8,128)} %get-tuple-element.11), calls=%async_computation.1 | async-start | bytes 131072 | tf_op jit(solution)/shard_map/all_to_all | solution.py:588
  36.9 0.6 %slot_marks.1 = (f32[8,256]{1,0:T(8,128)S(1)}, bf16[256,256]{1,0:T(8,128)(2,1)S(1)}, bf16[8,256,256]{2,1,0:T(8,128)(2,1)S(1)}) custom-call(s32[1]{0:T(128)} %bitcast.me_ref, bf16[8,4,2176]{2,1,0:T(4,128)(2,1)S(1)} %all-to-all-done.arrived_ref), custom_call_target="tpu_custom_call" | custom-call | flops 4194304 | bytes 4194304 | tf_op jit(solution)/shard_map/slot_marks/pallas_call | solution.py:129
  37.5 4.3 %all-to-all-done.1.stats_ref = f32[8,8,256]{2,1,0:T(8,128)S(1)} async-done(((f32[8,8,256]{2,1,0:T(8,128)}), f32[8,8,256]{2,1,0:T(8,128)S(1)}, u32[]{:S(2)}, u32[]{:S(2)}) %all-to-all-start.1) | async-done | bytes 65568 | tf_op jit(solution)/shard_map/all_to_all | solution.py:588
  41.8 0.0 copy-done
  41.8 3.1 %backward.1 = (f32[1,256]{1,0:T(1,128)}, f32[32,48]{1,0:T(8,128)S(1)}) custom-call(s32[1]{0:T(128)} %bitcast.me_ref, f32[8,8,256]{2,1,0:T(8,128)S(1)} %all-to-all-done.1.stats_ref, f32[8,256]{1,0:T(8,128)S(1)} %get-tuple-element.12.key_ref, bf16[256,256]{1,0:T(8,128)(2,1)S(1)} %get-tuple-element.13.hot_ref, f32[4,8,2048]{2,1,0:T(8,128)S(1)} %get-tuple-element.14.dense_ref, ...), custom_call_target="tpu_custom_call" | custom-call | tf_op jit(solution)/shard_map/backward/pallas_call | solution.py:540
  44.9 2.6 %collective-permute-start.1 = (f32[32,48]{1,0:T(8,128)S(1)}, f32[32,48]{1,0:T(8,128)S(1)}, u32[]{:S(2)}, u32[]{:S(2)}) collective-permute-start(f32[32,48]{1,0:T(8,128)S(1)} %get-tuple-element.18), channel_id=1, source_target_pairs={{0,2},{1,3},{2,0},{3,1},{4,6},{5,7},{6,4},{7,5},{8,10},{9,11},{10,... | collective-permute-start | bytes 18440 | tf_op jit(solution)/shard_map/ppermute | solution.py:559
  47.5 1.3 %collective-permute-start.2 = (f32[32,48]{1,0:T(8,128)S(1)}, f32[32,48]{1,0:T(8,128)S(1)}, u32[]{:S(2)}, u32[]{:S(2)}) collective-permute-start(f32[32,48]{1,0:T(8,128)S(1)} %get-tuple-element.18), channel_id=1, source_target_pairs={{0,3},{1,2},{2,1},{3,0},{4,7},{5,6},{6,5},{7,4},{8,11},{9,10},{10,... | collective-permute-start | bytes 18440 | tf_op jit(solution)/shard_map/ppermute | solution.py:559
  48.9 0.2 collective-permute-start
  49.1 0.5 collective-permute-done.1
  49.6 3.5 %collective-permute-done.2 = f32[32,48]{1,0:T(8,128)S(1)} collective-permute-done((f32[32,48]{1,0:T(8,128)S(1)}, f32[32,48]{1,0:T(8,128)S(1)}, u32[]{:S(2)}, u32[]{:S(2)}) %collective-permute-start.2) | collective-permute-done | bytes 6176 | tf_op jit(solution)/shard_map/ppermute | solution.py:559
  53.1 0.0 collective-permute-done
  53.1 0.6 %slice_bitcast_fusion = f32[1,16,32]{2,1,0:T(8,128)} fusion(f32[32,48]{1,0:T(8,128)S(1)} %add_add_fusion), kind=kLoop, calls=%fused_computation.1 | loop fusion | bytes 4096 | tf_op jit(solution)/shard_map/broadcast_in_dim | solution.py:595
  53.7 0.6 %slice.9 = f32[1,16]{1,0:T(1,128)} slice(f32[32,48]{1,0:T(8,128)S(1)} %add_add_fusion), slice={[16:17], [32:48]} | slice | bytes 128 | tf_op jit(solution)/shard_map/slice | solution.py:594
  (1 shorter events, 0.0 us)
Async XLA Ops:
  0.6 41.2 %copy-start = (bf16[1,16]{1,0:T(2,128)(2,1)S(1)}, bf16[1,16]{1,0:T(2,128)(2,1)}, u32[]{:S(2)}) copy-start(bf16[1,16]{1,0:T(2,128)(2,1)} %prop_out_ref.3) | copy-start | bytes 100
  2.4 10.8 %all-to-all-start = ((bf16[8,4,2176]{2,1,0:T(4,128)(2,1)}), bf16[8,4,2176]{2,1,0:T(4,128)(2,1)S(1)}, u32[]{:S(2)}, u32[]{:S(2)}) async-start(bf16[8,4,2176]{2,1,0:T(4,128)(2,1)} %pack.1), calls=%async_computation | async-start | bytes 278528 | tf_op jit(solution)/shard_map/all_to_all | solution.py:583
  33.5 8.3 %all-to-all-start.1 = ((f32[8,8,256]{2,1,0:T(8,128)}), f32[8,8,256]{2,1,0:T(8,128)S(1)}, u32[]{:S(2)}, u32[]{:S(2)}) async-start(f32[8,8,256]{2,1,0:T(8,128)} %get-tuple-element.11), calls=%async_computation.1 | async-start | bytes 131072 | tf_op jit(solution)/shard_map/all_to_all | solution.py:588
  44.9 4.6 %collective-permute-start.1 = (f32[32,48]{1,0:T(8,128)S(1)}, f32[32,48]{1,0:T(8,128)S(1)}, u32[]{:S(2)}, u32[]{:S(2)}) collective-permute-start(f32[32,48]{1,0:T(8,128)S(1)} %get-tuple-element.18), channel_id=1, source_target_pairs={{0,2},{1,3},{2,0},{3,1},{4,6},{5,7},{6,4},{7,5},{8,10},{9,11},{10,... | collective-permute-start | bytes 18440 | tf_op jit(solution)/shard_map/ppermute | solution.py:559
  47.5 5.5 %collective-permute-start.2 = (f32[32,48]{1,0:T(8,128)S(1)}, f32[32,48]{1,0:T(8,128)S(1)}, u32[]{:S(2)}, u32[]{:S(2)}) collective-permute-start(f32[32,48]{1,0:T(8,128)S(1)} %get-tuple-element.18), channel_id=1, source_target_pairs={{0,3},{1,2},{2,1},{3,0},{4,7},{5,6},{6,5},{7,4},{8,11},{9,10},{10,... | collective-permute-start | bytes 18440 | tf_op jit(solution)/shard_map/ppermute | solution.py:559
  48.9 4.2 %collective-permute-start = (f32[32,48]{1,0:T(8,128)S(1)}, f32[32,48]{1,0:T(8,128)S(1)}, u32[]{:S(2)}, u32[]{:S(2)}) collective-permute-start(f32[32,48]{1,0:T(8,128)S(1)} %get-tuple-element.18), channel_id=1, source_target_pairs={{0,1},{1,0},{2,3},{3,2},{4,5},{5,4},{6,7},{7,6},{8,9},{9,8},{10,11... | collective-permute-start | bytes 18440 | tf_op jit(solution)/shard_map/ppermute | solution.py:559

commit v6 on v5

--- a/solution.py
+++ b/solution.py
@@ -221,7 +221,6 @@
     prop_out_ref, saved_ref, dense_ref, summary_ref,
     idx_ref, idx_sem, table, grid_ref, grid_sem, rows, feats, hidden_rows, weights, spacing, first, head, fine_logit, prop_logit,
 ):
-    step = pl.program_id(0)
     parts = arrived_ref.shape[0]
     width = idx_ref.shape[0] // parts
     blocks = width // BLOCK
@@ -241,7 +240,7 @@
                 merged = loaded if merged is None else jnp.where(sub < 2 * e, merged, loaded)
             pair[2 * u : 2 * u + 8, :] = merged
 
-    def interpolate(block, pair, slot):
+    def interpolate(step, block, pair, slot):
         near = pair[pl.ds(0, BLOCK, stride=2), :].astype(BF16)
         far = pair[pl.ds(1, BLOCK, stride=2), :].astype(BF16)
         t = jnp.concatenate([near, far], axis=1).T.astype(F32)
@@ -258,10 +257,10 @@
     def stage(row, slot, layer, lanes):
         if layer == 0:
             feat = feats[slot, :, lanes]
-            saved_ref[:features, lanes] = feat
+            saved_ref[row, :features, lanes] = feat
             both = jnp.maximum(dot(first[...], feat), 0.0).astype(BF16)
             hidden_rows[:, lanes] = both
-            saved_ref[features:, lanes] = both[hidden:]
+            saved_ref[row, features:, lanes] = both[hidden:]
         elif layer <= layers:
             h = dot(mid_ref[layer - 1], hidden_rows[:hidden, lanes])
             hidden_rows[:hidden, lanes] = jnp.maximum(h, 0.0).astype(BF16)
@@ -279,78 +278,76 @@
             for h in range(parts_of)
         ]
 
-    @pl.when(step == 0)
-    def _():
-        fetch_idx = pltpu.make_async_copy(idx_hbm, idx_ref, idx_sem)
-        fetch_idx.start()
-        for c in reversed(range(CHUNKS)):
-            fetch_grid(grid_hbm, grid_ref, grid_sem, c).start()
-        feats[...] = jnp.zeros(feats.shape, BF16)
-        whole = [arrived_ref[q, :, :width].astype(F32) for q in range(parts)]
-        g = [stack_rows(whole, j) for j in range(4)]
-        spacing[...] = g[3]
-        first[:hidden, :] = fine_in_ref[...].astype(F32).T.astype(BF16)
-        first[hidden:, :] = prop_in_ref[...]
-        zero_f = jnp.zeros((1, prop_hidden), F32)
-        zero_p = jnp.zeros((1, hidden), F32)
-        top = jnp.concatenate([fine_out_ref[...].astype(F32), zero_f], axis=1)
-        low = jnp.concatenate([zero_p, prop_out_ref[...].astype(F32)], axis=1)
-        rest = jnp.zeros((6, hidden + prop_hidden), F32)
-        head[...] = jnp.concatenate([top, low, rest], axis=0).astype(BF16)
-        for corner in range(8):
-            bits = (corner // 4, corner // 2 % 2, corner % 2)
-            w = [x if bit else 1.0 - x for x, bit in zip(g, bits)]
-            weights[corner] = w[0] * w[1] * w[2]
-        build_table(grid_hbm, grid_ref, grid_sem, table)
-        fetch_idx.wait()
-        gather(0, 0, rows.at[0])
-
-    @pl.when(step < parts)
-    def _():
+    fetch_idx = pltpu.make_async_copy(idx_hbm, idx_ref, idx_sem)
+    fetch_idx.start()
+    for c in reversed(range(CHUNKS)):
+        fetch_grid(grid_hbm, grid_ref, grid_sem, c).start()
+    feats[...] = jnp.zeros(feats.shape, BF16)
+    whole = [arrived_ref[q, :, :width].astype(F32) for q in range(parts)]
+    g = [stack_rows(whole, j) for j in range(4)]
+    spacing[...] = g[3]
+    first[:hidden, :] = fine_in_ref[...].astype(F32).T.astype(BF16)
+    first[hidden:, :] = prop_in_ref[...]
+    zero_f = jnp.zeros((1, prop_hidden), F32)
+    zero_p = jnp.zeros((1, hidden), F32)
+    top = jnp.concatenate([fine_out_ref[...].astype(F32), zero_f], axis=1)
+    low = jnp.concatenate([zero_p, prop_out_ref[...].astype(F32)], axis=1)
+    rest = jnp.zeros((6, hidden + prop_hidden), F32)
+    head[...] = jnp.concatenate([top, low, rest], axis=0).astype(BF16)
+    for corner in range(8):
+        bits = (corner // 4, corner // 2 % 2, corner % 2)
+        w = [x if bit else 1.0 - x for x, bit in zip(g, bits)]
+        weights[corner] = w[0] * w[1] * w[2]
+    build_table(grid_hbm, grid_ref, grid_sem, table)
+    fetch_idx.wait()
+    gather(0, 0, rows.at[0])
+
+    def turn(step, carry):
         todo = stages(jnp.maximum(step - 1, 0), (step + 1) % 2)
         for j in range(blocks):
             for run in todo[j * len(todo) // blocks : (j + 1) * len(todo) // blocks]:
                 run()
-            interpolate(j, rows.at[j % DEPTH], step % 2)
+            interpolate(step, j, rows.at[j % DEPTH], step % 2)
             ahead = rows.at[(j + 1) % DEPTH]
             if j + 1 < blocks:
                 gather(step, j + 1, ahead)
             else:
                 gather(jnp.minimum(step + 1, parts - 1), 0, ahead)
-
-    @pl.when(step == parts)
-    def _():
-        for run in stages(parts - 1, (parts - 1) % 2):
-            run()
-        space = pieces_of(spacing[...])
-        results = []
-        for k, ref in enumerate((prop_logit, fine_logit)):
-            logit = pieces_of(ref[...])
-            optical = [softplus(x) * s for x, s in zip(logit, space)]
-            depth, whole = running(optical, cap)
-            early = [jnp.exp(o - d) for o, d in zip(optical, depth)]
-            absorb = [e - jnp.exp(-d) for e, d in zip(early, depth)]
-            results.append((absorb, whole))
-            if k == 0:
-                slope = [s * jax.nn.sigmoid(x) for x, s in zip(logit, space)]
-                dense_ref[0] = jnp.concatenate(early, axis=1)
-                dense_ref[3] = jnp.concatenate(slope, axis=1)
-        (a, log_prop), (b, log_fine) = results
-        dense_ref[1] = jnp.concatenate(a, axis=1)
-        dense_ref[2] = jnp.concatenate(b, axis=1)
-        sums = [lane_fold(sum(x * y for x, y in zip(s, t)), cap) for s, t in ((a, a), (a, b), (b, b))]
-        stats = [-log_prop, -log_fine] + sums
-        per = LANES // cap
-        group = lax.broadcasted_iota(jnp.int32, stats[0].shape, 1) // cap
-        slabs = []
-        for s in range(-(-len(stats) // per)):
-            slab = jnp.zeros_like(stats[0])
-            for k, x in enumerate(stats[s * per : (s + 1) * per]):
-                slab = jnp.where(group == k, x, slab)
-            slabs.append(slab)
-        summary = jnp.concatenate(slabs, axis=1)
-        for p in range(parts):
-            summary_ref[p] = summary
+        return carry
+
+    lax.fori_loop(0, parts, turn, 0)
+
+    for run in stages(parts - 1, (parts - 1) % 2):
+        run()
+    space = pieces_of(spacing[...])
+    results = []
+    for k, ref in enumerate((prop_logit, fine_logit)):
+        logit = pieces_of(ref[...])
+        optical = [softplus(x) * s for x, s in zip(logit, space)]
+        depth, whole = running(optical, cap)
+        early = [jnp.exp(o - d) for o, d in zip(optical, depth)]
+        absorb = [e - jnp.exp(-d) for e, d in zip(early, depth)]
+        results.append((absorb, whole))
+        if k == 0:
+            slope = [s * jax.nn.sigmoid(x) for x, s in zip(logit, space)]
+            dense_ref[0] = jnp.concatenate(early, axis=1)
+            dense_ref[3] = jnp.concatenate(slope, axis=1)
+    (a, log_prop), (b, log_fine) = results
+    dense_ref[1] = jnp.concatenate(a, axis=1)
+    dense_ref[2] = jnp.concatenate(b, axis=1)
+    sums = [lane_fold(sum(x * y for x, y in zip(s, t)), cap) for s, t in ((a, a), (a, b), (b, b))]
+    stats = [-log_prop, -log_fine] + sums
+    per = LANES // cap
+    group = lax.broadcasted_iota(jnp.int32, stats[0].shape, 1) // cap
+    slabs = []
+    for s in range(-(-len(stats) // per)):
+        slab = jnp.zeros_like(stats[0])
+        for k, x in enumerate(stats[s * per : (s + 1) * per]):
+            slab = jnp.where(group == k, x, slab)
+        slabs.append(slab)
+    summary = jnp.concatenate(slabs, axis=1)
+    for p in range(parts):
+        summary_ref[p] = summary
 
 
 def forward(cells, grid, arrived, fine_in, prop_in, mid, fine_out, prop_out, cap):
@@ -361,13 +358,12 @@
     prop_hidden = prop_in.shape[0]
     kept = features + prop_hidden
     stat_lanes = -(-5 // (LANES // cap)) * LANES
-    whole = lambda shape: pl.BlockSpec(shape, lambda q: (0,) * len(shape))
+    vmem = pl.BlockSpec(memory_space=pltpu.VMEM)
     small = (arrived, fine_in, prop_in, mid, fine_out, prop_out)
     return pl.pallas_call(
         functools.partial(forward_kernel, cap),
-        grid=(parts + 1,),
         out_shape=(
-            jax.ShapeDtypeStruct((kept, parts * width), BF16),
+            jax.ShapeDtypeStruct((parts, kept, width), BF16),
             jax.ShapeDtypeStruct((4, parts, width), F32),
             jax.ShapeDtypeStruct((parts, parts, stat_lanes), F32),
         ),
@@ -375,12 +371,8 @@
             pl.BlockSpec(memory_space=pltpu.HBM),
             pl.BlockSpec(memory_space=pltpu.HBM),
         ]
-        + [whole(x.shape) for x in small],
-        out_specs=(
-            pl.BlockSpec((kept, width), lambda q: (0, jnp.maximum(q - 1, 0))),
-            whole((4, parts, width)),
-            whole((parts, parts, stat_lanes)),
-        ),
+        + [vmem] * len(small),
+        out_specs=(vmem,) * 3,
         scratch_shapes=[
             pltpu.SMEM(cells.shape, jnp.int32),
             pltpu.SemaphoreType.DMA,
@@ -510,7 +502,7 @@
         for d, e, r, s in zip(d_absorb, early, back, slope)
     ]
     slope_ref[...] = jnp.concatenate(logit_grad, axis=1)
-    features = saved_ref.shape[0] - prop_hidden
+    features = saved_ref.shape[1] - prop_hidden
     wide = jnp.broadcast_to(prop_out_ref[...].astype(F32), (prop_hidden, prop_hidden))
     same = lax.broadcasted_iota(jnp.int32, wide.shape, 0) == lax.broadcasted_iota(
         jnp.int32, wide.shape, 1
@@ -519,15 +511,18 @@
     first_row = lax.broadcasted_iota(jnp.int32, (prop_hidden, width), 0) == 0
 
     def accumulate(q, total):
-        at = pl.ds(pl.multiple_of(q * width, width), width)
         row = slope_ref[pl.ds(q, 1), :]
-        kept = saved_ref[:, at]
+        kept = saved_ref[q]
         hidden_grad = jnp.where(kept[features:].astype(F32) > 0, out_col * row, 0.0).astype(BF16)
         alone = jnp.where(first_row, row, 0.0).astype(BF16)
         return total + dot_nt(jnp.concatenate([hidden_grad, alone], axis=0), kept)
 
-    total = jnp.zeros((2 * prop_hidden, saved_ref.shape[0]), F32)
-    total = lax.fori_loop(0, parts, accumulate, total)
+    total = jnp.zeros((2 * prop_hidden, saved_ref.shape[1]), F32)
+    if masks:
+        for q in range(parts):
+            total = accumulate(q, total)
+    else:
+        total = lax.fori_loop(0, parts, accumulate, total)
     grad_ref[...] = total
 
 
@@ -541,7 +536,7 @@
         functools.partial(backward_kernel, cap),
         out_shape=(
             jax.ShapeDtypeStruct((1, RAY_DEV), F32),
-            jax.ShapeDtypeStruct((2 * prop_hidden, saved.shape[0]), F32),
+            jax.ShapeDtypeStruct((2 * prop_hidden, saved.shape[1]), F32),
         ),
         in_specs=[pl.BlockSpec(memory_space=pltpu.SMEM)] + [vmem] * (6 + len(masks)),
         out_specs=(vmem, vmem),

time: 54.7 us -> 53.5 us (0.978)
  Pallas kernels: 25.8 us -> 24.6 us
    pallas_call x1, Pallas kernels: 3.1 us -> 2.38 us  [backward(): pl.pallas_call(functools.partial(backward_kernel, cap), out_shape=(jax.Sh...]
where the time goes in v6:
time: 53.5 us; the launch traced here: 53.1 us
  Pallas kernels  24.6 us (46%)
  starting transfers between devices  12.8 us (24%)
  waiting for transfers between devices  12.3 us (23%)
  local copies, waits for them, and re-layouts  2.67 us (5%)
  between operations  0.68 us (1%)
    pallas_call x1, Pallas kernels, forward(): pl.pallas_call(functools.partial(forward_kernel, cap), out_shape=(jax.Sha...  19.9 us
    all_to_all x1, starting transfers between devices, on_device(): lax.all_to_all(outgoing, 'dom', split_axis=0, concat_axis=0, tiled=True)  5.2 us
    all_to_all x1, waiting for transfers between devices, on_device(): lax.all_to_all(summary, 'dom', split_axis=0, concat_axis=0, tiled=True)  4.29 us
    ppermute x3, starting transfers between devices, sum_replicas(): lax.ppermute(x, 'rep', [(i, i ^ s) for i in range(count)])  4.2 us
    all_to_all x1, waiting for transfers between devices, on_device(): lax.all_to_all(outgoing, 'dom', split_axis=0, concat_axis=0, tiled=True)  4.11 us
    ppermute x3, waiting for transfers between devices, sum_replicas(): lax.ppermute(x, 'rep', [(i, i ^ s) for i in range(count)])  3.94 us
    all_to_all x1, starting transfers between devices, on_device(): lax.all_to_all(summary, 'dom', split_axis=0, concat_axis=0, tiled=True)  3.36 us
    pallas_call x1, Pallas kernels, backward(): pl.pallas_call(functools.partial(backward_kernel, cap), out_shape=(jax.Sh...  2.38 us
  transfers between devices with their start and end apart: 5, of which 4 were waited for; matrix products, arithmetic and copies ran while one was open for 3% of the time, Pallas kernels for 1%

profile of v6, /device:TPU:0, one launch (start us, length us, event | category | flops | bytes accessed | tf_op | source)
XLA Modules:
  0.0 53.1 jit_solution(972091215713274618)
XLA Ops:
  0.6 0.0 copy-start
  0.6 1.8 %pack.1 = bf16[8,4,2176]{2,1,0:T(4,128)(2,1)} custom-call(bf16[4,8,2048]{2,1,0:T(8,128)(2,1)} %bitcast.18, s32[8,32]{1,0:T(8,128)} %bitcast.22, s32[8,32]{1,0:T(8,128)} %bitcast.23, s32[8]{0:T(128)} %bitcast.25), custom_call_target="tpu_custom_call" | custom-call | tf_op jit(solution)/shard_map/pack/pallas_call | solution.py:86
  2.4 5.2 %all-to-all-start = ((bf16[8,4,2176]{2,1,0:T(4,128)(2,1)}), bf16[8,4,2176]{2,1,0:T(4,128)(2,1)S(1)}, u32[]{:S(2)}, u32[]{:S(2)}) async-start(bf16[8,4,2176]{2,1,0:T(4,128)(2,1)} %pack.1), calls=%async_computation | async-start | bytes 278528 | tf_op jit(solution)/shard_map/all_to_all | solution.py:578
  7.6 1.5 %copy.14 = s32[1,16,8,128]{3,1,2,0:T(8,128)} copy(s32[1,16,8,128]{3,2,1,0:T(8,128)} %bitcast.19) | data formatting | bytes 131072
  9.1 4.1 %all-to-all-done.arrived_ref = bf16[8,4,2176]{2,1,0:T(4,128)(2,1)S(1)} async-done(((bf16[8,4,2176]{2,1,0:T(4,128)(2,1)}), bf16[8,4,2176]{2,1,0:T(4,128)(2,1)S(1)}, u32[]{:S(2)}, u32[]{:S(2)}) %all-to-all-start) | async-done | bytes 139296 | tf_op jit(solution)/shard_map/all_to_all | solution.py:578
  13.2 19.9 %forward.1 = (bf16[8,48,2048]{2,1,0:T(8,128)(2,1)S(1)}, f32[4,8,2048]{2,1,0:T(8,128)S(1)}, f32[8,8,256]{2,1,0:T(8,128)}) custom-call(s32[16384]{0:T(1024)} %bitcast.17, bf16[32,32768]{1,0:T(8,128)(2,1)} %bitcast.16, bf16[8,4,2176]{2,1,0:T(4,128)(2,1)S(1)} %all-to-all-done.arrived_ref, bf16[32,64]{1,0:T(8,128)(2,1)} %bitcast.21, bf16[16,32]{1,0:T(8,128)(2,1)} %bitcast.24, ...), custom_call_target="tpu_custom_call" | custom-call | tf_op jit(solution)/shard_map/forward/pallas_call | solution.py:363
  33.1 3.4 %all-to-all-start.1 = ((f32[8,8,256]{2,1,0:T(8,128)}), f32[8,8,256]{2,1,0:T(8,128)S(1)}, u32[]{:S(2)}, u32[]{:S(2)}) async-start(f32[8,8,256]{2,1,0:T(8,128)} %get-tuple-element.11), calls=%async_computation.1 | async-start | bytes 131072 | tf_op jit(solution)/shard_map/all_to_all | solution.py:583
  36.4 0.6 %slot_marks.1 = (f32[8,256]{1,0:T(8,128)S(1)}, bf16[256,256]{1,0:T(8,128)(2,1)S(1)}, bf16[8,256,256]{2,1,0:T(8,128)(2,1)S(1)}) custom-call(s32[1]{0:T(128)} %bitcast.me_ref, bf16[8,4,2176]{2,1,0:T(4,128)(2,1)S(1)} %all-to-all-done.arrived_ref), custom_call_target="tpu_custom_call" | custom-call | flops 4194304 | bytes 4194304 | tf_op jit(solution)/shard_map/slot_marks/pallas_call | solution.py:129
  37.1 4.3 %all-to-all-done.1.stats_ref = f32[8,8,256]{2,1,0:T(8,128)S(1)} async-done(((f32[8,8,256]{2,1,0:T(8,128)}), f32[8,8,256]{2,1,0:T(8,128)S(1)}, u32[]{:S(2)}, u32[]{:S(2)}) %all-to-all-start.1) | async-done | bytes 65568 | tf_op jit(solution)/shard_map/all_to_all | solution.py:583
  41.4 0.0 copy-done
  41.4 2.4 %backward.1 = (f32[1,256]{1,0:T(1,128)}, f32[32,48]{1,0:T(8,128)S(1)}) custom-call(s32[1]{0:T(128)} %bitcast.me_ref, f32[8,8,256]{2,1,0:T(8,128)S(1)} %all-to-all-done.1.stats_ref, f32[8,256]{1,0:T(8,128)S(1)} %get-tuple-element.12.key_ref, bf16[256,256]{1,0:T(8,128)(2,1)S(1)} %get-tuple-element.13.hot_ref, f32[4,8,2048]{2,1,0:T(8,128)S(1)} %get-tuple-element.14.dense_ref, ...), custom_call_target="tpu_custom_call" | custom-call | tf_op jit(solution)/shard_map/backward/pallas_call | solution.py:535
  43.8 2.6 %collective-permute-start.1 = (f32[32,48]{1,0:T(8,128)S(1)}, f32[32,48]{1,0:T(8,128)S(1)}, u32[]{:S(2)}, u32[]{:S(2)}) collective-permute-start(f32[32,48]{1,0:T(8,128)S(1)} %get-tuple-element.18), channel_id=1, source_target_pairs={{0,2},{1,3},{2,0},{3,1},{4,6},{5,7},{6,4},{7,5},{8,10},{9,11},{10,... | collective-permute-start | bytes 18440 | tf_op jit(solution)/shard_map/ppermute | solution.py:554
  46.4 1.4 %collective-permute-start.2 = (f32[32,48]{1,0:T(8,128)S(1)}, f32[32,48]{1,0:T(8,128)S(1)}, u32[]{:S(2)}, u32[]{:S(2)}) collective-permute-start(f32[32,48]{1,0:T(8,128)S(1)} %get-tuple-element.18), channel_id=1, source_target_pairs={{0,3},{1,2},{2,1},{3,0},{4,7},{5,6},{6,5},{7,4},{8,11},{9,10},{10,... | collective-permute-start | bytes 18440 | tf_op jit(solution)/shard_map/ppermute | solution.py:554
  47.7 0.2 collective-permute-start
  48.0 0.4 collective-permute-done.1
  48.4 3.5 %collective-permute-done.2 = f32[32,48]{1,0:T(8,128)S(1)} collective-permute-done((f32[32,48]{1,0:T(8,128)S(1)}, f32[32,48]{1,0:T(8,128)S(1)}, u32[]{:S(2)}, u32[]{:S(2)}) %collective-permute-start.2) | collective-permute-done | bytes 6176 | tf_op jit(solution)/shard_map/ppermute | solution.py:554
  51.9 0.0 collective-permute-done
  51.9 0.6 %slice_bitcast_fusion = f32[1,16,32]{2,1,0:T(8,128)} fusion(f32[32,48]{1,0:T(8,128)S(1)} %add_add_fusion), kind=kLoop, calls=%fused_computation.1 | loop fusion | bytes 4096 | tf_op jit(solution)/shard_map/broadcast_in_dim | solution.py:590
  52.5 0.6 %slice.9 = f32[1,16]{1,0:T(1,128)} slice(f32[32,48]{1,0:T(8,128)S(1)} %add_add_fusion), slice={[16:17], [32:48]} | slice | bytes 128 | tf_op jit(solution)/shard_map/slice | solution.py:589
  (1 shorter events, 0.0 us)
Async XLA Ops:
  0.6 40.7 %copy-start = (bf16[1,16]{1,0:T(2,128)(2,1)S(1)}, bf16[1,16]{1,0:T(2,128)(2,1)}, u32[]{:S(2)}) copy-start(bf16[1,16]{1,0:T(2,128)(2,1)} %prop_out_ref.3) | copy-start | bytes 100
  2.4 10.8 %all-to-all-start = ((bf16[8,4,2176]{2,1,0:T(4,128)(2,1)}), bf16[8,4,2176]{2,1,0:T(4,128)(2,1)S(1)}, u32[]{:S(2)}, u32[]{:S(2)}) async-start(bf16[8,4,2176]{2,1,0:T(4,128)(2,1)} %pack.1), calls=%async_computation | async-start | bytes 278528 | tf_op jit(solution)/shard_map/all_to_all | solution.py:578
  33.1 8.3 %all-to-all-start.1 = ((f32[8,8,256]{2,1,0:T(8,128)}), f32[8,8,256]{2,1,0:T(8,128)S(1)}, u32[]{:S(2)}, u32[]{:S(2)}) async-start(f32[8,8,256]{2,1,0:T(8,128)} %get-tuple-element.11), calls=%async_computation.1 | async-start | bytes 131072 | tf_op jit(solution)/shard_map/all_to_all | solution.py:583
  43.8 4.6 %collective-permute-start.1 = (f32[32,48]{1,0:T(8,128)S(1)}, f32[32,48]{1,0:T(8,128)S(1)}, u32[]{:S(2)}, u32[]{:S(2)}) collective-permute-start(f32[32,48]{1,0:T(8,128)S(1)} %get-tuple-element.18), channel_id=1, source_target_pairs={{0,2},{1,3},{2,0},{3,1},{4,6},{5,7},{6,4},{7,5},{8,10},{9,11},{10,... | collective-permute-start | bytes 18440 | tf_op jit(solution)/shard_map/ppermute | solution.py:554
  46.4 5.5 %collective-permute-start.2 = (f32[32,48]{1,0:T(8,128)S(1)}, f32[32,48]{1,0:T(8,128)S(1)}, u32[]{:S(2)}, u32[]{:S(2)}) collective-permute-start(f32[32,48]{1,0:T(8,128)S(1)} %get-tuple-element.18), channel_id=1, source_target_pairs={{0,3},{1,2},{2,1},{3,0},{4,7},{5,6},{6,5},{7,4},{8,11},{9,10},{10,... | collective-permute-start | bytes 18440 | tf_op jit(solution)/shard_map/ppermute | solution.py:554
  47.7 4.2 %collective-permute-start = (f32[32,48]{1,0:T(8,128)S(1)}, f32[32,48]{1,0:T(8,128)S(1)}, u32[]{:S(2)}, u32[]{:S(2)}) collective-permute-start(f32[32,48]{1,0:T(8,128)S(1)} %get-tuple-element.18), channel_id=1, source_target_pairs={{0,1},{1,0},{2,3},{3,2},{4,5},{5,4},{6,7},{7,6},{8,9},{9,8},{10,11... | collective-permute-start | bytes 18440 | tf_op jit(solution)/shard_map/ppermute | solution.py:554

commit v7 on v6

--- a/solution.py
+++ b/solution.py
@@ -15,6 +15,7 @@
 TABLE_PAD = 8
 NET_SPLIT = 4
 DEPTH = 4
+AHEAD = 3
 
 distill_weight = 50.0
 F32 = jnp.float32
@@ -300,7 +301,8 @@
         weights[corner] = w[0] * w[1] * w[2]
     build_table(grid_hbm, grid_ref, grid_sem, table)
     fetch_idx.wait()
-    gather(0, 0, rows.at[0])
+    for j in range(AHEAD):
+        gather(0, j, rows.at[j])
 
     def turn(step, carry):
         todo = stages(jnp.maximum(step - 1, 0), (step + 1) % 2)
@@ -308,11 +310,8 @@
             for run in todo[j * len(todo) // blocks : (j + 1) * len(todo) // blocks]:
                 run()
             interpolate(step, j, rows.at[j % DEPTH], step % 2)
-            ahead = rows.at[(j + 1) % DEPTH]
-            if j + 1 < blocks:
-                gather(step, j + 1, ahead)
-            else:
-                gather(jnp.minimum(step + 1, parts - 1), 0, ahead)
+            row = step if j + AHEAD < blocks else jnp.minimum(step + 1, parts - 1)
+            gather(row, (j + AHEAD) % blocks, rows.at[(j + AHEAD) % DEPTH])
         return carry
 
     lax.fori_loop(0, parts, turn, 0)

time: 53.5 us -> 52.4 us (0.979)
  Pallas kernels: 24.6 us -> 23.5 us
    pallas_call x1, Pallas kernels: 19.9 us -> 18.7 us  [forward(): pl.pallas_call(functools.partial(forward_kernel, cap), out_shape=(jax.Sha...]
where the time goes in v7:
time: 52.4 us; the launch traced here: 52 us
  Pallas kernels  23.5 us (45%)
  starting transfers between devices  12.7 us (24%)
  waiting for transfers between devices  12.3 us (23%)
  local copies, waits for them, and re-layouts  2.67 us (5%)
  between operations  0.68 us (1%)
    pallas_call x1, Pallas kernels, forward(): pl.pallas_call(functools.partial(forward_kernel, cap), out_shape=(jax.Sha...  18.7 us
    all_to_all x1, starting transfers between devices, on_device(): lax.all_to_all(outgoing, 'dom', split_axis=0, concat_axis=0, tiled=True)  5.2 us
    all_to_all x1, waiting for transfers between devices, on_device(): lax.all_to_all(summary, 'dom', split_axis=0, concat_axis=0, tiled=True)  4.29 us
    ppermute x3, starting transfers between devices, sum_replicas(): lax.ppermute(x, 'rep', [(i, i ^ s) for i in range(count)])  4.17 us
    all_to_all x1, waiting for transfers between devices, on_device(): lax.all_to_all(outgoing, 'dom', split_axis=0, concat_axis=0, tiled=True)  4.11 us
    ppermute x3, waiting for transfers between devices, sum_replicas(): lax.ppermute(x, 'rep', [(i, i ^ s) for i in range(count)])  3.93 us
    all_to_all x1, starting transfers between devices, on_device(): lax.all_to_all(summary, 'dom', split_axis=0, concat_axis=0, tiled=True)  3.36 us
    pallas_call x1, Pallas kernels, backward(): pl.pallas_call(functools.partial(backward_kernel, cap), out_shape=(jax.Sh...  2.38 us
  transfers between devices with their start and end apart: 5, of which 4 were waited for; matrix products, arithmetic and copies ran while one was open for 3% of the time, Pallas kernels for 1%

profile of v7, /device:TPU:0, one launch (start us, length us, event | category | flops | bytes accessed | tf_op | source)
XLA Modules:
  0.0 52.0 jit_solution(13873657499603902720)
XLA Ops:
  0.6 0.0 copy-start
  0.6 1.8 %pack.1 = bf16[8,4,2176]{2,1,0:T(4,128)(2,1)} custom-call(bf16[4,8,2048]{2,1,0:T(8,128)(2,1)} %bitcast.18, s32[8,32]{1,0:T(8,128)} %bitcast.22, s32[8,32]{1,0:T(8,128)} %bitcast.23, s32[8]{0:T(128)} %bitcast.25), custom_call_target="tpu_custom_call" | custom-call | tf_op jit(solution)/shard_map/pack/pallas_call | solution.py:87
  2.4 5.2 %all-to-all-start = ((bf16[8,4,2176]{2,1,0:T(4,128)(2,1)}), bf16[8,4,2176]{2,1,0:T(4,128)(2,1)S(1)}, u32[]{:S(2)}, u32[]{:S(2)}) async-start(bf16[8,4,2176]{2,1,0:T(4,128)(2,1)} %pack.1), calls=%async_computation | async-start | bytes 278528 | tf_op jit(solution)/shard_map/all_to_all | solution.py:577
  7.6 1.5 %copy.14 = s32[1,16,8,128]{3,1,2,0:T(8,128)} copy(s32[1,16,8,128]{3,2,1,0:T(8,128)} %bitcast.19) | data formatting | bytes 131072
  9.1 4.1 %all-to-all-done.arrived_ref = bf16[8,4,2176]{2,1,0:T(4,128)(2,1)S(1)} async-done(((bf16[8,4,2176]{2,1,0:T(4,128)(2,1)}), bf16[8,4,2176]{2,1,0:T(4,128)(2,1)S(1)}, u32[]{:S(2)}, u32[]{:S(2)}) %all-to-all-start) | async-done | bytes 139296 | tf_op jit(solution)/shard_map/all_to_all | solution.py:577
  13.2 18.7 %forward.1 = (bf16[8,48,2048]{2,1,0:T(8,128)(2,1)S(1)}, f32[4,8,2048]{2,1,0:T(8,128)S(1)}, f32[8,8,256]{2,1,0:T(8,128)}) custom-call(s32[16384]{0:T(1024)} %bitcast.17, bf16[32,32768]{1,0:T(8,128)(2,1)} %bitcast.16, bf16[8,4,2176]{2,1,0:T(4,128)(2,1)S(1)} %all-to-all-done.arrived_ref, bf16[32,64]{1,0:T(8,128)(2,1)} %bitcast.21, bf16[16,32]{1,0:T(8,128)(2,1)} %bitcast.24, ...), custom_call_target="tpu_custom_call" | custom-call | tf_op jit(solution)/shard_map/forward/pallas_call | solution.py:362
  31.9 3.4 %all-to-all-start.1 = ((f32[8,8,256]{2,1,0:T(8,128)}), f32[8,8,256]{2,1,0:T(8,128)S(1)}, u32[]{:S(2)}, u32[]{:S(2)}) async-start(f32[8,8,256]{2,1,0:T(8,128)} %get-tuple-element.11), calls=%async_computation.1 | async-start | bytes 131072 | tf_op jit(solution)/shard_map/all_to_all | solution.py:582
  35.3 0.6 %slot_marks.1 = (f32[8,256]{1,0:T(8,128)S(1)}, bf16[256,256]{1,0:T(8,128)(2,1)S(1)}, bf16[8,256,256]{2,1,0:T(8,128)(2,1)S(1)}) custom-call(s32[1]{0:T(128)} %bitcast.me_ref, bf16[8,4,2176]{2,1,0:T(4,128)(2,1)S(1)} %all-to-all-done.arrived_ref), custom_call_target="tpu_custom_call" | custom-call | flops 4194304 | bytes 4194304 | tf_op jit(solution)/shard_map/slot_marks/pallas_call | solution.py:130
  36.0 4.3 %all-to-all-done.1.stats_ref = f32[8,8,256]{2,1,0:T(8,128)S(1)} async-done(((f32[8,8,256]{2,1,0:T(8,128)}), f32[8,8,256]{2,1,0:T(8,128)S(1)}, u32[]{:S(2)}, u32[]{:S(2)}) %all-to-all-start.1) | async-done | bytes 65568 | tf_op jit(solution)/shard_map/all_to_all | solution.py:582
  40.3 0.0 copy-done
  40.3 2.4 %backward.1 = (f32[1,256]{1,0:T(1,128)}, f32[32,48]{1,0:T(8,128)S(1)}) custom-call(s32[1]{0:T(128)} %bitcast.me_ref, f32[8,8,256]{2,1,0:T(8,128)S(1)} %all-to-all-done.1.stats_ref, f32[8,256]{1,0:T(8,128)S(1)} %get-tuple-element.12.key_ref, bf16[256,256]{1,0:T(8,128)(2,1)S(1)} %get-tuple-element.13.hot_ref, f32[4,8,2048]{2,1,0:T(8,128)S(1)} %get-tuple-element.14.dense_ref, ...), custom_call_target="tpu_custom_call" | custom-call | tf_op jit(solution)/shard_map/backward/pallas_call | solution.py:534
  42.7 2.6 %collective-permute-start.1 = (f32[32,48]{1,0:T(8,128)S(1)}, f32[32,48]{1,0:T(8,128)S(1)}, u32[]{:S(2)}, u32[]{:S(2)}) collective-permute-start(f32[32,48]{1,0:T(8,128)S(1)} %get-tuple-element.18), channel_id=1, source_target_pairs={{0,2},{1,3},{2,0},{3,1},{4,6},{5,7},{6,4},{7,5},{8,10},{9,11},{10,... | collective-permute-start | bytes 18440 | tf_op jit(solution)/shard_map/ppermute | solution.py:553
  45.2 1.4 %collective-permute-start.2 = (f32[32,48]{1,0:T(8,128)S(1)}, f32[32,48]{1,0:T(8,128)S(1)}, u32[]{:S(2)}, u32[]{:S(2)}) collective-permute-start(f32[32,48]{1,0:T(8,128)S(1)} %get-tuple-element.18), channel_id=1, source_target_pairs={{0,3},{1,2},{2,1},{3,0},{4,7},{5,6},{6,5},{7,4},{8,11},{9,10},{10,... | collective-permute-start | bytes 18440 | tf_op jit(solution)/shard_map/ppermute | solution.py:553
  46.6 0.2 collective-permute-start
  46.8 0.5 collective-permute-done.1
  47.3 3.5 %collective-permute-done.2 = f32[32,48]{1,0:T(8,128)S(1)} collective-permute-done((f32[32,48]{1,0:T(8,128)S(1)}, f32[32,48]{1,0:T(8,128)S(1)}, u32[]{:S(2)}, u32[]{:S(2)}) %collective-permute-start.2) | collective-permute-done | bytes 6176 | tf_op jit(solution)/shard_map/ppermute | solution.py:553
  50.8 0.0 collective-permute-done
  50.8 0.6 %slice_bitcast_fusion = f32[1,16,32]{2,1,0:T(8,128)} fusion(f32[32,48]{1,0:T(8,128)S(1)} %add_add_fusion), kind=kLoop, calls=%fused_computation.1 | loop fusion | bytes 4096 | tf_op jit(solution)/shard_map/broadcast_in_dim | solution.py:589
  51.4 0.6 %slice.9 = f32[1,16]{1,0:T(1,128)} slice(f32[32,48]{1,0:T(8,128)S(1)} %add_add_fusion), slice={[16:17], [32:48]} | slice | bytes 128 | tf_op jit(solution)/shard_map/slice | solution.py:588
  (1 shorter events, 0.0 us)
Async XLA Ops:
  0.6 39.6 %copy-start = (bf16[1,16]{1,0:T(2,128)(2,1)S(1)}, bf16[1,16]{1,0:T(2,128)(2,1)}, u32[]{:S(2)}) copy-start(bf16[1,16]{1,0:T(2,128)(2,1)} %prop_out_ref.3) | copy-start | bytes 100
  2.4 10.8 %all-to-all-start = ((bf16[8,4,2176]{2,1,0:T(4,128)(2,1)}), bf16[8,4,2176]{2,1,0:T(4,128)(2,1)S(1)}, u32[]{:S(2)}, u32[]{:S(2)}) async-start(bf16[8,4,2176]{2,1,0:T(4,128)(2,1)} %pack.1), calls=%async_computation | async-start | bytes 278528 | tf_op jit(solution)/shard_map/all_to_all | solution.py:577
  31.9 8.3 %all-to-all-start.1 = ((f32[8,8,256]{2,1,0:T(8,128)}), f32[8,8,256]{2,1,0:T(8,128)S(1)}, u32[]{:S(2)}, u32[]{:S(2)}) async-start(f32[8,8,256]{2,1,0:T(8,128)} %get-tuple-element.11), calls=%async_computation.1 | async-start | bytes 131072 | tf_op jit(solution)/shard_map/all_to_all | solution.py:582
  42.7 4.6 %collective-permute-start.1 = (f32[32,48]{1,0:T(8,128)S(1)}, f32[32,48]{1,0:T(8,128)S(1)}, u32[]{:S(2)}, u32[]{:S(2)}) collective-permute-start(f32[32,48]{1,0:T(8,128)S(1)} %get-tuple-element.18), channel_id=1, source_target_pairs={{0,2},{1,3},{2,0},{3,1},{4,6},{5,7},{6,4},{7,5},{8,10},{9,11},{10,... | collective-permute-start | bytes 18440 | tf_op jit(solution)/shard_map/ppermute | solution.py:553
  45.2 5.5 %collective-permute-start.2 = (f32[32,48]{1,0:T(8,128)S(1)}, f32[32,48]{1,0:T(8,128)S(1)}, u32[]{:S(2)}, u32[]{:S(2)}) collective-permute-start(f32[32,48]{1,0:T(8,128)S(1)} %get-tuple-element.18), channel_id=1, source_target_pairs={{0,3},{1,2},{2,1},{3,0},{4,7},{5,6},{6,5},{7,4},{8,11},{9,10},{10,... | collective-permute-start | bytes 18440 | tf_op jit(solution)/shard_map/ppermute | solution.py:553
  46.6 4.2 %collective-permute-start = (f32[32,48]{1,0:T(8,128)S(1)}, f32[32,48]{1,0:T(8,128)S(1)}, u32[]{:S(2)}, u32[]{:S(2)}) collective-permute-start(f32[32,48]{1,0:T(8,128)S(1)} %get-tuple-element.18), channel_id=1, source_target_pairs={{0,1},{1,0},{2,3},{3,2},{4,5},{5,4},{6,7},{7,6},{8,9},{9,8},{10,11... | collective-permute-start | bytes 18440 | tf_op jit(solution)/shard_map/ppermute | solution.py:553

commit v8 on v7

--- a/solution.py
+++ b/solution.py
@@ -546,12 +546,31 @@
     )(me, stats, key, hot, dense, saved, prop_out, *masks)
 
 
-def sum_replicas(x):
+def finish_kernel(own_ref, one_ref, two_ref, three_ref, in_ref, out_ref):
+    total = (own_ref[...] + one_ref[...]) + (two_ref[...] + three_ref[...])
+    prop_hidden, features = in_ref.shape
+    in_ref[...] = total[:prop_hidden, :features]
+    out_ref[...] = total[prop_hidden : prop_hidden + 1, features:]
+
+
+def sum_replicas(x, prop_hidden, features):
     count = lax.axis_size("rep")
     if count != 4:
-        return lax.psum(x, "rep")
+        x = lax.psum(x, "rep")
+        return x[:prop_hidden, :features], x[prop_hidden : prop_hidden + 1, features:]
     other = [lax.ppermute(x, "rep", [(i, i ^ s) for i in range(count)]) for s in (1, 2, 3)]
-    return (x + other[0]) + (other[1] + other[2])
+    vmem = pl.BlockSpec(memory_space=pltpu.VMEM)
+    return pl.pallas_call(
+        finish_kernel,
+        out_shape=(
+            jax.ShapeDtypeStruct((prop_hidden, features), F32),
+            jax.ShapeDtypeStruct((1, prop_hidden), F32),
+        ),
+        in_specs=[vmem] * 4,
+        out_specs=(vmem, vmem),
+        compiler_params=pltpu.CompilerParams(vmem_limit_bytes=4 * 1024 * 1024),
+        name="finish",
+    )(x, *other)
 
 
 def on_device(
@@ -583,10 +602,8 @@
     me = lax.axis_index("dom").reshape(1).astype(jnp.int32)
     marks = slot_marks(me, arrived, cap)
     ray_loss, grads = backward(me, stats, dense, saved, prop_out, marks, cap)
-    sums = sum_replicas(grads)
-    in_sum = sums[:prop_hidden, :features]
-    out_sum = sums[prop_hidden, features:]
-    return (ray_loss.reshape(1, 1, -1), in_sum[None], out_sum[None])
+    in_sum, out_sum = sum_replicas(grads, prop_hidden, features)
+    return (ray_loss.reshape(1, 1, -1), in_sum[None], out_sum)
 
 
 def solution(mesh):

time: 52.4 us -> 53.1 us (1.013)
  waiting for transfers between devices: 12.3 us -> 13.7 us
  local copies, waits for them, and re-layouts: 2.67 us -> 1.48 us
    ppermute x3, waiting for transfers between devices: 3.93 us -> 5.3 us  [sum_replicas(): lax.ppermute(x, 'rep', [(i, i ^ s) for i in range(count)])]
    pallas_call x0 -> x1, Pallas kernels: none -> 0.61 us  [sum_replicas(): pl.pallas_call(finish_kernel, out_shape=(jax.ShapeDtypeStruct((prop_hidde...]
    broadcast_in_dim x1 -> x0, local copies, waits for them, and re-layouts: 0.6 us -> none  [on_device(): return (ray_loss.reshape(1, 1, -1), in_sum[None], out_sum[None])]
    slice x1 -> x0, local copies, waits for them, and re-layouts: 0.58 us -> none  [on_device(): out_sum = sums[prop_hidden, features:]]
where the time goes in v8:
time: 53.1 us; the launch traced here: 52.7 us
  Pallas kernels  23.9 us (45%)
  waiting for transfers between devices  13.7 us (26%)
  starting transfers between devices  12.9 us (24%)
  local copies, waits for them, and re-layouts  1.48 us (3%)
  between operations  0.67 us (1%)
    pallas_call x1, Pallas kernels, forward(): pl.pallas_call(functools.partial(forward_kernel, cap), out_shape=(jax.Sha...  18.5 us
    ppermute x3, waiting for transfers between devices, sum_replicas(): lax.ppermute(x, 'rep', [(i, i ^ s) for i in range(count)])  5.3 us
    all_to_all x1, starting transfers between devices, on_device(): lax.all_to_all(outgoing, 'dom', split_axis=0, concat_axis=0, tiled=True)  5.2 us
    ppermute x3, starting transfers between devices, sum_replicas(): lax.ppermute(x, 'rep', [(i, i ^ s) for i in range(count)])  4.39 us
    all_to_all x1, waiting for transfers between devices, on_device(): lax.all_to_all(summary, 'dom', split_axis=0, concat_axis=0, tiled=True)  4.29 us
    all_to_all x1, waiting for transfers between devices, on_device(): lax.all_to_all(outgoing, 'dom', split_axis=0, concat_axis=0, tiled=True)  4.12 us
    all_to_all x1, starting transfers between devices, on_device(): lax.all_to_all(summary, 'dom', split_axis=0, concat_axis=0, tiled=True)  3.36 us
    pallas_call x1, Pallas kernels, backward(): pl.pallas_call(functools.partial(backward_kernel, cap), out_shape=(jax.Sh...  2.38 us
  transfers between devices with their start and end apart: 5, of which 4 were waited for; matrix products, arithmetic and copies ran while one was open for 3% of the time, Pallas kernels for 1%

profile of v8, /device:TPU:0, one launch (start us, length us, event | category | flops | bytes accessed | tf_op | source)
XLA Modules:
  0.0 52.7 jit_solution(4837064330850794519)
XLA Ops:
  0.6 0.0 copy-start
  0.6 1.8 %pack.1 = bf16[8,4,2176]{2,1,0:T(4,128)(2,1)} custom-call(bf16[4,8,2048]{2,1,0:T(8,128)(2,1)} %bitcast.17, s32[8,32]{1,0:T(8,128)} %bitcast.21, s32[8,32]{1,0:T(8,128)} %bitcast.22, s32[8]{0:T(128)} %bitcast.24), custom_call_target="tpu_custom_call" | custom-call | tf_op jit(solution)/shard_map/pack/pallas_call | solution.py:87
  2.4 5.2 %all-to-all-start = ((bf16[8,4,2176]{2,1,0:T(4,128)(2,1)}), bf16[8,4,2176]{2,1,0:T(4,128)(2,1)S(1)}, u32[]{:S(2)}, u32[]{:S(2)}) async-start(bf16[8,4,2176]{2,1,0:T(4,128)(2,1)} %pack.1), calls=%async_computation | async-start | bytes 278528 | tf_op jit(solution)/shard_map/all_to_all | solution.py:596
  7.6 1.5 %copy.14 = s32[1,16,8,128]{3,1,2,0:T(8,128)} copy(s32[1,16,8,128]{3,2,1,0:T(8,128)} %bitcast.18) | data formatting | bytes 131072
  9.1 4.1 %all-to-all-done.arrived_ref = bf16[8,4,2176]{2,1,0:T(4,128)(2,1)S(1)} async-done(((bf16[8,4,2176]{2,1,0:T(4,128)(2,1)}), bf16[8,4,2176]{2,1,0:T(4,128)(2,1)S(1)}, u32[]{:S(2)}, u32[]{:S(2)}) %all-to-all-start) | async-done | bytes 139296 | tf_op jit(solution)/shard_map/all_to_all | solution.py:596
  13.2 18.5 %forward.1 = (bf16[8,48,2048]{2,1,0:T(8,128)(2,1)S(1)}, f32[4,8,2048]{2,1,0:T(8,128)S(1)}, f32[8,8,256]{2,1,0:T(8,128)}) custom-call(s32[16384]{0:T(1024)} %bitcast.16, bf16[32,32768]{1,0:T(8,128)(2,1)} %bitcast.15, bf16[8,4,2176]{2,1,0:T(4,128)(2,1)S(1)} %all-to-all-done.arrived_ref, bf16[32,64]{1,0:T(8,128)(2,1)} %bitcast.20, bf16[16,32]{1,0:T(8,128)(2,1)} %bitcast.23, ...), custom_call_target="tpu_custom_call" | custom-call | tf_op jit(solution)/shard_map/forward/pallas_call | solution.py:362
  31.7 3.4 %all-to-all-start.1 = ((f32[8,8,256]{2,1,0:T(8,128)}), f32[8,8,256]{2,1,0:T(8,128)S(1)}, u32[]{:S(2)}, u32[]{:S(2)}) async-start(f32[8,8,256]{2,1,0:T(8,128)} %get-tuple-element.13), calls=%async_computation.1 | async-start | bytes 131072 | tf_op jit(solution)/shard_map/all_to_all | solution.py:601
  35.1 0.6 %slot_marks.1 = (f32[8,256]{1,0:T(8,128)S(1)}, bf16[256,256]{1,0:T(8,128)(2,1)S(1)}, bf16[8,256,256]{2,1,0:T(8,128)(2,1)S(1)}) custom-call(s32[1]{0:T(128)} %bitcast.me_ref, bf16[8,4,2176]{2,1,0:T(4,128)(2,1)S(1)} %all-to-all-done.arrived_ref), custom_call_target="tpu_custom_call" | custom-call | flops 4194304 | bytes 4194304 | tf_op jit(solution)/shard_map/slot_marks/pallas_call | solution.py:130
  35.7 4.3 %all-to-all-done.1.stats_ref = f32[8,8,256]{2,1,0:T(8,128)S(1)} async-done(((f32[8,8,256]{2,1,0:T(8,128)}), f32[8,8,256]{2,1,0:T(8,128)S(1)}, u32[]{:S(2)}, u32[]{:S(2)}) %all-to-all-start.1) | async-done | bytes 65568 | tf_op jit(solution)/shard_map/all_to_all | solution.py:601
  40.0 0.0 copy-done
  40.0 2.4 %backward.1 = (f32[1,256]{1,0:T(1,128)}, f32[32,48]{1,0:T(8,128)S(1)}) custom-call(s32[1]{0:T(128)} %bitcast.me_ref, f32[8,8,256]{2,1,0:T(8,128)S(1)} %all-to-all-done.1.stats_ref, f32[8,256]{1,0:T(8,128)S(1)} %get-tuple-element.14.key_ref, bf16[256,256]{1,0:T(8,128)(2,1)S(1)} %get-tuple-element.15.hot_ref, f32[4,8,2048]{2,1,0:T(8,128)S(1)} %get-tuple-element.16.dense_ref, ...), custom_call_target="tpu_custom_call" | custom-call | tf_op jit(solution)/shard_map/backward/pallas_call | solution.py:534
  42.4 1.6 %collective-permute-start = (f32[32,48]{1,0:T(8,128)S(1)}, f32[32,48]{1,0:T(8,128)S(1)}, u32[]{:S(2)}, u32[]{:S(2)}) collective-permute-start(f32[32,48]{1,0:T(8,128)S(1)} %get-tuple-element.20.own_ref), channel_id=1, source_target_pairs={{0,1},{1,0},{2,3},{3,2},{4,5},{5,4},{6,7},{7,6},{8,9},{9,8},{10,11... | collective-permute-start | bytes 18440 | tf_op jit(solution)/shard_map/ppermute | solution.py:561
  44.0 2.6 %collective-permute-start.1 = (f32[32,48]{1,0:T(8,128)S(1)}, f32[32,48]{1,0:T(8,128)S(1)}, u32[]{:S(2)}, u32[]{:S(2)}) collective-permute-start(f32[32,48]{1,0:T(8,128)S(1)} %get-tuple-element.20.own_ref), channel_id=1, source_target_pairs={{0,2},{1,3},{2,0},{3,1},{4,6},{5,7},{6,4},{7,5},{8,10},{9,11},{10,... | collective-permute-start | bytes 18440 | tf_op jit(solution)/shard_map/ppermute | solution.py:561
  46.5 0.2 collective-permute-start.2
  46.8 0.0 collective-permute-done.one_ref
  46.8 1.9 %collective-permute-done.1.two_ref = f32[32,48]{1,0:T(8,128)S(1)} collective-permute-done((f32[32,48]{1,0:T(8,128)S(1)}, f32[32,48]{1,0:T(8,128)S(1)}, u32[]{:S(2)}, u32[]{:S(2)}) %collective-permute-start.1) | collective-permute-done | bytes 6176 | tf_op jit(solution)/shard_map/ppermute | solution.py:561
  48.7 3.4 %collective-permute-done.2.three_ref = f32[32,48]{1,0:T(8,128)S(1)} collective-permute-done((f32[32,48]{1,0:T(8,128)S(1)}, f32[32,48]{1,0:T(8,128)S(1)}, u32[]{:S(2)}, u32[]{:S(2)}) %collective-permute-start.2) | collective-permute-done | bytes 6176 | tf_op jit(solution)/shard_map/ppermute | solution.py:561
  52.1 0.6 %finish.1 = (f32[16,32]{1,0:T(8,128)}, f32[1,16]{1,0:T(1,128)}) custom-call(f32[32,48]{1,0:T(8,128)S(1)} %get-tuple-element.20.own_ref, f32[32,48]{1,0:T(8,128)S(1)} %collective-permute-done.one_ref, f32[32,48]{1,0:T(8,128)S(1)} %collective-permute-done.1.two_ref, f32[32,48]{1,0:T(8,128)S(1)} %collective-permute-done.2.three_ref), custom_call_target="tpu_custom_call" | custom-call | tf_op jit(solution)/shard_map/finish/pallas_call | solution.py:563
Async XLA Ops:
  0.6 39.4 %copy-start = (bf16[1,16]{1,0:T(2,128)(2,1)S(1)}, bf16[1,16]{1,0:T(2,128)(2,1)}, u32[]{:S(2)}) copy-start(bf16[1,16]{1,0:T(2,128)(2,1)} %prop_out_ref.3) | copy-start | bytes 100
  2.4 10.8 %all-to-all-start = ((bf16[8,4,2176]{2,1,0:T(4,128)(2,1)}), bf16[8,4,2176]{2,1,0:T(4,128)(2,1)S(1)}, u32[]{:S(2)}, u32[]{:S(2)}) async-start(bf16[8,4,2176]{2,1,0:T(4,128)(2,1)} %pack.1), calls=%async_computation | async-start | bytes 278528 | tf_op jit(solution)/shard_map/all_to_all | solution.py:596
  31.7 8.3 %all-to-all-start.1 = ((f32[8,8,256]{2,1,0:T(8,128)}), f32[8,8,256]{2,1,0:T(8,128)S(1)}, u32[]{:S(2)}, u32[]{:S(2)}) async-start(f32[8,8,256]{2,1,0:T(8,128)} %get-tuple-element.13), calls=%async_computation.1 | async-start | bytes 131072 | tf_op jit(solution)/shard_map/all_to_all | solution.py:601
  42.4 4.4 %collective-permute-start = (f32[32,48]{1,0:T(8,128)S(1)}, f32[32,48]{1,0:T(8,128)S(1)}, u32[]{:S(2)}, u32[]{:S(2)}) collective-permute-start(f32[32,48]{1,0:T(8,128)S(1)} %get-tuple-element.20.own_ref), channel_id=1, source_target_pairs={{0,1},{1,0},{2,3},{3,2},{4,5},{5,4},{6,7},{7,6},{8,9},{9,8},{10,11... | collective-permute-start | bytes 18440 | tf_op jit(solution)/shard_map/ppermute | solution.py:561
  44.0 4.7 %collective-permute-start.1 = (f32[32,48]{1,0:T(8,128)S(1)}, f32[32,48]{1,0:T(8,128)S(1)}, u32[]{:S(2)}, u32[]{:S(2)}) collective-permute-start(f32[32,48]{1,0:T(8,128)S(1)} %get-tuple-element.20.own_ref), channel_id=1, source_target_pairs={{0,2},{1,3},{2,0},{3,1},{4,6},{5,7},{6,4},{7,5},{8,10},{9,11},{10,... | collective-permute-start | bytes 18440 | tf_op jit(solution)/shard_map/ppermute | solution.py:561
  46.5 5.5 %collective-permute-start.2 = (f32[32,48]{1,0:T(8,128)S(1)}, f32[32,48]{1,0:T(8,128)S(1)}, u32[]{:S(2)}, u32[]{:S(2)}) collective-permute-start(f32[32,48]{1,0:T(8,128)S(1)} %get-tuple-element.20.own_ref), channel_id=1, source_target_pairs={{0,3},{1,2},{2,1},{3,0},{4,7},{5,6},{6,5},{7,4},{8,11},{9,10},{10,... | collective-permute-start | bytes 18440 | tf_op jit(solution)/shard_map/ppermute | solution.py:561
